TPU v7x, 32 devices: a whole 2x2x4 slice. The times are simulated.
32 devices in a mesh: replica: 8 (over y, x, core), group: 4 (over z).
Axes of the slice: x: 2, y: 2, z: 4, core: 2. Of those that a mesh axis runs over, the one named last changes fastest.
Arguments:
- inputs: bfloat16 [8, 512, 2048], P('replica', 'group'), may hold values from -6 to 6
- seq_lengths: int32 [8], P('replica'), may hold values from 128 to 512, as said below
- bucket_ids: int32 [1023], replicated, may hold values from 0 to 31, as said below
- norm1_gain: bfloat16 [2048], P('group'), may hold values from 0.25 to 1.75
- w_query: bfloat16 [2048, 2048], P(None, 'group'), may hold values from -0.0625 to 0.0625
- w_key: bfloat16 [2048, 2048], P(None, 'group'), may hold values from -0.0625 to 0.0625
- w_value: bfloat16 [2048, 2048], P(None, 'group'), may hold values from -0.125 to 0.125
- w_attn_out: bfloat16 [2048, 2048], P('group'), may hold values from -0.5 to 0.5
- bias_table: bfloat16 [32, 32], P(None, 'group'), may hold values from -4 to 4
- norm2_gain: bfloat16 [2048], P('group'), may hold values from 0.25 to 1.75
- w_gate: bfloat16 [2048, 5120], P(None, 'group'), may hold values from -0.125 to 0.125
- w_up: bfloat16 [2048, 5120], P(None, 'group'), may hold values from -0.125 to 0.125
- w_ffn_out: bfloat16 [5120, 2048], P('group'), may hold values from -0.078125 to 0.078125
- cotangent: bfloat16 [8, 512, 2048], P('replica', 'group'), may hold values from -6 to 6
Outputs:
- result: bfloat16 [8, 512, 2048], P('replica', 'group')
- input_grad: bfloat16 [8, 512, 2048], P('replica', 'group')
- norm1_gain_grad: float32 [2048], P('group')
- query_grad: float32 [2048, 2048], P(None, 'group')
- key_grad: float32 [2048, 2048], P(None, 'group')
- value_grad: float32 [2048, 2048], P(None, 'group')
- attn_out_grad: float32 [2048, 2048], P('group')
- bias_table_grad: float32 [32, 32], P(None, 'group')
- norm2_gain_grad: float32 [2048], P('group')
- gate_grad: float32 [2048, 5120], P(None, 'group')
- up_grad: float32 [2048, 5120], P(None, 'group')
- ffn_out_grad: float32 [5120, 2048], P('group')
Inputs may be any that keep to these rules, and one draw needn't show every extreme that they name: `seq_lengths`: one sequence has exactly 512 valid positions and another exactly 128. `bucket_ids`: entry 511 + o is the bucket of the offset o = key position - query position; every bucket occurs.
All inputs are finite; a program needn't handle non-finite values.
Results may differ from a plain program's by a relative error of at most 0.02.
Values may be sent and summed in bfloat16 or wider, within the bound.
A program may use at most 448 MiB of HBM per device.

v0:
```python
import jax
import jax.numpy as jnp
from jax import lax
from jax.sharding import PartitionSpec as P

epsilon = 1e-06
negative = -1000000000.0
head_block = 8
highest = lax.Precision.HIGHEST


def rms_scale(values, gain):
    return values * lax.rsqrt(jnp.mean(values * values, axis=-1, keepdims=True) + epsilon) * gain


def gated_gelu(gate_pre, up_pre):
    return jax.nn.gelu(gate_pre, approximate=True) * up_pre


def inner_rows(left, right):
    return lax.dot_general(
        left, right, (((0,), (0,)), ((), ())), preferred_element_type=jnp.float32
    )


def inner_columns(left, right):
    return lax.dot_general(
        left, right, (((1,), (1,)), ((), ())), preferred_element_type=jnp.float32
    )


def split_heads(matrix, groups, block_size):
    return matrix.reshape(matrix.shape[0], groups, block_size, -1).transpose(1, 0, 2, 3)


def merge_heads(blocks):
    return blocks.transpose(1, 0, 2, 3).reshape(blocks.shape[1], -1)


def spread_offsets(vector, row_count, col_count):
    span_width = row_count + col_count + 1
    block_heads = vector.shape[0]
    tiled_rows = jnp.broadcast_to(vector[:, None, :], (block_heads, row_count, span_width))
    flattened = tiled_rows.reshape(block_heads, row_count * span_width)[
        :, : row_count * (span_width - 1)
    ]
    return flattened.reshape(block_heads, row_count, span_width - 1)[:, :, row_count:]


def fold_offsets(matrix):
    block_heads, row_count, col_count = matrix.shape
    padded = jnp.pad(matrix, ((0, 0), (0, 0), (row_count, 0)))
    flattened = jnp.pad(
        padded.reshape(block_heads, row_count * (row_count + col_count)), ((0, 0), (0, row_count))
    )
    sums_all = flattened.reshape(block_heads, row_count, row_count + col_count + 1).sum(axis=1)
    return sums_all[:, 1 : row_count + col_count]


def offset_table(table_part, one_hot, groups, block_size):
    per_offset = jnp.dot(one_hot, table_part.astype(jnp.float32), precision=highest)
    return jnp.pad(per_offset.T, ((0, 0), (1, 1))).reshape(groups, block_size, -1)


def attention_forward(query_low, key_all, value_all, offsets, key_valid, groups, block_size):
    row_count = query_low.shape[0]
    keys_total = key_all.shape[0]

    def attend_block(operands):
        query_blk, key_blk, value_blk, offset_blk = operands
        scores = jnp.einsum("qhd,khd->hqk", query_blk, key_blk, preferred_element_type=jnp.float32)
        scores = jnp.where(
            key_valid, scores + spread_offsets(offset_blk, row_count, keys_total), negative
        )
        top_score = jnp.max(scores, axis=-1, keepdims=True)
        weights_exp = jnp.exp(scores - top_score)
        total_exp = jnp.sum(weights_exp, axis=-1, keepdims=True)
        probs_low = (weights_exp / total_exp).astype(jnp.bfloat16)
        attended_blk = jnp.einsum(
            "hqk,khd->qhd", probs_low, value_blk, preferred_element_type=jnp.float32
        )
        return (attended_blk, top_score[..., 0] + jnp.log(total_exp[..., 0]))

    operands = (
        split_heads(query_low, groups, block_size),
        split_heads(key_all, groups, block_size),
        split_heads(value_all, groups, block_size),
        offsets,
    )
    attended, log_totals = lax.map(attend_block, operands)
    return (merge_heads(attended).astype(jnp.bfloat16), log_totals)


def attention_backward(
    query_low, key_all, value_all, offsets, key_valid, grad_attended, log_totals, groups, block_size
):
    row_count = query_low.shape[0]
    keys_total = key_all.shape[0]

    def attend_back(operands):
        query_blk, key_blk, value_blk, offset_blk, grad_blk, log_blk = operands
        scores = jnp.einsum("qhd,khd->hqk", query_blk, key_blk, preferred_element_type=jnp.float32)
        scores = jnp.where(
            key_valid, scores + spread_offsets(offset_blk, row_count, keys_total), negative
        )
        probs = jnp.exp(scores - log_blk[..., None])
        grad_probs = jnp.einsum(
            "qhd,khd->hqk", grad_blk, value_blk, preferred_element_type=jnp.float32
        )
        inner_sum = jnp.sum(probs * grad_probs, axis=-1, keepdims=True)
        grad_scores = (probs * (grad_probs - inner_sum)).astype(jnp.bfloat16)
        probs_low = probs.astype(jnp.bfloat16)
        grad_query = jnp.einsum(
            "hqk,khd->qhd", grad_scores, key_blk, preferred_element_type=jnp.float32
        )
        grad_key = jnp.einsum(
            "hqk,qhd->khd", grad_scores, query_blk, preferred_element_type=jnp.float32
        )
        grad_value = jnp.einsum(
            "hqk,qhd->khd", probs_low, grad_blk, preferred_element_type=jnp.float32
        )
        return (grad_query, grad_key, grad_value, fold_offsets(grad_scores.astype(jnp.float32)))

    operands = (
        split_heads(query_low, groups, block_size),
        split_heads(key_all, groups, block_size),
        split_heads(value_all, groups, block_size),
        offsets,
        split_heads(grad_attended, groups, block_size),
        log_totals,
    )
    grad_query_blk, grad_key_blk, grad_value_blk, offset_sums = lax.map(attend_back, operands)
    return (
        merge_heads(grad_query_blk),
        merge_heads(grad_key_blk),
        merge_heads(grad_value_blk),
        offset_sums,
    )


def local(
    inputs,
    seq_lengths,
    bucket_ids,
    norm1_gain,
    w_query,
    w_key,
    w_value,
    w_attn_out,
    bias_table,
    norm2_gain,
    w_gate,
    w_up,
    w_ffn_out,
    cotangent,
):
    hidden_in = inputs[0].astype(jnp.float32)
    row_count = hidden_in.shape[0]
    keys_total = row_count * lax.axis_size("group")
    query_start = lax.axis_index("group") * row_count
    length = seq_lengths[0]
    buckets = bias_table.shape[0]
    key_valid = (jnp.arange(keys_total) < length)[None, None, :]
    row_valid = query_start + jnp.arange(row_count) < length
    gain_one, gain_two, query_full, key_full, value_full, attn_full, table_full = (
        lax.all_gather(norm1_gain, "group", axis=0, tiled=True),
        lax.all_gather(norm2_gain, "group", axis=0, tiled=True),
        lax.all_gather(w_query, "group", axis=1, tiled=True),
        lax.all_gather(w_key, "group", axis=1, tiled=True),
        lax.all_gather(w_value, "group", axis=1, tiled=True),
        lax.all_gather(w_attn_out, "group", axis=0, tiled=True),
        lax.all_gather(bias_table, "group", axis=1, tiled=True),
    )
    gain_first = gain_one.astype(jnp.float32)
    gain_second = gain_two.astype(jnp.float32)
    head_count = table_full.shape[1]
    groups = head_count // head_block
    normed_one = rms_scale(hidden_in, gain_first).astype(jnp.bfloat16)
    query_low = jnp.dot(normed_one, query_full, preferred_element_type=jnp.float32).astype(
        jnp.bfloat16
    )
    key_low = jnp.dot(normed_one, key_full, preferred_element_type=jnp.float32).astype(jnp.bfloat16)
    value_low = jnp.dot(normed_one, value_full, preferred_element_type=jnp.float32).astype(
        jnp.bfloat16
    )
    key_all, value_all = (
        lax.all_gather(key_low, "group", axis=0, tiled=True),
        lax.all_gather(value_low, "group", axis=0, tiled=True),
    )
    window = lax.dynamic_slice_in_dim(
        bucket_ids, keys_total - row_count - query_start, row_count + keys_total - 1
    )
    one_hot = (window[:, None] == jnp.arange(buckets)[None, :]).astype(jnp.float32)
    offsets = offset_table(table_full, one_hot, groups, head_block)
    attended_low, log_totals = attention_forward(
        query_low, key_all, value_all, offsets, key_valid, groups, head_block
    )
    middle = hidden_in + jnp.dot(attended_low, attn_full, preferred_element_type=jnp.float32)
    normed_two = rms_scale(middle, gain_second).astype(jnp.bfloat16)
    grad_out = cotangent[0].astype(jnp.float32) * row_valid[:, None].astype(jnp.float32)
    grad_low = grad_out.astype(jnp.bfloat16)
    gate_full, up_full, ffn_full = (
        lax.all_gather(w_gate, "group", axis=1, tiled=True),
        lax.all_gather(w_up, "group", axis=1, tiled=True),
        lax.all_gather(w_ffn_out, "group", axis=0, tiled=True),
    )
    gate_pre = jnp.dot(normed_two, gate_full, preferred_element_type=jnp.float32)
    up_pre = jnp.dot(normed_two, up_full, preferred_element_type=jnp.float32)
    hidden_low = gated_gelu(gate_pre, up_pre).astype(jnp.bfloat16)
    branch_ffn = jnp.dot(hidden_low, ffn_full, preferred_element_type=jnp.float32)
    result = (middle + branch_ffn).astype(jnp.bfloat16)
    gate_back, up_back, ffn_back = (
        lax.all_gather(w_gate, "group", axis=1, tiled=True),
        lax.all_gather(w_up, "group", axis=1, tiled=True),
        lax.all_gather(w_ffn_out, "group", axis=0, tiled=True),
    )
    grad_hidden = inner_columns(grad_low, ffn_back)
    _, pull_gelu = jax.vjp(gated_gelu, gate_pre, up_pre)
    grad_gate, grad_up = pull_gelu(grad_hidden)
    grad_gate = grad_gate.astype(jnp.bfloat16)
    grad_up = grad_up.astype(jnp.bfloat16)
    grad_normed = inner_columns(grad_gate, gate_back) + inner_columns(grad_up, up_back)
    gate_grad, up_grad, ffn_out_grad = (
        lax.psum_scatter(
            inner_rows(normed_two, grad_gate).astype(jnp.bfloat16),
            "group",
            scatter_dimension=1,
            tiled=True,
        ).astype(jnp.float32),
        lax.psum_scatter(
            inner_rows(normed_two, grad_up).astype(jnp.bfloat16),
            "group",
            scatter_dimension=1,
            tiled=True,
        ).astype(jnp.float32),
        lax.psum_scatter(
            inner_rows(hidden_low, grad_low).astype(jnp.bfloat16),
            "group",
            scatter_dimension=0,
            tiled=True,
        ).astype(jnp.float32),
    )
    _, pull_two = jax.vjp(rms_scale, middle, gain_second)
    grad_mid_norm, gain_two_grad = pull_two(grad_normed)
    grad_middle = grad_out + grad_mid_norm
    grad_branch = grad_middle.astype(jnp.bfloat16)
    query_back, key_back, value_back, attn_back, table_back = (
        lax.all_gather(w_query, "group", axis=1, tiled=True),
        lax.all_gather(w_key, "group", axis=1, tiled=True),
        lax.all_gather(w_value, "group", axis=1, tiled=True),
        lax.all_gather(w_attn_out, "group", axis=0, tiled=True),
        lax.all_gather(bias_table, "group", axis=1, tiled=True),
    )
    attn_out_grad = inner_rows(attended_low, grad_branch)
    grad_attended = inner_columns(grad_branch, attn_back).astype(jnp.bfloat16)
    offset_bwd = offset_table(table_back, one_hot, groups, head_block)
    grad_query, grad_key, grad_value, offset_sums = attention_backward(
        query_low,
        key_all,
        value_all,
        offset_bwd,
        key_valid,
        grad_attended,
        log_totals,
        groups,
        head_block,
    )
    key_sum, value_sum = (
        lax.psum_scatter(
            grad_key.astype(jnp.bfloat16), "group", scatter_dimension=0, tiled=True
        ).astype(jnp.float32),
        lax.psum_scatter(
            grad_value.astype(jnp.bfloat16), "group", scatter_dimension=0, tiled=True
        ).astype(jnp.float32),
    )
    grad_query_low = grad_query.astype(jnp.bfloat16)
    grad_key_low = key_sum.astype(jnp.bfloat16)
    grad_value_low = value_sum.astype(jnp.bfloat16)
    table_grad = jnp.dot(offset_sums.reshape(head_count, -1), one_hot, precision=highest).T
    query_grad = inner_rows(normed_one, grad_query_low)
    key_grad = inner_rows(normed_one, grad_key_low)
    value_grad = inner_rows(normed_one, grad_value_low)
    grad_normed_one = (
        inner_columns(grad_query_low, query_back)
        + inner_columns(grad_key_low, key_back)
        + inner_columns(grad_value_low, value_back)
    )
    _, pull_one = jax.vjp(rms_scale, hidden_in, gain_first)
    grad_in_norm, gain_one_grad = pull_one(grad_normed_one)
    input_grad = (grad_middle + grad_in_norm).astype(jnp.bfloat16)
    gain_one_part, gain_two_part, query_part, key_part, value_part, attn_part, table_part = (
        lax.psum_scatter(
            gain_one_grad.astype(jnp.bfloat16), "group", scatter_dimension=0, tiled=True
        ).astype(jnp.float32),
        lax.psum_scatter(
            gain_two_grad.astype(jnp.bfloat16), "group", scatter_dimension=0, tiled=True
        ).astype(jnp.float32),
        lax.psum_scatter(
            query_grad.astype(jnp.bfloat16), "group", scatter_dimension=1, tiled=True
        ).astype(jnp.float32),
        lax.psum_scatter(
            key_grad.astype(jnp.bfloat16), "group", scatter_dimension=1, tiled=True
        ).astype(jnp.float32),
        lax.psum_scatter(
            value_grad.astype(jnp.bfloat16), "group", scatter_dimension=1, tiled=True
        ).astype(jnp.float32),
        lax.psum_scatter(
            attn_out_grad.astype(jnp.bfloat16), "group", scatter_dimension=0, tiled=True
        ).astype(jnp.float32),
        lax.psum_scatter(
            table_grad.astype(jnp.bfloat16), "group", scatter_dimension=1, tiled=True
        ).astype(jnp.float32),
    )
    summed = (
        lax.psum(gain_one_part.astype(jnp.bfloat16), "replica").astype(jnp.float32),
        lax.psum(query_part.astype(jnp.bfloat16), "replica").astype(jnp.float32),
        lax.psum(key_part.astype(jnp.bfloat16), "replica").astype(jnp.float32),
        lax.psum(value_part.astype(jnp.bfloat16), "replica").astype(jnp.float32),
        lax.psum(attn_part.astype(jnp.bfloat16), "replica").astype(jnp.float32),
        lax.psum(table_part.astype(jnp.bfloat16), "replica").astype(jnp.float32),
        lax.psum(gain_two_part.astype(jnp.bfloat16), "replica").astype(jnp.float32),
        lax.psum(gate_grad.astype(jnp.bfloat16), "replica").astype(jnp.float32),
        lax.psum(up_grad.astype(jnp.bfloat16), "replica").astype(jnp.float32),
        lax.psum(ffn_out_grad.astype(jnp.bfloat16), "replica").astype(jnp.float32),
    )
    return (
        result[None],
        input_grad[None],
        summed[0],
        summed[1],
        summed[2],
        summed[3],
        summed[4],
        summed[5],
        summed[6],
        summed[7],
        summed[8],
        summed[9],
    )


def solution(mesh):
    placed = (
        P("replica", "group", None),
        P("replica"),
        P(),
        P("group"),
        P(None, "group"),
        P(None, "group"),
        P(None, "group"),
        P("group", None),
        P(None, "group"),
        P("group"),
        P(None, "group"),
        P(None, "group"),
        P("group", None),
        P("replica", "group", None),
    )
    return jax.shard_map(
        local,
        mesh=mesh,
        in_specs=placed,
        out_specs=(
            P("replica", "group", None),
            P("replica", "group", None),
            P("group"),
            P(None, "group"),
            P(None, "group"),
            P(None, "group"),
            P("group", None),
            P(None, "group"),
            P("group"),
            P(None, "group"),
            P(None, "group"),
            P("group", None),
        ),
        check_vma=False,
    )
```

profile of v0, /device:TPU:17, one launch (start us, length us, event | category | flops | bytes accessed | tf_op | source)
XLA Modules:
  0.0 4005.6 jit_solution(15519130537218076561)
XLA Ops:
  9.5 7.5 all-gather
  17.3 141.3 %all-gather.12.cloned.1.call-done = bf16[2048,2048]{1,0:T(8,128)(2,1)} async-done(((bf16[2048,512]{1,0:T(8,128)(2,1)}), bf16[2048,2048]{1,0:T(8,128)(2,1)}) %all-gather.12.cloned.1.call-update) | async-done | bytes 8388624 | tf_op jit(solution)/shard_map/all_gather | solution.py:170
  158.5 5.5 convolution_convert_fusion.10
  164.1 143.9 %all-gather.18.cloned.1.call-done = bf16[2048,2048]{1,0:T(8,128)(2,1)} async-done(((bf16[2048,512]{1,0:T(8,128)(2,1)}), bf16[2048,2048]{1,0:T(8,128)(2,1)}) %all-gather.18.cloned.1.call-update) | async-done | bytes 8388624 | tf_op jit(solution)/shard_map/all_gather | solution.py:169
  308.0 5.5 convolution_convert_fusion.8
  316.4 10.2 all-gather.1
  327.4 11.4 all_gather.50
  339.1 118.5 %all-gather.16.cloned.1.call-done = bf16[2048,2048]{1,0:T(8,128)(2,1)} async-done(((bf16[2048,512]{1,0:T(8,128)(2,1)}), bf16[2048,2048]{1,0:T(8,128)(2,1)}) %all-gather.16.cloned.1.call-update) | async-done | bytes 8388624 | tf_op jit(solution)/shard_map/all_gather | solution.py:168
  463.3 40.9 %all-gather.14.cloned.1.call-done = bf16[512,2048]{1,0:T(8,128)(2,1)} async-done(((bf16[128,2048]{1,0:T(8,128)(2,1)}), bf16[512,2048]{1,0:T(8,128)(2,1)}) %all-gather.14.cloned.1.call-update) | async-done | bytes 2097168 | tf_op jit(solution)/shard_map/all_gather | solution.py:188
  508.1 42.8 %all-gather.20.cloned.1.call-done = bf16[512,2048]{1,0:T(8,128)(2,1)} async-done(((bf16[128,2048]{1,0:T(8,128)(2,1)}), bf16[512,2048]{1,0:T(8,128)(2,1)}) %all-gather.20.cloned.1.call-update) | async-done | bytes 2097168 | tf_op jit(solution)/shard_map/all_gather | solution.py:187
  555.7 46.0 %while.32 = (s32[]{:T(128)}, bf16[4,128,8,64]{1,3,2,0:T(8,128)(2,1)}, f32[4,8,128]{2,1,0:T(8,128)S(1)}, bf16[4,512,8,64]{1,3,2,0:T(8,128)(2,1)}, bf16[4,128,8,64...) while((s32[]{:T(128)}, ...), condition=%wide.region_4.5_spmd.clone, body=%wide.region_1.4_spmd.clone.sunk | while | flops 138411520 | bytes 35106080 | solution.py:90
  601.7 98.5 %all-gather.22.cloned.1.call-done = bf16[2048,2048]{1,0:T(8,128)(2,1)} async-done(((bf16[512,2048]{1,0:T(8,128)(2,1)}), bf16[2048,2048]{1,0:T(8,128)(2,1)}) %all-gather.22.cloned.1.call-update) | async-done | bytes 8388624 | tf_op jit(solution)/shard_map/all_gather | solution.py:171
  700.2 4.9 multiply_reduce_fusion.3
  705.4 351.9 %all-gather.24.cloned.1.call-done = bf16[2048,5120]{1,0:T(8,128)(2,1)} async-done(((bf16[2048,1280]{1,0:T(8,128)(2,1)}), bf16[2048,5120]{1,0:T(8,128)(2,1)}) %all-gather.24.cloned.1.call-update) | async-done | bytes 20971536 | tf_op jit(solution)/shard_map/all_gather | solution.py:203
  1057.3 11.3 fusion.89
  1068.6 345.7 %all-gather.26.cloned.1.call-done = bf16[2048,5120]{1,0:T(8,128)(2,1)} async-done(((bf16[2048,1280]{1,0:T(8,128)(2,1)}), bf16[2048,5120]{1,0:T(8,128)(2,1)}) %all-gather.26.cloned.1.call-update) | async-done | bytes 20971536 | tf_op jit(solution)/shard_map/all_gather | solution.py:204
  1414.3 11.3 fusion.90
  1425.6 345.7 %all-gather.28.cloned.1.call-done = bf16[5120,2048]{1,0:T(8,128)(2,1)} async-done(((bf16[1280,2048]{1,0:T(8,128)(2,1)}), bf16[5120,2048]{1,0:T(8,128)(2,1)}) %all-gather.28.cloned.1.call-update) | async-done | bytes 20971536 | tf_op jit(solution)/shard_map/all_gather | solution.py:205
  1771.3 14.3 multiply_convert_fusion.1
  1785.7 12.4 fusion.91
  1798.0 13.4 multiply_reduce_fusion.1
  1819.0 106.5 %while.33 = (s32[]{:T(128)}, bf16[4,128,8,64]{1,3,2,0:T(8,128)(2,1)}, bf16[4,512,8,64]{1,3,2,0:T(8,128)(2,1)}, bf16[4,512,8,64]{1,3,2,0:T(8,128)(2,1)}, f32[4,8,...) while((s32[]{:T(128)}, ...), condition=%wide.region_10.11_spmd.clone, body=%wide.region_7.10_spmd.clone.sunk | while | flops 341570048 | bytes 102152648 | solution.py:132
  1822.8 4.9 reshape.225
  1849.3 4.9 reshape.225
  1875.9 4.9 reshape.225
  1932.1 6.9 convolution_convert_fusion.6
  1940.4 5.6 convolution_convert_fusion.3
  1946.0 26.9 reduce-scatter.28.cloned.1.call-done
  1972.9 6.9 convolution_convert_fusion.5
  1979.9 39.2 reduce-scatter.30.cloned.1.call-done
  2019.1 6.9 convolution_convert_fusion.4
  2027.5 10.1 convolution_convert_fusion.2
  2038.9 10.1 convolution_convert_fusion.1
  2050.5 10.1 convolution_convert_fusion
  2060.9 106.3 %reduce-scatter.14.cloned.1.call-done = bf16[2048,512]{1,0:T(8,128)(2,1)} async-done(((bf16[2048,2048]{1,0:T(8,128)(2,1)}), bf16[2048,512]{1,0:T(8,128)(2,1)}) %reduce-scatter.14.cloned.1.call-update) | async-done | bytes 2097168 | tf_op jit(solution)/shard_map/reduce_scatter | solution.py:298
  2167.2 147.6 %reduce-scatter.20.cloned.1.call-done = bf16[512,2048]{1,0:T(8,128)(2,1)} async-done(((bf16[2048,2048]{1,0:T(8,128)(2,1)}), bf16[512,2048]{1,0:T(8,128)(2,1)}) %reduce-scatter.20.cloned.1.call-update) | async-done | bytes 2097168 | tf_op jit(solution)/shard_map/reduce_scatter | solution.py:307
  2314.7 148.0 %reduce-scatter.16.cloned.1.call-done = bf16[2048,512]{1,0:T(8,128)(2,1)} async-done(((bf16[2048,2048]{1,0:T(8,128)(2,1)}), bf16[2048,512]{1,0:T(8,128)(2,1)}) %reduce-scatter.16.cloned.1.call-update) | async-done | bytes 2097168 | tf_op jit(solution)/shard_map/reduce_scatter | solution.py:301
  2462.8 148.0 %reduce-scatter.18.cloned.1.call-done = bf16[2048,512]{1,0:T(8,128)(2,1)} async-done(((bf16[2048,2048]{1,0:T(8,128)(2,1)}), bf16[2048,512]{1,0:T(8,128)(2,1)}) %reduce-scatter.18.cloned.1.call-update) | async-done | bytes 2097168 | tf_op jit(solution)/shard_map/reduce_scatter | solution.py:304
  2610.8 350.9 %reduce-scatter.22.cloned.1.call-done = bf16[2048,1280]{1,0:T(8,128)(2,1)} async-done(((bf16[2048,5120]{1,0:T(8,128)(2,1)}), bf16[2048,1280]{1,0:T(8,128)(2,1)}) %reduce-scatter.22.cloned.1.call-update) | async-done | bytes 5242896 | tf_op jit(solution)/shard_map/reduce_scatter | solution.py:224
  2961.6 351.0 %reduce-scatter.24.cloned.1.call-done = bf16[2048,1280]{1,0:T(8,128)(2,1)} async-done(((bf16[2048,5120]{1,0:T(8,128)(2,1)}), bf16[2048,1280]{1,0:T(8,128)(2,1)}) %reduce-scatter.24.cloned.1.call-update) | async-done | bytes 5242896 | tf_op jit(solution)/shard_map/reduce_scatter | solution.py:230
  3312.7 350.9 %reduce-scatter.26.cloned.1.call-done = bf16[1280,2048]{1,0:T(8,128)(2,1)} async-done(((bf16[5120,2048]{1,0:T(8,128)(2,1)}), bf16[1280,2048]{1,0:T(8,128)(2,1)}) %reduce-scatter.26.cloned.1.call-update) | async-done | bytes 5242896 | tf_op jit(solution)/shard_map/reduce_scatter | solution.py:236
  3666.5 6.6 fusion.92
  3673.1 12.0 fusion.51
  3691.2 11.8 all-reduce.8
  3703.2 15.7 all-reduce.6
  3721.8 248.0 %all-reduce.11.cloned.1.call-done = (bf16[2048,512]{1,0:T(8,128)(2,1)}, bf16[2048,512]{1,0:T(8,128)(2,1)}, bf16[2048,512]{1,0:T(8,128)(2,1)}, bf16[512,2048]{1,0...) async-done(((bf16[2048,512]{1,0:T(8,128)(2,1)}, bf16[2048,512]{1,0:T(8,128)(2,1)}, bf16[2048,512]{1,0:T(8,128)(2,1)}, ...) | async-done | bytes 24117264 | tf_op jit(solution)/shard_map/psum | solution.py:316
  3983.3 5.2 convert_element_type.276
  3993.4 5.5 convert_element_type.280
  (360 shorter events, 205.6 us)
Async XLA Ops:
  7.2 151.3 %all-gather.12.cloned.1.call-start = ((), (), s32[]{:S(2)}) async-start(), calls=%async_computation.9 | async-start | bytes 10485760 | tf_op jit(solution)/shard_map/all_gather | solution.py:170
  7.9 9.1 copy-start
  7.9 300.0 %all-gather.18.cloned.1.call-start = ((), (), s32[]{:S(2)}) async-start(), calls=%async_computation.12 | async-start | bytes 10485760 | tf_op jit(solution)/shard_map/all_gather | solution.py:169
  8.7 448.9 %all-gather.16.cloned.1.call-start = ((), (), s32[]{:S(2)}) async-start(), calls=%async_computation.11 | async-start | bytes 10485760 | tf_op jit(solution)/shard_map/all_gather | solution.py:168
  9.4 494.8 %all-gather.14.cloned.1.call-start = ((), (), s32[]{:S(2)}) async-start(), calls=%async_computation.10 | async-start | bytes 2621440 | tf_op jit(solution)/shard_map/all_gather | solution.py:188
  17.1 440.5 %copy-start.16 = (f32[4,1,512]{2,1,0:T(1,128)}, f32[4,1,512]{2,1,0:T(1,128)S(1)}, u32[]{:S(2)}) copy-start(f32[4,1,512]{2,1,0:T(1,128)S(1)} %convert_element_type.283) | copy-start | bytes 24580
  17.2 146.8 %copy-start.39 = (f32[128]{0:T(128)}, f32[128]{0:T(128)S(1)}, u32[]{:S(2)}) copy-start(f32[128]{0:T(128)S(1)} %fusion.60) | copy-start | bytes 1540
  17.3 440.3 %copy-start.30 = (f32[128]{0:T(128)}, f32[128]{0:T(128)S(1)}, u32[]{:S(2)}) copy-start(f32[128]{0:T(128)S(1)} %fusion.81) | copy-start | bytes 1540
  164.0 386.8 %all-gather.20.cloned.1.call-start = ((), (), s32[]{:S(2)}) async-start(), calls=%async_computation.13 | async-start | bytes 2621440 | tf_op jit(solution)/shard_map/all_gather | solution.py:187
  313.5 386.8 %all-gather.22.cloned.1.call-start = ((), (), s32[]{:S(2)}) async-start(), calls=%async_computation.14 | async-start | bytes 10485760 | tf_op jit(solution)/shard_map/all_gather | solution.py:171
  314.0 743.2 %all-gather.24.cloned.1.call-start = ((), (), s32[]{:S(2)}) async-start(), calls=%async_computation.15 | async-start | bytes 26214400 | tf_op jit(solution)/shard_map/all_gather | solution.py:203
  314.8 1099.5 %all-gather.26.cloned.1.call-start = ((), (), s32[]{:S(2)}) async-start(), calls=%async_computation.16 | async-start | bytes 26214400 | tf_op jit(solution)/shard_map/all_gather | solution.py:204
  315.6 11.7 copy-start.33
  315.6 11.8 copy-start.36
  315.6 1455.8 %all-gather.28.cloned.1.call-start = ((), (), s32[]{:S(2)}) async-start(), calls=%async_computation.17 | async-start | bytes 26214400 | tf_op jit(solution)/shard_map/all_gather | solution.py:205
  316.3 1656.6 %reduce-scatter.28.cloned.1.call-start = ((), (), s32[]{:S(2)}) async-start(), calls=%async_computation.25 | async-start | bytes 2621440
  327.4 134.9 %copy-start.34 = (s32[639]{0:T(1024)}, s32[639]{0:T(1024)S(1)}, u32[]{:S(2)}) copy-start(s32[639]{0:T(1024)S(1)} %dynamic_slice.55) | copy-start | bytes 7672
  705.2 1106.3 %copy-start.3 = (f32[128,2048]{1,0:T(8,128)}, f32[128,2048]{1,0:T(8,128)S(1)}, u32[]{:S(2)}) copy-start(f32[128,2048]{1,0:T(8,128)S(1)} %get-tuple-element.324) | copy-start | bytes 3145732
  705.4 708.9 %copy-start.7 = (bf16[128,2048]{1,0:T(8,128)(2,1)}, bf16[128,2048]{1,0:T(8,128)(2,1)S(1)}, u32[]{:S(2)}) copy-start(bf16[128,2048]{1,0:T(8,128)(2,1)S(1)} %multiply_convert_fusion.3) | copy-start | bytes 1572868
  1068.6 702.7 %copy-start.18 = (bf16[1,128,2048]{2,1,0:T(8,128)(2,1)S(1)}, bf16[1,128,2048]{2,1,0:T(8,128)(2,1)}, u32[]{:S(2)}) copy-start(bf16[1,128,2048]{2,1,0:T(8,128)(2,1)} %param.31) | copy-start | bytes 1572868
  1785.7 12.4 copy-start.9
  1798.0 16.1 slice-start.2
  1798.0 16.1 slice-start.3
  1925.4 4.1 copy-start.28
  1929.5 89.6 %reduce-scatter.30.cloned.1.call-start = ((), (), s32[]{:S(2)}) async-start(), calls=%async_computation.26 | async-start | bytes 2621440
  1932.0 235.1 %reduce-scatter.14.cloned.1.call-start = ((), (), s32[]{:S(2)}) async-start(), calls=%async_computation.18 | async-start | bytes 10485760 | tf_op jit(solution)/shard_map/reduce_scatter | solution.py:298
  1939.0 375.7 %reduce-scatter.20.cloned.1.call-start = ((), (), s32[]{:S(2)}) async-start(), calls=%async_computation.21 | async-start | bytes 10485760 | tf_op jit(solution)/shard_map/reduce_scatter | solution.py:307
  1946.0 516.8 %reduce-scatter.16.cloned.1.call-start = ((), (), s32[]{:S(2)}) async-start(), calls=%async_computation.19 | async-start | bytes 10485760 | tf_op jit(solution)/shard_map/reduce_scatter | solution.py:301
  1979.8 630.9 %reduce-scatter.18.cloned.1.call-start = ((), (), s32[]{:S(2)}) async-start(), calls=%async_computation.20 | async-start | bytes 10485760 | tf_op jit(solution)/shard_map/reduce_scatter | solution.py:304
  2026.0 935.6 %reduce-scatter.22.cloned.1.call-start = ((), (), s32[]{:S(2)}) async-start(), calls=%async_computation.22 | async-start | bytes 26214400 | tf_op jit(solution)/shard_map/reduce_scatter | solution.py:224
  2037.7 1275.0 %reduce-scatter.24.cloned.1.call-start = ((), (), s32[]{:S(2)}) async-start(), calls=%async_computation.23 | async-start | bytes 26214400 | tf_op jit(solution)/shard_map/reduce_scatter | solution.py:230
  2049.1 1614.5 %reduce-scatter.26.cloned.1.call-start = ((), (), s32[]{:S(2)}) async-start(), calls=%async_computation.24 | async-start | bytes 26214400 | tf_op jit(solution)/shard_map/reduce_scatter | solution.py:236
  2060.7 1909.1 %all-reduce.11.cloned.1.call-start = ((), (), s32[]{:S(2)}) async-start(), calls=%async_computation.27 | async-start | bytes 48234496 | tf_op jit(solution)/shard_map/psum | solution.py:316
  3666.4 6.7 copy-start.4
  3666.4 18.7 slice-start.6
  3666.5 21.6 slice-start.4
  3673.1 12.1 slice-start.7
  3673.1 12.0 copy-start.29
  3673.1 14.9 slice-start.5
  3688.1 32.5 copy-start.40
  3969.8 4.4 copy-start.22
  3974.1 9.1 slice-start.12
  3976.9 3.7 copy-start.20
  3976.9 6.4 slice-start.13
  3980.6 7.9 slice-start.10
  3983.3 5.2 slice-start.11
  3983.3 10.1 slice-start.8
  3988.5 4.9 slice-start.9
  (54 other events, 99.0 us)
Sparse Core Ops, SparseCore 0:
  9.6 148.8 all-gather.11
  160.1 147.8 all-gather.17
  309.5 147.9 all-gather.15
  459.6 44.5 all-gather.13
  506.2 44.6 all-gather.19
  552.3 147.8 all-gather.21
  701.8 355.4 all-gather.23
  1058.9 355.3 all-gather.25
  1415.9 355.3 all-gather.27
  1929.7 43.2 reduce-scatter.27
  1975.9 43.1 reduce-scatter.29
  2021.9 145.2 reduce-scatter.13
  2169.5 145.1 reduce-scatter.19
  2317.5 145.1 reduce-scatter.15
  2465.5 145.1 reduce-scatter.17
  2613.0 348.6 reduce-scatter.21
  2964.0 348.6 reduce-scatter.23
  3314.9 348.6 reduce-scatter.25
  3669.6 300.1 all-reduce.10
where the time goes:
time: 4020 us; the launch traced here: 4010 us
  waiting for transfers between devices  3550 us (88%)
  matrix products  211 us (5%)
  local copies, waits for them, and re-layouts  117 us (3%)
  blocking collectives  56.6 us (1%)
  other arithmetic  50.8 us (1%)
    all_gather x1, waiting for transfers between devices, local(): lax.all_gather(w_gate, 'group', axis=1, tiled=True)  352 us
    reduce_scatter x1, waiting for transfers between devices, local(): lax.psum_scatter(inner_rows(normed_two, grad_up).astype(jnp.bfloat16), 'g...  351 us
    reduce_scatter x1, waiting for transfers between devices, local(): lax.psum_scatter(inner_rows(hidden_low, grad_low).astype(jnp.bfloat16), '...  351 us
    reduce_scatter x1, waiting for transfers between devices, local(): lax.psum_scatter(inner_rows(normed_two, grad_gate).astype(jnp.bfloat16),...  351 us
    all_gather x1, waiting for transfers between devices, local(): lax.all_gather(w_ffn_out, 'group', axis=0, tiled=True)  346 us
    all_gather x1, waiting for transfers between devices, local(): lax.all_gather(w_up, 'group', axis=1, tiled=True)  346 us
    psum x1, waiting for transfers between devices, local(): lax.psum(query_part.astype(jnp.bfloat16), 'replica').astype(jnp.float32)  248 us
    reduce_scatter x1, waiting for transfers between devices, local(): lax.psum_scatter(key_grad.astype(jnp.bfloat16), 'group', scatter_dimensio...  148 us
  transfers between devices with their start and end apart: 19, of which 19 were waited for; matrix products, arithmetic and copies ran while one was open for 4% of the time, Pallas kernels for 0%

commit v1 on v0

v1 whole, which is shorter than its diff:
```python
import jax
import jax.numpy as jnp
from jax import lax
from jax.sharding import PartitionSpec as P

epsilon = 1e-06
negative = -1000000000.0
highest = lax.Precision.HIGHEST
head_dim = 64


def rms_scale(values, gain):
    return values * lax.rsqrt(jnp.mean(values * values, axis=-1, keepdims=True) + epsilon) * gain


def gated_gelu(gate_pre, up_pre):
    return jax.nn.gelu(gate_pre, approximate=True) * up_pre


def rows_dot(left, right):
    return lax.dot_general(
        left, right, (((0,), (0,)), ((), ())), preferred_element_type=jnp.float32
    )


def cols_dot(left, right):
    return lax.dot_general(
        left, right, (((1,), (1,)), ((), ())), preferred_element_type=jnp.float32
    )


def plain_dot(left, right):
    return jnp.dot(left, right, preferred_element_type=jnp.float32)


def spread_offsets(vector, row_count, col_count):
    span_width = row_count + col_count + 1
    block_heads = vector.shape[0]
    tiled_rows = jnp.broadcast_to(vector[:, None, :], (block_heads, row_count, span_width))
    flattened = tiled_rows.reshape(block_heads, row_count * span_width)[
        :, : row_count * (span_width - 1)
    ]
    return flattened.reshape(block_heads, row_count, span_width - 1)[:, :, row_count:]


def fold_offsets(matrix):
    block_heads, row_count, col_count = matrix.shape
    padded = jnp.pad(matrix, ((0, 0), (0, 0), (row_count, 0)))
    flattened = jnp.pad(
        padded.reshape(block_heads, row_count * (row_count + col_count)), ((0, 0), (0, row_count))
    )
    sums_all = flattened.reshape(block_heads, row_count, row_count + col_count + 1).sum(axis=1)
    return sums_all[:, 1 : row_count + col_count]


def heads(matrix):
    return matrix.reshape(matrix.shape[0], -1, head_dim)


def local(
    inputs,
    seq_lengths,
    bucket_ids,
    norm1_gain,
    w_query,
    w_key,
    w_value,
    w_attn_out,
    bias_table,
    norm2_gain,
    w_gate,
    w_up,
    w_ffn_out,
    cotangent,
):
    group = lax.axis_index("group")
    rows = inputs.shape[1]
    length = seq_lengths[0]
    total = rows * lax.axis_size("group")
    start = group * rows
    valid = jnp.arange(total) < length

    def gather(values):
        return lax.all_gather(values, "group", axis=0, tiled=True)

    def scatter(values):
        return lax.psum_scatter(
            values.astype(jnp.bfloat16), "group", scatter_dimension=0, tiled=True
        ).astype(jnp.float32)

    x_all_low = gather(inputs[0])
    g_all = jnp.where(valid[:, None], gather(cotangent[0]), jnp.bfloat16(0))
    gains = lax.all_gather(jnp.stack([norm1_gain, norm2_gain]), "group", axis=1, tiled=True)
    gains = gains.astype(jnp.float32)
    gain_first, gain_second = gains[0], gains[1]
    x_local = inputs[0].astype(jnp.float32)
    normed_one = rms_scale(x_all_low.astype(jnp.float32), gain_first).astype(jnp.bfloat16)
    query = plain_dot(normed_one, w_query).astype(jnp.bfloat16)
    key = plain_dot(normed_one, w_key).astype(jnp.bfloat16)
    value = plain_dot(normed_one, w_value).astype(jnp.bfloat16)

    buckets = bias_table.shape[0]
    one_hot = (bucket_ids[:, None] == jnp.arange(buckets)[None, :]).astype(jnp.float32)
    per_offset = jnp.dot(one_hot, bias_table.astype(jnp.float32), precision=highest)
    bias = spread_offsets(jnp.pad(per_offset.T, ((0, 0), (1, 1))), total, total)
    scores = jnp.einsum(
        "qhd,khd->hqk", heads(query), heads(key), preferred_element_type=jnp.float32
    )
    scores = jnp.where(valid[None, None, :], scores + bias, negative)
    probs = jax.nn.softmax(scores, axis=-1)
    probs_low = probs.astype(jnp.bfloat16)
    attended = jnp.einsum(
        "hqk,khd->qhd", probs_low, heads(value), preferred_element_type=jnp.float32
    )
    attended = attended.reshape(total, -1).astype(jnp.bfloat16)
    middle = x_local + scatter(plain_dot(attended, w_attn_out))
    normed_two = gather(rms_scale(middle, gain_second).astype(jnp.bfloat16))

    gate_pre = plain_dot(normed_two, w_gate)
    up_pre = plain_dot(normed_two, w_up)
    hidden_low = gated_gelu(gate_pre, up_pre).astype(jnp.bfloat16)
    grad_hidden = cols_dot(g_all, w_ffn_out)
    _, pull_gelu = jax.vjp(gated_gelu, gate_pre, up_pre)
    grad_gate, grad_up = pull_gelu(grad_hidden)
    grad_gate = grad_gate.astype(jnp.bfloat16)
    grad_up = grad_up.astype(jnp.bfloat16)
    grad_normed_two = scatter(cols_dot(grad_gate, w_gate) + cols_dot(grad_up, w_up))
    ffn_out_grad = rows_dot(hidden_low, g_all)
    gate_grad = rows_dot(normed_two, grad_gate)
    up_grad = rows_dot(normed_two, grad_up)

    def total_sum(values):
        return lax.psum(values.astype(jnp.bfloat16), "replica").astype(jnp.float32)

    ffn_out_grad, gate_grad, up_grad = (
        total_sum(ffn_out_grad), total_sum(gate_grad), total_sum(up_grad)
    )
    result = (middle + scatter(plain_dot(hidden_low, w_ffn_out))).astype(jnp.bfloat16)

    row_valid = start + jnp.arange(rows) < length
    g_local = jnp.where(row_valid[:, None], cotangent[0], jnp.bfloat16(0)).astype(jnp.float32)
    _, pull_two = jax.vjp(rms_scale, middle, gain_second)
    grad_mid_norm, gain_two_grad = pull_two(grad_normed_two)
    grad_middle = g_local + grad_mid_norm
    grad_branch = gather(grad_middle.astype(jnp.bfloat16))

    attn_out_grad = rows_dot(attended, grad_branch)
    grad_attended = cols_dot(grad_branch, w_attn_out).astype(jnp.bfloat16)
    grad_probs = jnp.einsum(
        "qhd,khd->hqk", heads(grad_attended), heads(value), preferred_element_type=jnp.float32
    )
    inner_sum = jnp.sum(probs * grad_probs, axis=-1, keepdims=True)
    grad_scores = (probs * (grad_probs - inner_sum)).astype(jnp.bfloat16)

    def merge(values):
        return values.reshape(total, -1).astype(jnp.bfloat16)

    grad_query = merge(
        jnp.einsum("hqk,khd->qhd", grad_scores, heads(key), preferred_element_type=jnp.float32)
    )
    grad_key = merge(
        jnp.einsum("hqk,qhd->khd", grad_scores, heads(query), preferred_element_type=jnp.float32)
    )
    grad_value = merge(
        jnp.einsum(
            "hqk,qhd->khd", probs_low, heads(grad_attended), preferred_element_type=jnp.float32
        )
    )
    offset_sums = fold_offsets(grad_scores.astype(jnp.float32))
    table_grad = jnp.dot(offset_sums, one_hot, precision=highest).T
    query_grad = rows_dot(normed_one, grad_query)
    key_grad = rows_dot(normed_one, grad_key)
    value_grad = rows_dot(normed_one, grad_value)
    grad_normed_one = scatter(
        cols_dot(grad_query, w_query) + cols_dot(grad_key, w_key) + cols_dot(grad_value, w_value)
    )
    query_grad, key_grad, value_grad, attn_out_grad = (
        total_sum(query_grad), total_sum(key_grad), total_sum(value_grad), total_sum(attn_out_grad)
    )
    table_grad = lax.psum(table_grad, "replica")
    _, pull_one = jax.vjp(rms_scale, x_local, gain_first)
    grad_in_norm, gain_one_grad = pull_one(grad_normed_one)
    input_grad = (grad_middle + grad_in_norm).astype(jnp.bfloat16)
    gain_sums = lax.psum(jnp.stack([gain_one_grad, gain_two_grad]), ("replica", "group"))
    width = norm1_gain.shape[0]
    gain_sums = lax.dynamic_slice_in_dim(gain_sums, group * width, width, axis=1)
    return (
        result[None],
        input_grad[None],
        gain_sums[0],
        query_grad,
        key_grad,
        value_grad,
        attn_out_grad,
        table_grad,
        gain_sums[1],
        gate_grad,
        up_grad,
        ffn_out_grad,
    )

def solution(mesh):
    placed = (
        P("replica", "group", None),
        P("replica"),
        P(),
        P("group"),
        P(None, "group"),
        P(None, "group"),
        P(None, "group"),
        P("group", None),
        P(None, "group"),
        P("group"),
        P(None, "group"),
        P(None, "group"),
        P("group", None),
        P("replica", "group", None),
    )
    return jax.shard_map(
        local,
        mesh=mesh,
        in_specs=placed,
        out_specs=(
            P("replica", "group", None),
            P("replica", "group", None),
            P("group"),
            P(None, "group"),
            P(None, "group"),
            P(None, "group"),
            P("group", None),
            P(None, "group"),
            P("group"),
            P(None, "group"),
            P(None, "group"),
            P("group", None),
        ),
        check_vma=False,
    )
```

time: 4020 us -> 862 us (0.21)
  waiting for transfers between devices: 3550 us -> 427 us
  matrix products: 211 us -> 118 us
  local copies, waits for them, and re-layouts: 117 us -> 160 us
    reduce_scatter x7 -> x4, waiting for transfers between devices: 1600 us -> 90.9 us  [scatter(): lax.psum_scatter(values.astype(jnp.bfloat16), 'group', scatter_dimension=...]
    all_gather x9 -> x4, waiting for transfers between devices: 1630 us -> 119 us  [gather(): return lax.all_gather(values, 'group', axis=0, tiled=True)]
    dot_general x51 -> x29, matrix products: 211 us -> 118 us  [the longest x7 31.9 us: cols_dot(): lax.dot_general(left, right, (((1,), (1,)), ((), ())), preferred_element_...]
    unnamed x102 -> x95, local copies, waits for them, and re-layouts: 14.8 us -> 93.3 us
    unnamed x21 -> x9, waiting for transfers between devices: 71 us -> 1.32 us
  transfers between devices with their start and end apart: 19 -> 9, of which waited for: 19 -> 6; matrix products, arithmetic and copies ran while one was open for 4% -> 26% of each run, Pallas kernels for 0% -> 0%
where the time goes in v1:
time: 862 us; the launch traced here: 853 us
  waiting for transfers between devices  427 us (50%)
  local copies, waits for them, and re-layouts  160 us (19%)
  matrix products  118 us (14%)
  other arithmetic  68.9 us (8%)
  blocking collectives  62.6 us (7%)
  between operations  15.4 us (2%)
    psum x1, waiting for transfers between devices, total_sum(): return lax.psum(values.astype(jnp.bfloat16), 'replica').astype(jnp.float32)  215 us
    all_gather x4, waiting for transfers between devices, gather(): return lax.all_gather(values, 'group', axis=0, tiled=True)  119 us
    unnamed x95, local copies, waits for them, and re-layouts  93.3 us
    reduce_scatter x4, waiting for transfers between devices, scatter(): lax.psum_scatter(values.astype(jnp.bfloat16), 'group', scatter_dimension=...  90.9 us
    psum x1, blocking collectives, local(): lax.psum(jnp.stack([gain_one_grad, gain_two_grad]), ('replica', 'group'))  42 us
    dot_general x7, matrix products, cols_dot(): lax.dot_general(left, right, (((1,), (1,)), ((), ())), preferred_element_...  31.9 us
    dot_general x7, matrix products, plain_dot(): return jnp.dot(left, right, preferred_element_type=jnp.float32)  31.1 us
    reshape x1, local copies, waits for them, and re-layouts, fold_offsets(): flattened.reshape(block_heads, row_count, row_count + col_count + 1)  30.6 us
  transfers between devices with their start and end apart: 9, of which 6 were waited for; matrix products, arithmetic and copies ran while one was open for 26% of the time, Pallas kernels for 0%

profile of v1, /device:TPU:17, one launch (start us, length us, event | category | flops | bytes accessed | tf_op | source)
XLA Modules:
  0.0 852.7 jit_solution(4421860915725678596)
XLA Ops:
  11.1 7.8 broadcast_in_dim.67
  18.9 25.4 %reshape.150 = f32[4198400]{0:T(1024)} reshape(f32[8,512,1025]{2,1,0:T(8,128)} %broadcast_in_dim.67) | data formatting | bytes 33587200
  44.3 16.4 %reshape.135 = f32[8,524800]{1,0:T(8,128)} reshape(f32[4198400]{0:T(1024)} %reshape.150) | data formatting | bytes 33587200 | tf_op jit(solution)/shard_map/reshape | solution.py:40
  60.8 5.8 slice-done
  66.5 16.0 %copy.45 = f32[1,8,512,1024]{3,2,1,0:T(8,128)S(1)} copy(f32[1,8,512,1024]{3,1,2,0:T(8,128)S(1)} %bitcast.126) | data formatting | bytes 33554432
  82.5 4.4 slice.30
  86.9 9.1 %copy.40 = f32[8,512,512]{1,2,0:T(8,128)} copy(f32[8,512,512]{2,1,0:T(8,128)} %slice.30) | data formatting | bytes 16777216
  96.1 7.7 all_gather.16
  106.1 3.8 convolution_convert_fusion.13
  114.3 5.0 fusion.52
  121.8 8.1 fusion.15
  132.6 47.5 %reduce-scatter.5.cloned.1.call-done = bf16[128,2048]{1,0:T(8,128)(2,1)} async-done(((bf16[512,2048]{1,0:T(8,128)(2,1)}), bf16[128,2048]{1,0:T(8,128)(2,1)}) %reduce-scatter.5.cloned.1.call-update) | async-done | bytes 524304 | tf_op jit(solution)/shard_map/reduce_scatter | solution.py:87
  184.4 43.8 %all-gather.7.cloned.1.call-done = bf16[512,2048]{1,0:T(8,128)(2,1)} async-done(((bf16[128,2048]{1,0:T(8,128)(2,1)}), bf16[512,2048]{1,0:T(8,128)(2,1)}) %all-gather.7.cloned.1.call-update) | async-done | bytes 2097168 | tf_op jit(solution)/shard_map/all_gather | solution.py:84
  228.2 7.6 fusion.53
  235.9 7.2 fusion.54
  243.0 31.4 %all-gather.13.cloned.1.call-done = bf16[1,512,2048]{2,1,0:T(8,128)(2,1)} async-done(((bf16[1,128,2048]{2,1,0:T(8,128)(2,1)}), bf16[1,512,2048]{2,1,0:T(8,128)(2,1)}) %all-gather.13.cloned.1.call-update) | async-done | bytes 2097168 | tf_op jit(solution)/shard_map/all_gather | solution.py:84
  274.4 10.4 %multiply_convert_fusion.1 = (bf16[512,1280]{1,0:T(8,128)(2,1)S(1)}, bf16[512,1280]{1,0:T(8,128)(2,1)S(1)}, bf16[512,1280]{1,0:T(8,128)(2,1)}) fusion(f32[512,1280]{1,0:T(8,128)} %fusion.53, f32[512,1280]{1,0:T(8,128)} %fusion.54, bf16[1280,2048]{1,0:T(8,128)(2,1)} %param.26, bf16[1,512,2048]{2,1,0:T(8,128)(2,1)} %all-gather.13.cloned.1.call-done, ...), kind=kOutput, calls=%fused_computation.34 | convolution fusion | flops 2702442496 | bytes 16515584 | tf_op jit(solution)/shard_map/dot_general | solution.py:27
  284.8 5.8 fusion.55
  290.6 6.7 add_convert_fusion.1
  297.4 43.4 %reduce-scatter.9.cloned.1.call-done = bf16[128,2048]{1,0:T(8,128)(2,1)} async-done(((bf16[512,2048]{1,0:T(8,128)(2,1)}), bf16[128,2048]{1,0:T(8,128)(2,1)}) %reduce-scatter.9.cloned.1.call-update) | async-done | bytes 524304 | tf_op jit(solution)/shard_map/reduce_scatter | solution.py:87
  345.4 44.2 %all-gather.9.cloned.1.call-done = bf16[512,2048]{1,0:T(8,128)(2,1)} async-done(((bf16[128,2048]{1,0:T(8,128)(2,1)}), bf16[512,2048]{1,0:T(8,128)(2,1)}) %all-gather.9.cloned.1.call-update) | async-done | bytes 2097168 | tf_op jit(solution)/shard_map/all_gather | solution.py:84
  389.6 3.7 convolution_convert_fusion.11
  393.3 8.2 fusion.18
  401.6 4.8 multiply_reduce_fusion
  416.7 2.7 add_convert_fusion
  419.7 7.1 convolution_convert_fusion.7
  426.9 7.3 convolution_convert_fusion.1
  434.2 4.7 convolution_convert_fusion.2
  438.9 4.8 convolution_convert_fusion
  443.7 6.7 copy.41
  450.3 6.7 pad_bitcast_fusion
  457.0 11.7 %copy.43 = bf16[1,8,512,1024]{3,1,2,0:T(8,128)(2,1)} copy(bf16[1,8,512,1024]{3,2,1,0:T(8,128)(2,1)} %pad_bitcast_fusion) | data formatting | bytes 16777216
  468.7 2.6 convolution_convert_fusion.3
  471.3 2.9 convolution_convert_fusion.4
  474.2 2.9 convolution_convert_fusion.5
  477.0 2.9 convolution_convert_fusion.6
  479.9 10.2 %pad_convert_fusion = f32[8,524800]{1,0:T(8,128)} fusion(bf16[8,524288]{1,0:T(8,128)(2,1)} %bitcast.132), kind=kLoop, calls=%fused_computation.2 | loop fusion | flops 4198400 | bytes 25182208 | tf_op jit(solution)/shard_map/reshape | solution.py:52
  490.1 12.7 %reshape.152 = f32[4198400]{0:T(1024)} reshape(f32[8,524800]{1,0:T(8,128)} %pad_convert_fusion) | data formatting | bytes 33587200
  502.9 30.6 %reshape.144 = f32[8,512,1025]{2,1,0:T(8,128)} reshape(f32[4198400]{0:T(1024)} %reshape.152) | data formatting | bytes 33587200 | tf_op jit(solution)/shard_map/reshape | solution.py:52
  533.4 7.8 reduce_sum.104
  541.6 12.9 %psum.68 = f32[32,8]{0,1:T(8,128)} all-reduce(f32[32,8]{0,1:T(8,128)S(1)} %fusion.35), channel_id=1, replica_groups=mesh['replica'=8,'group'=4] {'replica'}, use_global_device_ids=true, to_apply=%region_20.21 | all-reduce | flops 256 | bytes 2048 | tf_op jit(solution)/shard_map/psum | solution.py:180
  556.2 42.0 %psum.63 = f32[2,2048]{1,0:T(2,128)S(1)} all-reduce(f32[2,2048]{1,0:T(2,128)S(1)} %pad_maximum_fusion), channel_id=1, replica_groups=mesh['replica'=8,'group'=4] {'replica','group'}, use_global_device_ids=true, to_apply=%region_14.15 | all-reduce | flops 4096 | bytes 32768 | tf_op jit(solution)/shard_map/psum | solution.py:184
  598.8 3.3 fusion.34
  602.1 214.9 %all-reduce.6.cloned.1.call-done = (bf16[2048,512]{1,0:T(8,128)(2,1)}, bf16[2048,512]{1,0:T(8,128)(2,1)}, bf16[2048,512]{1,0:T(8,128)(2,1)}, bf16[512,2048]{1,0:...) async-done(((bf16[2048,512]{1,0:T(8,128)(2,1)}, bf16[2048,512]{1,0:T(8,128)(2,1)}, bf16[2048,512]{1,0:T(8,128)(2,1)}, ...) | async-done | bytes 24117264 | tf_op jit(solution)/shard_map/psum | solution.py:133
  817.0 7.9 convert_element_type.212
  825.0 4.9 convert_element_type.214
  829.9 5.5 convert_element_type.216
  835.4 2.6 convert_element_type.204
  (147 shorter events, 44.9 us)
Async XLA Ops:
  7.2 122.8 %copy-start = (bf16[512,2048]{1,0:T(8,128)(2,1)S(1)}, bf16[512,2048]{1,0:T(8,128)(2,1)}, u32[]{:S(2)}) copy-start(bf16[512,2048]{1,0:T(8,128)(2,1)} %param.21) | copy-start | bytes 6291460
  7.2 96.6 %all-gather.11.cloned.1.call-start = ((), (), s32[]{:S(2)}) async-start(), calls=%async_computation.10 | async-start | bytes 2621440 | tf_op jit(solution)/shard_map/all_gather | solution.py:84
  7.9 172.3 %reduce-scatter.5.cloned.1.call-start = ((), (), s32[]{:S(2)}) async-start(), calls=%async_computation.4 | async-start | bytes 2621440 | tf_op jit(solution)/shard_map/reduce_scatter | solution.py:87
  60.8 5.8 slice-start
  103.8 6.0 copy-start.21
  106.1 3.8 copy-start.19
  106.1 6.1 slice-start.3
  109.9 2.4 slice-start.4
  114.3 6.1 copy-start.3
  114.3 6.1 copy-start.9
  121.8 8.1 copy-start.31
  129.9 2.6 copy-start.29
  130.0 50.2 %copy-start.4 = (bf16[1,128,2048]{2,1,0:T(8,128)(2,1)S(1)}, bf16[1,128,2048]{2,1,0:T(8,128)(2,1)}, u32[]{:S(2)}) copy-start(bf16[1,128,2048]{2,1,0:T(8,128)(2,1)} %param.14) | copy-start | bytes 1572868
  132.6 95.6 %all-gather.7.cloned.1.call-start = ((), (), s32[]{:S(2)}) async-start(), calls=%async_computation.5 | async-start | bytes 2621440 | tf_op jit(solution)/shard_map/all_gather | solution.py:84
  183.6 90.8 %all-gather.13.cloned.1.call-start = ((), (), s32[]{:S(2)}) async-start(), calls=%async_computation.11 | async-start | bytes 2621440 | tf_op jit(solution)/shard_map/all_gather | solution.py:84
  184.1 156.7 %reduce-scatter.9.cloned.1.call-start = ((), (), s32[]{:S(2)}) async-start(), calls=%async_computation.7 | async-start | bytes 2621440 | tf_op jit(solution)/shard_map/reduce_scatter | solution.py:87
  228.2 7.6 copy-start.24
  284.8 5.8 copy-start.35
  284.8 5.8 copy-start.34
  290.6 50.2 %copy-start.5 = (bf16[128,2048]{1,0:T(8,128)(2,1)S(1)}, bf16[128,2048]{1,0:T(8,128)(2,1)}, u32[]{:S(2)}) copy-start(bf16[128,2048]{1,0:T(8,128)(2,1)} %reduce-scatter.5.cloned.1.call-done) | copy-start | bytes 1572868
  297.4 92.2 %all-gather.9.cloned.1.call-start = ((), (), s32[]{:S(2)}) async-start(), calls=%async_computation.8 | async-start | bytes 2621440 | tf_op jit(solution)/shard_map/all_gather | solution.py:84
  345.0 209.6 %reduce-scatter.11.cloned.1.call-start = ((), (), s32[]{:S(2)}) async-start(), calls=%async_computation.9 | async-start | bytes 2621440 | tf_op jit(solution)/shard_map/reduce_scatter | solution.py:87
  393.3 8.2 copy-start.32
  393.3 8.2 copy-start.33
  401.5 4.9 slice-start.1
  401.5 5.8 slice-start.2
  407.4 2.5 copy-start.18
  409.9 2.0 copy-start.2
  419.4 179.4 %reduce-scatter.7.cloned.1.call-start = ((), (), s32[]{:S(2)}) async-start(), calls=%async_computation.6 | async-start | bytes 2621440 | tf_op jit(solution)/shard_map/reduce_scatter | solution.py:87
  426.8 390.2 %all-reduce.6.cloned.1.call-start = ((), (), s32[]{:S(2)}) async-start(), calls=%async_computation.12 | async-start | bytes 48234496 | tf_op jit(solution)/shard_map/psum | solution.py:133
  426.8 7.3 copy-start.25
  426.8 7.3 copy-start.36
  434.2 4.7 copy-start.26
  434.2 4.7 copy-start.37
  457.0 11.7 %copy-start.27 = (bf16[512,2048]{1,0:T(8,128)(2,1)S(1)}, bf16[512,2048]{1,0:T(8,128)(2,1)}, u32[]{:S(2)}) copy-start(bf16[512,2048]{1,0:T(8,128)(2,1)} %all-gather.9.cloned.1.call-done) | copy-start | bytes 6291460
  457.0 11.7 %copy-start.30 = (bf16[8,64,512]{2,1,0:T(8,128)(2,1)S(1)}, bf16[8,64,512]{2,1,0:T(8,128)(2,1)}, u32[]{:S(2)}) copy-start(bf16[8,64,512]{2,1,0:T(8,128)(2,1)} %copy-done.29) | copy-start | bytes 1572868
  468.7 2.6 copy-start.20
  533.4 7.8 copy-start.28
  533.4 65.4 %copy-start.7 = (bf16[128,2048]{1,0:T(8,128)(2,1)S(1)}, bf16[128,2048]{1,0:T(8,128)(2,1)}, u32[]{:S(2)}) copy-start(bf16[128,2048]{1,0:T(8,128)(2,1)} %reduce-scatter.9.cloned.1.call-done) | copy-start | bytes 1572868
  533.4 65.4 %copy-start.8 = (bf16[1,128,2048]{2,1,0:T(8,128)(2,1)S(1)}, bf16[1,128,2048]{2,1,0:T(8,128)(2,1)}, u32[]{:S(2)}) copy-start(bf16[1,128,2048]{2,1,0:T(8,128)(2,1)} %param.27) | copy-start | bytes 1572868
  817.0 7.9 copy-start.6
  817.0 12.8 %slice-start.5 = ((s8[5242880]{0:T(1024)(128)(4,1)}), s8[4194304]{0:T(1024)(128)(4,1)S(1)}, s32[]{:S(2)}) async-start(s8[5242880]{0:T(1024)(128)(4,1)} %bitcast.133), calls=%async_computation.18 | async-start | bytes 8388608
  825.0 4.9 slice-start.6
  829.9 5.5 copy-start.14
  835.4 2.6 copy-start.13
  838.0 2.6 copy-start.12
  840.6 2.6 copy-start.11
  843.2 2.5 copy-start.1
  (6 other events, 9.1 us)
Sparse Core Ops, SparseCore 0:
  9.6 45.6 all-gather.10
  132.7 47.4 reduce-scatter.4
  183.7 44.4 all-gather.6
  229.7 44.6 all-gather.12
  297.5 43.2 reduce-scatter.8
  345.1 44.4 all-gather.8
  419.6 43.3 reduce-scatter.10
  465.9 43.1 reduce-scatter.6
  515.4 301.5 all-reduce.5

commit v2 on v1

--- a/solution.py
+++ b/solution.py
@@ -1,12 +1,391 @@
+import functools
 import jax
 import jax.numpy as jnp
 from jax import lax
+from jax.experimental import pallas as pl
+from jax.experimental.pallas import tpu as pltpu
 from jax.sharding import PartitionSpec as P
 
 epsilon = 1e-06
 negative = -1000000000.0
+head_dim = 64
+lanes = 128
+MESH = pl.DeviceIdType.MESH
+any_space = pl.BlockSpec(memory_space=pl.ANY)
+vmem_space = pl.BlockSpec(memory_space=pltpu.VMEM)
+smem_space = pl.BlockSpec(memory_space=pltpu.SMEM)
+
+
+def nn_dot(left, right):
+    return jnp.dot(left, right, preferred_element_type=jnp.float32)
+
+
+def nt_dot(left, right):
+    return lax.dot_general(
+        left, right, (((1,), (1,)), ((), ())), preferred_element_type=jnp.float32
+    )
+
+
+def line_barrier(me, count):
+    barrier = pltpu.get_barrier_semaphore()
+
+    @pl.when(me > 0)
+    def _():
+        pl.semaphore_signal(barrier, inc=1, device_id={"group": me - 1}, device_id_type=MESH)
+
+    @pl.when(me < count - 1)
+    def _():
+        pl.semaphore_signal(barrier, inc=1, device_id={"group": me + 1}, device_id_type=MESH)
+
+    peers = jnp.where(me > 0, 1, 0) + jnp.where(me < count - 1, 1, 0)
+    pl.semaphore_wait(barrier, peers)
+
+
+class LineGather:
+    def __init__(self, me, count, buffer, sems):
+        self.me, self.count, self.buffer, self.sems = me, count, buffer, sems
+
+    def copy(self, side, step):
+        shift = 1 if side == 0 else -1
+        block = self.me - step if side == 0 else self.me + step
+        return pltpu.make_async_remote_copy(
+            src_ref=self.buffer.at[block],
+            dst_ref=self.buffer.at[block],
+            send_sem=self.sems.at[side, 0, step],
+            recv_sem=self.sems.at[side, 1, step],
+            device_id={"group": self.me + shift},
+            device_id_type=MESH,
+        )
+
+    def sends(self, side, step):
+        if side == 0:
+            return (self.me - step >= 0) & (self.me + 1 < self.count)
+        return (self.me + step < self.count) & (self.me >= 1)
+
+    def arrives(self, side, step):
+        if side == 0:
+            return self.me - 1 - step >= 0
+        return self.me + 1 + step < self.count
+
+    def arrived_block(self, side, step):
+        return self.me - 1 - step if side == 0 else self.me + 1 + step
+
+    def start(self, step):
+        for side in range(2):
+            @pl.when(self.sends(side, step))
+            def _():
+                self.copy(side, step).start()
+
+    def wait_arrival(self, side, step):
+        @pl.when(self.arrives(side, step))
+        def _():
+            block = self.arrived_block(side, step)
+            pltpu.make_async_remote_copy(
+                src_ref=self.buffer.at[block],
+                dst_ref=self.buffer.at[block],
+                send_sem=self.sems.at[side, 0, step],
+                recv_sem=self.sems.at[side, 1, step],
+                device_id={"group": self.me},
+                device_id_type=MESH,
+            ).wait_recv()
+
+    def wait_sends(self):
+        for step in range(self.count - 1):
+            for side in range(2):
+                @pl.when(self.sends(side, step))
+                def _():
+                    self.copy(side, step).wait_send()
+
+
+class LineScatter:
+    def __init__(self, me, count, parts, inbox, sems):
+        self.me, self.count, self.parts, self.inbox, self.sems = me, count, parts, inbox, sems
+
+    def target(self, side, step):
+        return step if side == 0 else self.count - 1 - step
+
+    def passes(self, side, step):
+        if side == 0:
+            return step < self.me
+        return self.count - 1 - step > self.me
+
+    def receives(self, side, step):
+        if side == 0:
+            return (step <= self.me) & (self.me + 1 < self.count)
+        return (self.count - 1 - step >= self.me) & (self.me >= 1)
+
+    def copy(self, side, step):
+        shift = -1 if side == 0 else 1
+        return pltpu.make_async_remote_copy(
+            src_ref=self.parts.at[self.target(side, step)],
+            dst_ref=self.inbox.at[side, step],
+            send_sem=self.sems.at[side, 0, step],
+            recv_sem=self.sems.at[side, 1, step],
+            device_id={"group": self.me + shift},
+            device_id_type=MESH,
+        )
+
+    def forward(self, side, step):
+        @pl.when(self.passes(side, step))
+        def _():
+            @pl.when(self.receives(side, step))
+            def _():
+                self.copy(side, step).wait_recv()
+                target = self.target(side, step)
+                self.parts[target] = (
+                    self.parts[target].astype(jnp.float32)
+                    + self.inbox[side, step].astype(jnp.float32)
+                ).astype(jnp.bfloat16)
+
+            self.copy(side, step).start()
+
+    def finish(self, total_ref):
+        for side in range(2):
+            has = self.me + 1 < self.count if side == 0 else self.me >= 1
+
+            @pl.when(has)
+            def _():
+                step = self.me if side == 0 else self.count - 1 - self.me
+                self.copy(side, step).wait_recv()
+                total_ref[...] += self.inbox[side, step].astype(jnp.float32)
+
+    def wait_sends(self):
+        for step in range(self.count - 1):
+            for side in range(2):
+                @pl.when(self.passes(side, step))
+                def _():
+                    self.copy(side, step).wait_send()
+
+
+def head_masks():
+    lane = lax.broadcasted_iota(jnp.int32, (1, lanes), 1)
+    first = (lane < head_dim).astype(jnp.float32)
+    return first.astype(jnp.bfloat16), (1.0 - first).astype(jnp.bfloat16)
+
+
+def offset_bias(bias_ref, head, row_start, rows, total):
+    width = bias_ref.shape[1]
+    shift = lax.rem(row_start + (width - (total - 1)), width)
+    vector = pltpu.roll(jnp.broadcast_to(bias_ref[pl.ds(head, 1), :], (8, width)), shift, 1)
+    vector = jnp.broadcast_to(vector[0:1, :], (rows, width))
+    return pltpu.roll(vector, 0, 1, stride=1, stride_axis=0)[:, :total]
+
+
+def rms_rows(values):
+    return lax.rsqrt(jnp.mean(values * values, axis=-1, keepdims=True) + epsilon)
+
+
+def attention_forward_kernel(
+    count,
+    length_ref,
+    x_hbm, cot_hbm, gains_hbm, wq_hbm, wk_hbm, wv_hbm, wo_hbm, ids_ref, table_ref,
+    n1_out, q_out, k_out, v_out, att_out, lse_out, cot_out, middle_out, n2_out, gains_out, bias_out,
+    x_all, gains_all, wq, wk, wv, wo, parts, inbox, n1_buf, q_buf, k_buf, v_buf, att_buf, lse_buf, total_buf, n2_buf,
+    local_sems, x_sems, g_sems, c_sems, s_sems, out_sems,
+):
+    me = lax.axis_index("group")
+    rows, width = x_hbm.shape
+    total = rows * count
+    columns = wq.shape[1]
+    local_heads = columns // head_dim
+    loads = [
+        pltpu.make_async_copy(source, target, local_sems.at[index])
+        for index, (source, target) in enumerate(
+            [
+                (x_hbm, x_all.at[me]),
+                (gains_hbm, gains_all.at[me]),
+                (wq_hbm, wq),
+                (wk_hbm, wk),
+                (wv_hbm, wv),
+                (wo_hbm, wo),
+                (cot_hbm, cot_out.at[me]),
+            ]
+        )
+    ]
+    for load in loads:
+        load.start()
+    line_barrier(me, count)
+    x_line = LineGather(me, count, x_all, x_sems)
+    g_line = LineGather(me, count, gains_all, g_sems)
+    c_line = LineGather(me, count, cot_out, c_sems)
+    loads[1].wait()
+    g_line.start(0)
+    loads[0].wait()
+    x_line.start(0)
+
+    bucket = lax.broadcasted_iota(jnp.int32, (table_ref.shape[1], ids_ref.shape[1]), 0)
+    one_hot = (bucket == ids_ref[...]).astype(jnp.float32).astype(jnp.bfloat16)
+    bias_out[...] = nn_dot(table_ref[...], one_hot)
+
+    for step in range(count - 1):
+        for side in range(2):
+            g_line.wait_arrival(side, step)
+        if step + 1 < count - 1:
+            g_line.start(step + 1)
+    for owner in range(count):
+        gains_out[:, owner * (width // count) : (owner + 1) * (width // count)] = gains_all[owner]
+    for load in loads[2:5]:
+        load.wait()
+
+    def project(block):
+        values = x_all[block].astype(jnp.float32)
+        normed = (values * rms_rows(values) * gains_out[0:1, :]).astype(jnp.bfloat16)
+        n1_buf[block] = normed
+        q_buf[block] = nn_dot(normed, wq[...]).astype(jnp.bfloat16)
+        k_buf[block] = nn_dot(normed, wk[...]).astype(jnp.bfloat16)
+        v_buf[block] = nn_dot(normed, wv[...]).astype(jnp.bfloat16)
+
+    project(me)
+    for step in range(count - 1):
+        for side in range(2):
+            x_line.wait_arrival(side, step)
+        if step + 1 < count - 1:
+            x_line.start(step + 1)
+
+        @pl.loop(0, 2)
+        def _(side):
+            arrives = jnp.where(side == 0, me - 1 - step >= 0, me + 1 + step < count)
+
+            @pl.when(arrives)
+            def _():
+                project(jnp.where(side == 0, me - 1 - step, me + 1 + step))
+
+    loads[6].wait()
+    c_line.start(0)
+    loads[5].wait()
+    mask_first, mask_second = head_masks()
+    key_valid = lax.broadcasted_iota(jnp.int32, (1, total), 1) < length_ref[0]
+    lane = lax.broadcasted_iota(jnp.int32, (1, lanes), 1)
+
+    def attend(block):
+        lse_buf[block] = jnp.zeros((rows, lanes), jnp.float32)
+
+        @pl.loop(0, local_heads // 2)
+        def _(pair):
+            cols = pl.ds(pl.multiple_of(pair * lanes, lanes), lanes)
+            query = q_buf[block, :, cols]
+            key = k_buf[:, :, cols].reshape(total, lanes)
+            value = v_buf[:, :, cols].reshape(total, lanes)
+            outs = []
+            for half, mask in enumerate((mask_first, mask_second)):
+                head = pair * 2 + half
+                scores = nt_dot(query * mask, key)
+                scores = scores + offset_bias(bias_out, head, block * rows, rows, total)
+                scores = jnp.where(key_valid, scores, negative)
+                top = jnp.max(scores, axis=-1, keepdims=True)
+                expd = jnp.exp(scores - top)
+                summed = jnp.sum(expd, axis=-1, keepdims=True)
+                probs = (expd * (1.0 / summed)).astype(jnp.bfloat16)
+                outs.append(nn_dot(probs, value))
+                lse_buf[block] = jnp.where(lane == head, top + jnp.log(summed), lse_buf[block])
+            att_buf[block, :, cols] = jnp.where(lane < head_dim, outs[0], outs[1]).astype(
+                jnp.bfloat16
+            )
+
+    def attend_and_project(block):
+        attend(block)
+        parts[block] = nn_dot(att_buf[block], wo[...]).astype(jnp.bfloat16)
+
+    scatter = LineScatter(me, count, parts, inbox, s_sems)
+    for step in range(count - 1):
+        @pl.loop(0, 2)
+        def _(side):
+            passes = jnp.where(side == 0, step < me, count - 1 - step > me)
+
+            @pl.when(passes)
+            def _():
+                attend_and_project(jnp.where(side == 0, step, count - 1 - step))
+
+        for side in range(2):
+            scatter.forward(side, step)
+        if step < count - 2:
+            for side in range(2):
+                c_line.wait_arrival(side, step)
+            c_line.start(step + 1)
+    attend(me)
+    outs = [
+        pltpu.make_async_copy(source, target, out_sems.at[index])
+        for index, (source, target) in enumerate(
+            [(n1_buf, n1_out), (q_buf, q_out), (k_buf, k_out), (v_buf, v_out), (att_buf, att_out), (lse_buf, lse_out)]
+        )
+    ]
+    for copy in outs:
+        copy.start()
+    total_buf[...] = x_all[me].astype(jnp.float32) + nn_dot(att_buf[me], wo[...])
+    scatter.finish(total_buf)
+    middle = total_buf[...]
+    n2_buf[...] = (middle * rms_rows(middle) * gains_out[1:2, :]).astype(jnp.bfloat16)
+    tail = [
+        pltpu.make_async_copy(total_buf, middle_out, out_sems.at[len(outs)]),
+        pltpu.make_async_copy(n2_buf, n2_out, out_sems.at[len(outs) + 1]),
+    ]
+    for copy in tail:
+        copy.start()
+    for side in range(2):
+        c_line.wait_arrival(side, count - 2)
+    for line in (g_line, x_line, c_line, scatter):
+        line.wait_sends()
+    for copy in outs + tail:
+        copy.wait()
+
+
+def attention_forward(count, length, x, cot, gains, wq, wk, wv, wo, ids, table):
+    rows, width = x.shape
+    columns = wq.shape[1]
+    local_heads = columns // head_dim
+    bf, f32 = jnp.bfloat16, jnp.float32
+    shape = jax.ShapeDtypeStruct
+    steps = count - 1
+    dma = pltpu.SemaphoreType.DMA
+    return pl.pallas_call(
+        functools.partial(attention_forward_kernel, count),
+        name="attention_forward",
+        out_shape=(
+            shape((count, rows, width), bf),
+            shape((count, rows, columns), bf),
+            shape((count, rows, columns), bf),
+            shape((count, rows, columns), bf),
+            shape((count, rows, columns), bf),
+            shape((count, rows, lanes), f32),
+            shape((count, rows, width), bf),
+            shape((rows, width), f32),
+            shape((rows, width), bf),
+            shape((8, width), f32),
+            shape((local_heads, ids.shape[1]), f32),
+        ),
+        in_specs=[smem_space] + [any_space] * 7 + [vmem_space] * 2,
+        out_specs=[any_space] * 9 + [vmem_space] * 2,
+        scratch_shapes=[
+            pltpu.VMEM((count, rows, width), bf),
+            pltpu.VMEM((count,) + gains.shape, f32),
+            pltpu.VMEM(wq.shape, bf),
+            pltpu.VMEM(wk.shape, bf),
+            pltpu.VMEM(wv.shape, bf),
+            pltpu.VMEM(wo.shape, bf),
+            pltpu.VMEM((count, rows, width), bf),
+            pltpu.VMEM((2, steps, rows, width), bf),
+            pltpu.VMEM((count, rows, width), bf),
+            pltpu.VMEM((count, rows, columns), bf),
+            pltpu.VMEM((count, rows, columns), bf),
+            pltpu.VMEM((count, rows, columns), bf),
+            pltpu.VMEM((count, rows, columns), bf),
+            pltpu.VMEM((count, rows, lanes), f32),
+            pltpu.VMEM((rows, width), f32),
+            pltpu.VMEM((rows, width), bf),
+            dma((7,)),
+            dma((2, 2, steps)),
+            dma((2, 2, steps)),
+            dma((2, 2, steps)),
+            dma((2, 2, steps)),
+            dma((8,)),
+        ],
+        compiler_params=pltpu.CompilerParams(
+            collective_id=0, has_side_effects=True, vmem_limit_bytes=56 * 2**20
+        ),
+    )(length, x, cot, gains, wq, wk, wv, wo, ids, table)
+
+
 highest = lax.Precision.HIGHEST
-head_dim = 64
 
 
 def rms_scale(values, gain):
@@ -88,33 +467,34 @@
             values.astype(jnp.bfloat16), "group", scatter_dimension=0, tiled=True
         ).astype(jnp.float32)
 
-    x_all_low = gather(inputs[0])
-    g_all = jnp.where(valid[:, None], gather(cotangent[0]), jnp.bfloat16(0))
-    gains = lax.all_gather(jnp.stack([norm1_gain, norm2_gain]), "group", axis=1, tiled=True)
-    gains = gains.astype(jnp.float32)
+    count = lax.axis_size("group")
+    gains_local = jnp.pad(
+        jnp.stack([norm1_gain, norm2_gain]).astype(jnp.float32), ((0, 6), (0, 0))
+    )
+    ids = jnp.pad(bucket_ids, (0, 1))[None, :]
+    (
+        normed_one, query, key, value, attended, log_totals, g_all, middle, normed_two, gains, bias_rows,
+    ) = attention_forward(
+        count, seq_lengths, inputs[0], cotangent[0], gains_local,
+        w_query, w_key, w_value, w_attn_out, ids, bias_table.T,
+    )
+    normed_one, query, key, value, attended, g_all = (
+        array.reshape(total, -1) for array in (normed_one, query, key, value, attended, g_all)
+    )
+    g_all = jnp.where(valid[:, None], g_all, jnp.bfloat16(0))
     gain_first, gain_second = gains[0], gains[1]
     x_local = inputs[0].astype(jnp.float32)
-    normed_one = rms_scale(x_all_low.astype(jnp.float32), gain_first).astype(jnp.bfloat16)
-    query = plain_dot(normed_one, w_query).astype(jnp.bfloat16)
-    key = plain_dot(normed_one, w_key).astype(jnp.bfloat16)
-    value = plain_dot(normed_one, w_value).astype(jnp.bfloat16)
-
     buckets = bias_table.shape[0]
     one_hot = (bucket_ids[:, None] == jnp.arange(buckets)[None, :]).astype(jnp.float32)
-    per_offset = jnp.dot(one_hot, bias_table.astype(jnp.float32), precision=highest)
-    bias = spread_offsets(jnp.pad(per_offset.T, ((0, 0), (1, 1))), total, total)
+    bias = spread_offsets(jnp.pad(bias_rows[:, :-1], ((0, 0), (1, 1))), total, total)
     scores = jnp.einsum(
         "qhd,khd->hqk", heads(query), heads(key), preferred_element_type=jnp.float32
     )
     scores = jnp.where(valid[None, None, :], scores + bias, negative)
-    probs = jax.nn.softmax(scores, axis=-1)
+    log_rows = log_totals.reshape(total, -1)[:, : bias.shape[0]].T
+    probs = jnp.exp(scores - log_rows[:, :, None])
     probs_low = probs.astype(jnp.bfloat16)
-    attended = jnp.einsum(
-        "hqk,khd->qhd", probs_low, heads(value), preferred_element_type=jnp.float32
-    )
-    attended = attended.reshape(total, -1).astype(jnp.bfloat16)
-    middle = x_local + scatter(plain_dot(attended, w_attn_out))
-    normed_two = gather(rms_scale(middle, gain_second).astype(jnp.bfloat16))
+    normed_two = gather(normed_two)
 
     gate_pre = plain_dot(normed_two, w_gate)
     up_pre = plain_dot(normed_two, w_up)
@@ -199,6 +579,7 @@
         ffn_out_grad,
     )
 
+
 def solution(mesh):
     placed = (
         P("replica", "group", None),

time: 862 us -> 809 us (0.939)
  waiting for transfers between devices: 427 us -> 318 us
  Pallas kernels: 0 us -> 101 us
  matrix products: 118 us -> 76.2 us
    pallas_call x0 -> x1, Pallas kernels: none -> 101 us  [attention_forward(): pl.pallas_call(functools.partial(attention_forward_kernel, count), name='...]
    all_gather x4 -> x2, waiting for transfers between devices: 119 us -> 60.7 us  [gather(): return lax.all_gather(values, 'group', axis=0, tiled=True)]
    reduce_scatter x4 -> x3, waiting for transfers between devices: 90.9 us -> 40.6 us  [scatter(): lax.psum_scatter(values.astype(jnp.bfloat16), 'group', scatter_dimension=...]
    dot_general x7 -> x3, matrix products: 31.1 us -> 18.8 us  [plain_dot(): return jnp.dot(left, right, preferred_element_type=jnp.float32)]
    dot_general x7, matrix products: 31.9 us -> 21.9 us  [cols_dot(): lax.dot_general(left, right, (((1,), (1,)), ((), ())), preferred_element_...]
    dot_general x2 -> x0, matrix products: 9.13 us -> none  [the longest x1 8.12 us: local(): jnp.einsum('hqk,khd->qhd', probs_low, heads(value), preferred_element_typ...]
    unnamed x95 -> x113, local copies, waits for them, and re-layouts: 93.3 us -> 95 us
  transfers between devices with their start and end apart: 9 -> 6, of which waited for: 6 -> 3; matrix products, arithmetic and copies ran while one was open for 26% -> 26% of each run, Pallas kernels for 0% -> 0%
where the time goes in v2:
time: 809 us; the launch traced here: 799 us
  waiting for transfers between devices  318 us (39%)
  local copies, waits for them, and re-layouts  167 us (21%)
  Pallas kernels  101 us (12%)
  matrix products  76.2 us (9%)
  other arithmetic  66.3 us (8%)
  blocking collectives  54.8 us (7%)
  between operations  15.9 us (2%)
    psum x1, waiting for transfers between devices, total_sum(): return lax.psum(values.astype(jnp.bfloat16), 'replica').astype(jnp.float32)  216 us
    pallas_call x1, Pallas kernels, attention_forward(): pl.pallas_call(functools.partial(attention_forward_kernel, count), name='...  101 us
    unnamed x113, local copies, waits for them, and re-layouts  95 us
    all_gather x2, waiting for transfers between devices, gather(): return lax.all_gather(values, 'group', axis=0, tiled=True)  60.7 us
    psum x1, blocking collectives, local(): lax.psum(jnp.stack([gain_one_grad, gain_two_grad]), ('replica', 'group'))  42 us
    reduce_scatter x3, waiting for transfers between devices, scatter(): lax.psum_scatter(values.astype(jnp.bfloat16), 'group', scatter_dimension=...  40.6 us
    reshape x1, local copies, waits for them, and re-layouts, fold_offsets(): flattened.reshape(block_heads, row_count, row_count + col_count + 1)  30.5 us
    convert_element_type x7, other arithmetic, total_sum(): return lax.psum(values.astype(jnp.bfloat16), 'replica').astype(jnp.float32)  28.7 us
  transfers between devices with their start and end apart: 6, of which 3 were waited for; matrix products, arithmetic and copies ran while one was open for 26% of the time, Pallas kernels for 0%

profile of v2, /device:TPU:17, one launch (start us, length us, event | category | flops | bytes accessed | tf_op | source)
XLA Modules:
  0.0 799.4 jit_solution(4691828848359065689)
XLA Ops:
  11.1 101.3 %attention_forward.1 = (bf16[4,128,2048]{2,1,0:T(8,128)(2,1)}, bf16[4,128,512]{2,1,0:T(8,128)(2,1)}, bf16[4,128,512]{2,1,0:T(8,128)(2,1)}, bf16[4,128,512]{2,1,0...) custom-call(s32[1]{0:T(128)} %copy.60.length_ref, ...), custom_call_target="tpu_custom_call" | custom-call | tf_op jit(solution)/shard_map/attention_forward/pallas_call | solution.py:340
  114.5 60.7 %all-gather.3.cloned.1.call-done = bf16[512,2048]{1,0:T(8,128)(2,1)} async-done(((bf16[128,2048]{1,0:T(8,128)(2,1)}), bf16[512,2048]{1,0:T(8,128)(2,1)}) %all-gather.3.cloned.1.call-update) | async-done | bytes 2097168 | tf_op jit(solution)/shard_map/all_gather | solution.py:463
  175.3 6.1 fusion.37
  181.5 5.5 fusion.38
  187.0 5.7 multiply_convert_fusion.1
  192.8 2.9 fusion.39
  195.7 4.1 add_convert_fusion.1
  202.8 40.6 %reduce-scatter.6.cloned.1.call-done = bf16[128,2048]{1,0:T(8,128)(2,1)} async-done(((bf16[512,2048]{1,0:T(8,128)(2,1)}), bf16[128,2048]{1,0:T(8,128)(2,1)}) %reduce-scatter.6.cloned.1.call-update) | async-done | bytes 524304 | tf_op jit(solution)/shard_map/reduce_scatter | solution.py:466
  243.4 2.0 fusion.16
  245.3 2.3 fusion.34
  249.6 8.0 broadcast_in_dim.74
  257.6 25.4 %reshape.139 = f32[4198400]{0:T(1024)} reshape(f32[8,512,1025]{2,1,0:T(8,128)} %broadcast_in_dim.74) | data formatting | bytes 33587200
  283.0 16.5 %reshape.125 = f32[8,524800]{1,0:T(8,128)} reshape(f32[4198400]{0:T(1024)} %reshape.139) | data formatting | bytes 33587200 | tf_op jit(solution)/shard_map/reshape | solution.py:419
  299.5 5.8 slice-done
  305.2 16.0 %copy.52 = f32[1,8,512,1024]{3,2,1,0:T(8,128)S(1)} copy(f32[1,8,512,1024]{3,1,2,0:T(8,128)S(1)} %bitcast.100) | data formatting | bytes 33554432
  321.2 4.4 slice.37
  325.6 9.5 %copy.47 = f32[8,512,512]{1,2,0:T(8,128)} copy(f32[8,512,512]{2,1,0:T(8,128)} %slice.37) | data formatting | bytes 16777216
  335.3 3.7 convolution_convert_fusion.10
  341.2 3.0 multiply_reduce_fusion
  346.0 2.0 copy-done.1
  348.0 8.1 %multiply_convert_fusion = bf16[8,512,512]{1,2,0:T(8,128)(2,1)S(1)} fusion(f32[8,512,512]{1,2,0:T(8,128)} %copy-done.1, f32[8,512,512]{1,2,0:T(8,128)} %copy-done, f32[8,512]{1,0:T(8,128)S(1)} %get-tuple-element.54), kind=kLoop, calls=%fused_computation.3 | loop fusion | flops 6291456 | bytes 20987904 | tf_op jit(solution)/shard_map/convert_element_type | solution.py:533
  362.8 2.7 add_convert_fusion
  365.6 7.1 convolution_convert_fusion.7
  373.1 7.3 convolution_convert_fusion
  380.4 4.7 convolution_convert_fusion.1
  385.1 4.7 convolution_convert_fusion.2
  389.8 6.6 copy.48
  396.4 6.7 pad_bitcast_fusion
  403.1 11.7 %copy.50 = bf16[1,8,512,1024]{3,1,2,0:T(8,128)(2,1)} copy(bf16[1,8,512,1024]{3,2,1,0:T(8,128)(2,1)} %pad_bitcast_fusion) | data formatting | bytes 16777216
  414.8 2.6 convolution_convert_fusion.4
  417.5 2.6 convolution_convert_fusion.5
  420.1 2.6 convolution_convert_fusion.6
  422.8 2.7 convolution_convert_fusion.3
  425.5 10.1 %pad_convert_fusion = f32[8,524800]{1,0:T(8,128)} fusion(bf16[8,524288]{1,0:T(8,128)(2,1)} %bitcast.102), kind=kLoop, calls=%fused_computation.1 | loop fusion | flops 4198400 | bytes 25182208 | tf_op jit(solution)/shard_map/reshape | solution.py:431
  435.6 12.8 %reshape.141 = f32[4198400]{0:T(1024)} reshape(f32[8,524800]{1,0:T(8,128)} %pad_convert_fusion) | data formatting | bytes 33587200
  448.4 30.5 %reshape.137 = f32[8,512,1025]{2,1,0:T(8,128)} reshape(f32[4198400]{0:T(1024)} %reshape.141) | data formatting | bytes 33587200 | tf_op jit(solution)/shard_map/reshape | solution.py:431
  479.0 7.8 reduce_sum.83
  487.2 12.8 %psum.68 = f32[32,8]{0,1:T(8,128)} all-reduce(f32[32,8]{0,1:T(8,128)S(1)} %fusion.25), channel_id=1, replica_groups=mesh['replica'=8,'group'=4] {'replica'}, use_global_device_ids=true, to_apply=%region_16.17 | all-reduce | flops 256 | bytes 2048 | tf_op jit(solution)/shard_map/psum | solution.py:560
  501.6 42.0 %psum.63 = f32[2,2048]{1,0:T(2,128)S(1)} all-reduce(f32[2,2048]{1,0:T(2,128)S(1)} %pad_maximum_fusion), channel_id=1, replica_groups=mesh['replica'=8,'group'=4] {'replica','group'}, use_global_device_ids=true, to_apply=%region_10.11 | all-reduce | flops 4096 | bytes 32768 | tf_op jit(solution)/shard_map/psum | solution.py:564
  544.4 2.9 fusion.24
  547.3 216.1 %all-reduce.8.cloned.1.call-done = (bf16[2048,512]{1,0:T(8,128)(2,1)}, bf16[2048,512]{1,0:T(8,128)(2,1)}, bf16[2048,512]{1,0:T(8,128)(2,1)}, bf16[512,2048]{1,0:...) async-done(((bf16[2048,512]{1,0:T(8,128)(2,1)}, bf16[2048,512]{1,0:T(8,128)(2,1)}, bf16[2048,512]{1,0:T(8,128)(2,1)}, ...) | async-done | bytes 24117264 | tf_op jit(solution)/shard_map/psum | solution.py:513
  763.4 7.9 convert_element_type.172
  771.4 4.9 convert_element_type.174
  776.3 5.5 convert_element_type.176
  781.8 2.6 convert_element_type.164
  784.4 2.6 convert_element_type.166
  787.0 2.6 convert_element_type.168
  789.6 2.5 convert_element_type.170
  (159 shorter events, 24.1 us)
Async XLA Ops:
  7.2 168.1 %all-gather.3.cloned.1.call-start = ((), (), s32[]{:S(2)}) async-start(), calls=%async_computation.3 | async-start | bytes 2621440 | tf_op jit(solution)/shard_map/all_gather | solution.py:463
  112.5 130.9 %reduce-scatter.6.cloned.1.call-start = ((), (), s32[]{:S(2)}) async-start(), calls=%async_computation.5 | async-start | bytes 2621440 | tf_op jit(solution)/shard_map/reduce_scatter | solution.py:466
  114.5 72.4 %copy-start.17 = (bf16[512,2048]{1,0:T(8,128)(2,1)}, bf16[512,2048]{1,0:T(8,128)(2,1)S(1)}, u32[]{:S(2)}) copy-start(bf16[512,2048]{1,0:T(8,128)(2,1)S(1)} %bitcast_select_fusion) | copy-start | bytes 6291460
  175.3 6.1 copy-start.35
  175.3 11.7 %slice-start.9 = ((s8[5242880]{0:T(1024)(128)(4,1)}), s8[4194304]{0:T(1024)(128)(4,1)S(1)}, s32[]{:S(2)}) async-start(s8[5242880]{0:T(1024)(128)(4,1)} %bitcast.134), calls=%async_computation.18 | async-start | bytes 8388608
  181.4 5.6 slice-start.10
  181.4 11.3 %slice-start.5 = ((s8[5242880]{0:T(1024)(128)(4,1)}), s8[4194304]{0:T(1024)(128)(4,1)S(1)}, s32[]{:S(2)}) async-start(s8[5242880]{0:T(1024)(128)(4,1)} %bitcast.130), calls=%async_computation.14 | async-start | bytes 8388608
  181.4 14.2 %slice-start.7 = ((s8[5242880]{0:T(1024)(128)(4,1)}), s8[4194304]{0:T(1024)(128)(4,1)S(1)}, s32[]{:S(2)}) async-start(s8[5242880]{0:T(1024)(128)(4,1)} %bitcast.132), calls=%async_computation.16 | async-start | bytes 8388608
  187.0 5.7 slice-start.6
  187.0 8.7 %slice-start.8 = ((s8[5242880]{0:T(1024)(128)(4,1)}), s8[1048576]{0:T(1024)(128)(4,1)S(1)}, s32[]{:S(2)}) async-start(s8[5242880]{0:T(1024)(128)(4,1)} %bitcast.132), calls=%async_computation.17 | async-start | bytes 2097152
  192.7 2.9 copy-start.41
  192.7 2.9 copy-start.39
  199.8 45.5 %copy-start.10 = (bf16[1,128,2048]{2,1,0:T(8,128)(2,1)S(1)}, bf16[1,128,2048]{2,1,0:T(8,128)(2,1)}, u32[]{:S(2)}) copy-start(bf16[1,128,2048]{2,1,0:T(8,128)(2,1)} %param.27) | copy-start | bytes 1572868
  199.8 135.5 %all-gather.5.cloned.1.call-start = ((), (), s32[]{:S(2)}) async-start(), calls=%async_computation.6 | async-start | bytes 2621440 | tf_op jit(solution)/shard_map/all_gather | solution.py:463
  199.9 47.7 %copy-start.30 = (pred[128]{0:T(512)(128)(4,1)}, pred[128]{0:T(512)(128)(4,1)S(1)}, u32[]{:S(2)}) copy-start(pred[128]{0:T(512)(128)(4,1)S(1)} %add_compare_fusion) | copy-start | bytes 388
  201.2 46.7 %copy-start.20 = (bf16[4,128,512]{2,1,0:T(8,128)(2,1)S(1)}, bf16[4,128,512]{2,1,0:T(8,128)(2,1)}, u32[]{:S(2)}) copy-start(bf16[4,128,512]{2,1,0:T(8,128)(2,1)} %get-tuple-element.31) | copy-start | bytes 1572868
  201.2 47.0 %copy-start.27 = (f32[128]{0:T(128)}, f32[128]{0:T(128)S(1)}, u32[]{:S(2)}) copy-start(f32[128]{0:T(128)S(1)} %fusion.32) | copy-start | bytes 1540
  202.8 45.5 %copy-start.22 = (f32[1,2048]{1,0:T(1,128)}, f32[1,2048]{1,0:T(1,128)S(1)}, u32[]{:S(2)}) copy-start(f32[1,2048]{1,0:T(1,128)S(1)} %get-tuple-element.51) | copy-start | bytes 24580
  245.3 3.1 copy-start.32
  245.3 3.1 copy-start.19
  247.6 252.4 %reduce-scatter.8.cloned.1.call-start = ((), (), s32[]{:S(2)}) async-start(), calls=%async_computation.7 | async-start | bytes 2621440 | tf_op jit(solution)/shard_map/reduce_scatter | solution.py:466
  299.5 5.8 slice-start
  325.6 9.6 %copy-start.21 = (f32[4,128,128]{2,1,0:T(8,128)S(1)}, f32[4,128,128]{2,1,0:T(8,128)}, u32[]{:S(2)}) copy-start(f32[4,128,128]{2,1,0:T(8,128)} %get-tuple-element.30) | copy-start | bytes 786436
  335.3 5.0 slice-start.1
  341.2 3.4 copy-start
  344.6 3.4 copy-start.1
  365.6 178.7 %reduce-scatter.4.cloned.1.call-start = ((), (), s32[]{:S(2)}) async-start(), calls=%async_computation.4 | async-start | bytes 2621440 | tf_op jit(solution)/shard_map/reduce_scatter | solution.py:466
  365.6 7.2 copy-start.6
  372.8 390.6 %all-reduce.8.cloned.1.call-start = ((), (), s32[]{:S(2)}) async-start(), calls=%async_computation.8 | async-start | bytes 48234496 | tf_op jit(solution)/shard_map/psum | solution.py:513
  373.1 7.3 copy-start.36
  373.1 7.3 copy-start.40
  380.4 4.7 copy-start.42
  403.1 11.7 %copy-start.34 = (bf16[4,128,2048]{2,1,0:T(8,128)(2,1)S(1)}, bf16[4,128,2048]{2,1,0:T(8,128)(2,1)}, u32[]{:S(2)}) copy-start(bf16[4,128,2048]{2,1,0:T(8,128)(2,1)} %get-tuple-element.32) | copy-start | bytes 6291460
  420.1 2.7 copy-start.38
  478.9 7.9 copy-start.29
  478.9 21.1 %copy-start.24 = (f32[1,2048]{1,0:T(1,128)S(1)}, f32[1,2048]{1,0:T(1,128)}, u32[]{:S(2)}) copy-start(f32[1,2048]{1,0:T(1,128)} %get-tuple-element.50) | copy-start | bytes 24580
  478.9 22.7 %copy-start.25 = (f32[2048]{0:T(1024)S(1)}, f32[2048]{0:T(1024)}, u32[]{:S(2)}) copy-start(f32[2048]{0:T(1024)} %get-tuple-element.34) | copy-start | bytes 24580
  478.9 65.4 %copy-start.4 = (f32[128,2048]{1,0:T(8,128)S(1)}, f32[128,2048]{1,0:T(8,128)}, u32[]{:S(2)}) copy-start(f32[128,2048]{1,0:T(8,128)} %get-tuple-element.23) | copy-start | bytes 3145732
  478.9 65.4 %copy-start.11 = (bf16[1,128,2048]{2,1,0:T(8,128)(2,1)S(1)}, bf16[1,128,2048]{2,1,0:T(8,128)(2,1)}, u32[]{:S(2)}) copy-start(bf16[1,128,2048]{2,1,0:T(8,128)(2,1)} %param.27) | copy-start | bytes 1572868
  478.9 65.4 %copy-start.12 = (bf16[128,2048]{1,0:T(8,128)(2,1)S(1)}, bf16[128,2048]{1,0:T(8,128)(2,1)}, u32[]{:S(2)}) copy-start(bf16[128,2048]{1,0:T(8,128)(2,1)} %reduce-scatter.6.cloned.1.call-done) | copy-start | bytes 1572868
  478.9 65.4 %copy-start.23 = (f32[1,2048]{1,0:T(1,128)S(1)}, f32[1,2048]{1,0:T(1,128)}, u32[]{:S(2)}) copy-start(f32[1,2048]{1,0:T(1,128)} %copy-done.22) | copy-start | bytes 24580
  478.9 65.4 %copy-start.28 = (f32[128]{0:T(128)S(1)}, f32[128]{0:T(128)}, u32[]{:S(2)}) copy-start(f32[128]{0:T(128)} %copy-done.27) | copy-start | bytes 1540
  478.9 65.4 %copy-start.31 = (pred[128]{0:T(512)(128)(4,1)S(1)}, pred[128]{0:T(512)(128)(4,1)}, u32[]{:S(2)}) copy-start(pred[128]{0:T(512)(128)(4,1)} %copy-done.30) | copy-start | bytes 388
  479.0 65.4 %copy-start.33 = (f32[128]{0:T(128)S(1)}, f32[128]{0:T(128)}, u32[]{:S(2)}) copy-start(f32[128]{0:T(128)} %copy-done.32) | copy-start | bytes 1540
  763.4 7.9 copy-start.9
  763.4 12.8 %slice-start.3 = ((s8[5242880]{0:T(1024)(128)(4,1)}), s8[4194304]{0:T(1024)(128)(4,1)S(1)}, s32[]{:S(2)}) async-start(s8[5242880]{0:T(1024)(128)(4,1)} %bitcast.106), calls=%async_computation.12 | async-start | bytes 8388608
  771.4 4.9 slice-start.4
  776.3 5.5 copy-start.16
  (12 other events, 23.4 us)
Sparse Core Ops, SparseCore 0:
  112.6 62.6 all-gather.2
  200.0 43.3 reduce-scatter.5
  247.8 44.4 all-gather.4
  365.7 43.1 reduce-scatter.7
  411.6 43.1 reduce-scatter.3
  461.8 301.5 all-reduce.7

commit v3 on v2

--- a/solution.py
+++ b/solution.py
@@ -385,6 +385,174 @@
     )(length, x, cot, gains, wq, wk, wv, wo, ids, table)
 
 
+def gelu_parts(gate):
+    root = 0.7978845608028654
+    inner = root * (gate + 0.044715 * gate * gate * gate)
+    tanh = jnp.tanh(inner)
+    half = 0.5 * (1.0 + tanh)
+    slope = half + 0.5 * gate * (1.0 - tanh * tanh) * root * (1.0 + 3 * 0.044715 * gate * gate)
+    return gate * half, slope
+
+
+def feed_forward_kernel(
+    count, tile,
+    length_ref,
+    n2_hbm, cot_hbm, wg_hbm, wu_hbm, wf_hbm,
+    gate_out, up_out, ffn_out, back_out, res_out,
+    n2_all, g_all, wg, wu, wf, hid, grad_gate, grad_up, back_buf, res_buf, turned, stage,
+    local_sems, n_sems, out_sems, stage_sems,
+):
+    me = lax.axis_index("group")
+    rows, width = n2_hbm.shape
+    total = rows * count
+    units = wg.shape[1]
+    loads = [
+        pltpu.make_async_copy(source, target, local_sems.at[index])
+        for index, (source, target) in enumerate(
+            [(n2_hbm, n2_all.at[me]), (wg_hbm, wg), (wu_hbm, wu), (wf_hbm, wf), (cot_hbm, g_all)]
+        )
+    ]
+    for load in loads:
+        load.start()
+    line_barrier(me, count)
+    line = LineGather(me, count, n2_all, n_sems)
+    loads[0].wait()
+    line.start(0)
+    for load in loads[1:]:
+        load.wait()
+
+    def mask_rows(block):
+        position = block * rows + lax.broadcasted_iota(jnp.int32, (rows, 1), 0)
+        valid = (position < length_ref[0]).astype(jnp.float32).astype(jnp.bfloat16)
+        g_all[block] = g_all[block] * valid
+
+    def block_pass(block):
+        mask_rows(block)
+        normed = n2_all[block]
+        grads = g_all[block]
+
+        @pl.loop(0, units // tile)
+        def _(index):
+            cols = pl.ds(pl.multiple_of(index * tile, tile), tile)
+            gate = nn_dot(normed, wg[:, cols])
+            up = nn_dot(normed, wu[:, cols])
+            grad_hidden = nt_dot(grads, wf[cols, :])
+            act, slope = gelu_parts(gate)
+            hid[block, :, cols] = (act * up).astype(jnp.bfloat16)
+            grad_gate[block, :, cols] = (grad_hidden * up * slope).astype(jnp.bfloat16)
+            grad_up[block, :, cols] = (grad_hidden * act).astype(jnp.bfloat16)
+
+        chunk = 2 * tile
+
+        @pl.loop(0, width // chunk)
+        def _(index):
+            cols = pl.ds(pl.multiple_of(index * chunk, chunk), chunk)
+            back_buf[block, :, cols] = (
+                nt_dot(grad_gate[block], wg[cols, :]) + nt_dot(grad_up[block], wu[cols, :])
+            ).astype(jnp.bfloat16)
+            res_buf[block, :, cols] = nn_dot(hid[block], wf[:, cols]).astype(jnp.bfloat16)
+
+    block_pass(me)
+    for step in range(count - 1):
+        for side in range(2):
+            line.wait_arrival(side, step)
+        if step + 1 < count - 1:
+            line.start(step + 1)
+
+        @pl.loop(0, 2)
+        def _(side):
+            arrives = jnp.where(side == 0, me - 1 - step >= 0, me + 1 + step < count)
+
+            @pl.when(arrives)
+            def _():
+                block_pass(jnp.where(side == 0, me - 1 - step, me + 1 + step))
+
+    outs = [
+        pltpu.make_async_copy(back_buf, back_out, out_sems.at[0]),
+        pltpu.make_async_copy(res_buf, res_out, out_sems.at[1]),
+    ]
+    for copy in outs:
+        copy.start()
+
+    def weight_grad(left, right, target, first):
+        height = target.shape[0]
+        depth = right.shape[2]
+        factor = right[...].reshape(total, depth)
+
+        @pl.loop(0, height // tile)
+        def _(index):
+            slot = lax.rem(index, 2)
+            here = pl.ds(pl.multiple_of(index * tile, tile), tile)
+            turned[...] = left[:, :, here].reshape(total, tile).T
+
+            @pl.when(index >= 2)
+            def _():
+                pltpu.make_async_copy(
+                    stage.at[slot, :, pl.ds(0, depth)], target.at[here], stage_sems.at[slot]
+                ).wait()
+
+            stage[slot, :, pl.ds(0, depth)] = nn_dot(turned[...], factor).astype(jnp.bfloat16)
+            pltpu.make_async_copy(
+                stage.at[slot, :, pl.ds(0, depth)], target.at[here], stage_sems.at[slot]
+            ).start()
+
+        for slot in range(2):
+            pltpu.make_async_copy(
+                stage.at[slot, :, pl.ds(0, depth)], target.at[pl.ds(0, tile)], stage_sems.at[slot]
+            ).wait()
+
+    weight_grad(hid, g_all, ffn_out, 0)
+    weight_grad(n2_all, grad_gate, gate_out, 0)
+    weight_grad(n2_all, grad_up, up_out, 0)
+    line.wait_sends()
+    for copy in outs:
+        copy.wait()
+
+
+def feed_forward(count, length, n2, cot, wg, wu, wf):
+    rows, width = n2.shape
+    units = wg.shape[1]
+    tile = 128 if units % 256 else 256
+    bf = jnp.bfloat16
+    shape = jax.ShapeDtypeStruct
+    steps = count - 1
+    dma = pltpu.SemaphoreType.DMA
+    return pl.pallas_call(
+        functools.partial(feed_forward_kernel, count, tile),
+        name="feed_forward",
+        out_shape=(
+            shape(wg.shape, bf),
+            shape(wu.shape, bf),
+            shape(wf.shape, bf),
+            shape((count, rows, width), bf),
+            shape((count, rows, width), bf),
+        ),
+        in_specs=[smem_space] + [any_space] * 5,
+        out_specs=[any_space] * 5,
+        scratch_shapes=[
+            pltpu.VMEM((count, rows, width), bf),
+            pltpu.VMEM((count, rows, width), bf),
+            pltpu.VMEM(wg.shape, bf),
+            pltpu.VMEM(wu.shape, bf),
+            pltpu.VMEM(wf.shape, bf),
+            pltpu.VMEM((count, rows, units), bf),
+            pltpu.VMEM((count, rows, units), bf),
+            pltpu.VMEM((count, rows, units), bf),
+            pltpu.VMEM((count, rows, width), bf),
+            pltpu.VMEM((count, rows, width), bf),
+            pltpu.VMEM((tile, count * rows), bf),
+            pltpu.VMEM((2, tile, max(width, units)), bf),
+            dma((5,)),
+            dma((2, 2, steps)),
+            dma((2,)),
+            dma((2,)),
+        ],
+        compiler_params=pltpu.CompilerParams(
+            collective_id=1, has_side_effects=True, vmem_limit_bytes=56 * 2**20
+        ),
+    )(length, n2, cot, wg, wu, wf)
+
+
 highest = lax.Precision.HIGHEST
 
 
@@ -478,10 +646,19 @@
         count, seq_lengths, inputs[0], cotangent[0], gains_local,
         w_query, w_key, w_value, w_attn_out, ids, bias_table.T,
     )
-    normed_one, query, key, value, attended, g_all = (
-        array.reshape(total, -1) for array in (normed_one, query, key, value, attended, g_all)
-    )
-    g_all = jnp.where(valid[:, None], g_all, jnp.bfloat16(0))
+    gate_part, up_part, ffn_part, back_part, result_part = feed_forward(
+        count, seq_lengths, normed_two, g_all, w_gate, w_up, w_ffn_out
+    )
+
+    def total_sum(values):
+        return lax.psum(values.astype(jnp.bfloat16), "replica").astype(jnp.float32)
+
+    ffn_out_grad, gate_grad, up_grad = total_sum(ffn_part), total_sum(gate_part), total_sum(up_part)
+    grad_normed_two = scatter(back_part.reshape(total, -1))
+    result = (middle + scatter(result_part.reshape(total, -1))).astype(jnp.bfloat16)
+    normed_one, query, key, value, attended = (
+        array.reshape(total, -1) for array in (normed_one, query, key, value, attended)
+    )
     gain_first, gain_second = gains[0], gains[1]
     x_local = inputs[0].astype(jnp.float32)
     buckets = bias_table.shape[0]
@@ -494,28 +671,6 @@
     log_rows = log_totals.reshape(total, -1)[:, : bias.shape[0]].T
     probs = jnp.exp(scores - log_rows[:, :, None])
     probs_low = probs.astype(jnp.bfloat16)
-    normed_two = gather(normed_two)
-
-    gate_pre = plain_dot(normed_two, w_gate)
-    up_pre = plain_dot(normed_two, w_up)
-    hidden_low = gated_gelu(gate_pre, up_pre).astype(jnp.bfloat16)
-    grad_hidden = cols_dot(g_all, w_ffn_out)
-    _, pull_gelu = jax.vjp(gated_gelu, gate_pre, up_pre)
-    grad_gate, grad_up = pull_gelu(grad_hidden)
-    grad_gate = grad_gate.astype(jnp.bfloat16)
-    grad_up = grad_up.astype(jnp.bfloat16)
-    grad_normed_two = scatter(cols_dot(grad_gate, w_gate) + cols_dot(grad_up, w_up))
-    ffn_out_grad = rows_dot(hidden_low, g_all)
-    gate_grad = rows_dot(normed_two, grad_gate)
-    up_grad = rows_dot(normed_two, grad_up)
-
-    def total_sum(values):
-        return lax.psum(values.astype(jnp.bfloat16), "replica").astype(jnp.float32)
-
-    ffn_out_grad, gate_grad, up_grad = (
-        total_sum(ffn_out_grad), total_sum(gate_grad), total_sum(up_grad)
-    )
-    result = (middle + scatter(plain_dot(hidden_low, w_ffn_out))).astype(jnp.bfloat16)
 
     row_valid = start + jnp.arange(rows) < length
     g_local = jnp.where(row_valid[:, None], cotangent[0], jnp.bfloat16(0)).astype(jnp.float32)

time: 809 us -> 809 us (level)
  Pallas kernels: 101 us -> 162 us
  matrix products: 76.2 us -> 31.7 us
  waiting for transfers between devices: 318 us -> 309 us
    all_gather x2 -> x1, waiting for transfers between devices: 60.7 us -> 0.02 us  [gather(): return lax.all_gather(values, 'group', axis=0, tiled=True)]
    pallas_call x0 -> x1, Pallas kernels: none -> 60.3 us  [feed_forward(): pl.pallas_call(functools.partial(feed_forward_kernel, count, tile), name=...]
    reduce_scatter x3, waiting for transfers between devices: 40.6 us -> 68.9 us  [scatter(): lax.psum_scatter(values.astype(jnp.bfloat16), 'group', scatter_dimension=...]
    psum x1, waiting for transfers between devices: 216 us -> 240 us  [total_sum(): return lax.psum(values.astype(jnp.bfloat16), 'replica').astype(jnp.float32)]
    dot_general x3 -> x0, matrix products: 18.8 us -> none  [plain_dot(): return jnp.dot(left, right, preferred_element_type=jnp.float32)]
    dot_general x7 -> x4, matrix products: 27.3 us -> 10.5 us  [rows_dot(): lax.dot_general(left, right, (((0,), (0,)), ((), ())), preferred_element_...]
    dot_general x7 -> x4, matrix products: 21.9 us -> 9.48 us  [cols_dot(): lax.dot_general(left, right, (((1,), (1,)), ((), ())), preferred_element_...]
    unnamed x113 -> x77, local copies, waits for them, and re-layouts: 95 us -> 92 us
  transfers between devices with their start and end apart: 6 -> 5, of which waited for: 3 -> 2; matrix products, arithmetic and copies ran while one was open for 26% -> 23% of each run, Pallas kernels for 0% -> 0%
where the time goes in v3:
time: 809 us; the launch traced here: 799 us
  waiting for transfers between devices  309 us (38%)
  local copies, waits for them, and re-layouts  164 us (20%)
  Pallas kernels  162 us (20%)
  other arithmetic  62.9 us (8%)
  blocking collectives  54.3 us (7%)
  matrix products  31.7 us (4%)
  between operations  15.1 us (2%)
    psum x1, waiting for transfers between devices, total_sum(): return lax.psum(values.astype(jnp.bfloat16), 'replica').astype(jnp.float32)  240 us
    pallas_call x1, Pallas kernels, attention_forward(): pl.pallas_call(functools.partial(attention_forward_kernel, count), name='...  101 us
    unnamed x77, local copies, waits for them, and re-layouts  92 us
    reduce_scatter x3, waiting for transfers between devices, scatter(): lax.psum_scatter(values.astype(jnp.bfloat16), 'group', scatter_dimension=...  68.9 us
    pallas_call x1, Pallas kernels, feed_forward(): pl.pallas_call(functools.partial(feed_forward_kernel, count, tile), name=...  60.3 us
    psum x1, blocking collectives, local(): lax.psum(jnp.stack([gain_one_grad, gain_two_grad]), ('replica', 'group'))  41.4 us
    reshape x1, local copies, waits for them, and re-layouts, fold_offsets(): flattened.reshape(block_heads, row_count, row_count + col_count + 1)  30.5 us
    convert_element_type x7, other arithmetic, total_sum(): return lax.psum(values.astype(jnp.bfloat16), 'replica').astype(jnp.float32)  28.1 us
  transfers between devices with their start and end apart: 5, of which 2 were waited for; matrix products, arithmetic and copies ran while one was open for 23% of the time, Pallas kernels for 0%

profile of v3, /device:TPU:17, one launch (start us, length us, event | category | flops | bytes accessed | tf_op | source)
XLA Modules:
  0.0 799.2 jit_solution(1850309220051089774)
XLA Ops:
  9.2 1.3 pad.26
  11.1 101.4 %attention_forward.1 = (bf16[4,128,2048]{2,1,0:T(8,128)(2,1)}, bf16[4,128,512]{2,1,0:T(8,128)(2,1)}, bf16[4,128,512]{2,1,0:T(8,128)(2,1)}, bf16[4,128,512]{2,1,0...) custom-call(s32[1]{0:T(128)} %copy.60.length_ref, ...), custom_call_target="tpu_custom_call" | custom-call | tf_op jit(solution)/shard_map/attention_forward/pallas_call | solution.py:340
  112.5 60.3 %feed_forward.1 = (bf16[2048,1280]{1,0:T(8,128)(2,1)}, bf16[2048,1280]{1,0:T(8,128)(2,1)}, bf16[1280,2048]{1,0:T(8,128)(2,1)}, bf16[4,128,2048]{2,1,0:T(8,128)(2,1)}, bf16[4,128,2048]{2,1,0:T(8,128)(2,1)}) custom-call(s32[1]{0:T(128)} %copy.60.length_ref, bf16[128,2048]{1,0:T(8,128)(2,1)} %get-tuple-element.29.n2_hbm, ...), custom_call_target="tpu_custom_call" | custom-call | tf_op jit(solution)/shard_map/feed_forward/pallas_call | solution.py:520
  173.1 1.0 fusion.28
  174.1 68.9 %reduce-scatter.6.cloned.1.call-done = bf16[128,2048]{1,0:T(8,128)(2,1)} async-done(((bf16[512,2048]{1,0:T(8,128)(2,1)}), bf16[128,2048]{1,0:T(8,128)(2,1)}) %reduce-scatter.6.cloned.1.call-update) | async-done | bytes 524304 | tf_op jit(solution)/shard_map/reduce_scatter | solution.py:634
  243.1 1.4 fusion.9
  244.5 2.3 fusion.27
  248.5 1.0 reshape_reshape.13
  249.6 8.0 broadcast_in_dim.59
  257.6 25.2 %reshape.139 = f32[4198400]{0:T(1024)} reshape(f32[8,512,1025]{2,1,0:T(8,128)} %broadcast_in_dim.59) | data formatting | bytes 33587200
  282.8 16.4 %reshape.125 = f32[8,524800]{1,0:T(8,128)} reshape(f32[4198400]{0:T(1024)} %reshape.139) | data formatting | bytes 33587200 | tf_op jit(solution)/shard_map/reshape | solution.py:587
  299.2 5.8 slice-done
  305.0 16.0 %copy.52 = f32[1,8,512,1024]{3,2,1,0:T(8,128)S(1)} copy(f32[1,8,512,1024]{3,1,2,0:T(8,128)S(1)} %bitcast.82) | data formatting | bytes 33554432
  321.0 4.4 slice.37
  325.4 9.3 %copy.47 = f32[8,512,512]{1,2,0:T(8,128)} copy(f32[8,512,512]{2,1,0:T(8,128)} %slice.37) | data formatting | bytes 16777216
  334.8 3.7 convolution_convert_fusion.6
  339.2 2.5 fusion.30
  341.8 3.0 multiply_reduce_fusion
  345.2 3.6 fusion.2
  348.7 8.1 %multiply_convert_fusion = bf16[8,512,512]{1,2,0:T(8,128)(2,1)S(1)} fusion(f32[8,512,512]{1,2,0:T(8,128)} %copy-done.1, f32[8,512,512]{1,2,0:T(8,128)} %copy-done, f32[8,512]{1,0:T(8,128)S(1)} %get-tuple-element.61), kind=kLoop, calls=%fused_computation.3 | loop fusion | flops 6291456 | bytes 20987904 | tf_op jit(solution)/shard_map/convert_element_type | solution.py:688
  356.8 1.4 convolution_convert_fusion.4
  360.0 1.3 fusion.32
  361.6 1.8 fusion.31
  363.4 2.7 add_convert_fusion
  367.4 6.4 copy.48
  373.8 6.7 pad_bitcast_fusion
  380.5 11.7 %copy.50 = bf16[1,8,512,1024]{3,1,2,0:T(8,128)(2,1)} copy(bf16[1,8,512,1024]{3,2,1,0:T(8,128)(2,1)} %pad_bitcast_fusion) | data formatting | bytes 16777216
  392.2 2.6 convolution_convert_fusion.3
  394.8 2.6 convolution_convert_fusion.2
  397.5 2.6 convolution_convert_fusion.1
  400.1 2.6 convolution_convert_fusion
  402.8 10.1 %pad_convert_fusion = f32[8,524800]{1,0:T(8,128)} fusion(bf16[8,524288]{1,0:T(8,128)(2,1)} %bitcast.84), kind=kLoop, calls=%fused_computation.1 | loop fusion | flops 4198400 | bytes 25182208 | tf_op jit(solution)/shard_map/reshape | solution.py:599
  412.9 12.8 %reshape.141 = f32[4198400]{0:T(1024)} reshape(f32[8,524800]{1,0:T(8,128)} %pad_convert_fusion) | data formatting | bytes 33587200
  425.7 30.5 %reshape.137 = f32[8,512,1025]{2,1,0:T(8,128)} reshape(f32[4198400]{0:T(1024)} %reshape.141) | data formatting | bytes 33587200 | tf_op jit(solution)/shard_map/reshape | solution.py:599
  456.2 7.4 reduce_sum.83
  464.0 12.9 %psum.68 = f32[32,8]{0,1:T(8,128)} all-reduce(f32[32,8]{0,1:T(8,128)S(1)} %fusion.18), channel_id=1, replica_groups=mesh['replica'=8,'group'=4] {'replica'}, use_global_device_ids=true, to_apply=%region_16.17 | all-reduce | flops 256 | bytes 2048 | tf_op jit(solution)/shard_map/psum | solution.py:715
  476.9 1.6 fusion.10
  478.6 41.4 %psum.63 = f32[2,2048]{1,0:T(2,128)S(1)} all-reduce(f32[2,2048]{1,0:T(2,128)S(1)} %pad_maximum_fusion), channel_id=1, replica_groups=mesh['replica'=8,'group'=4] {'replica','group'}, use_global_device_ids=true, to_apply=%region_10.11 | all-reduce | flops 4096 | bytes 32768 | tf_op jit(solution)/shard_map/psum | solution.py:719
  520.7 3.1 fusion.17
  523.7 239.6 %all-reduce.8.cloned.1.call-done = (bf16[2048,512]{1,0:T(8,128)(2,1)}, bf16[2048,512]{1,0:T(8,128)(2,1)}, bf16[2048,512]{1,0:T(8,128)(2,1)}, bf16[512,2048]{1,0:...) async-done(((bf16[2048,512]{1,0:T(8,128)(2,1)}, bf16[2048,512]{1,0:T(8,128)(2,1)}, bf16[2048,512]{1,0:T(8,128)(2,1)}, ...) | async-done | bytes 24117264 | tf_op jit(solution)/shard_map/psum | solution.py:654
  763.4 4.3 convert_element_type.135
  767.8 2.7 convert_element_type.137
  770.5 2.7 convert_element_type.139
  773.2 1.0 copy-done.13
  774.2 2.7 convert_element_type.141
  776.9 5.2 convert_element_type.142
  782.1 4.9 convert_element_type.143
  787.0 5.5 convert_element_type.144
  (110 shorter events, 9.6 us)
Async XLA Ops:
  7.2 235.9 %reduce-scatter.6.cloned.1.call-start = ((), (), s32[]{:S(2)}) async-start(), calls=%async_computation.4 | async-start | bytes 2621440 | tf_op jit(solution)/shard_map/reduce_scatter | solution.py:634
  112.5 60.4 %copy-start.3 = (f32[128,2048]{1,0:T(8,128)S(1)}, f32[128,2048]{1,0:T(8,128)}, u32[]{:S(2)}) copy-start(f32[128,2048]{1,0:T(8,128)} %get-tuple-element.28) | copy-start | bytes 3145732
  172.8 71.7 %copy-start.8 = (bf16[1,128,2048]{2,1,0:T(8,128)(2,1)S(1)}, bf16[1,128,2048]{2,1,0:T(8,128)(2,1)}, u32[]{:S(2)}) copy-start(bf16[1,128,2048]{2,1,0:T(8,128)(2,1)} %param.27) | copy-start | bytes 1572868
  172.8 74.2 %copy-start.21 = (f32[4,128,128]{2,1,0:T(8,128)S(1)}, f32[4,128,128]{2,1,0:T(8,128)}, u32[]{:S(2)}) copy-start(f32[4,128,128]{2,1,0:T(8,128)} %get-tuple-element.37) | copy-start | bytes 786436
  172.8 74.3 %copy-start.20 = (bf16[4,128,512]{2,1,0:T(8,128)(2,1)S(1)}, bf16[4,128,512]{2,1,0:T(8,128)(2,1)}, u32[]{:S(2)}) copy-start(bf16[4,128,512]{2,1,0:T(8,128)(2,1)} %get-tuple-element.34) | copy-start | bytes 1572868
  172.8 161.9 %all-gather.2.cloned.1.call-start = ((), (), s32[]{:S(2)}) async-start(), calls=%async_computation.5 | async-start | bytes 2621440 | tf_op jit(solution)/shard_map/all_gather | solution.py:631
  172.9 74.7 %copy-start.19 = (bf16[4,128,512]{2,1,0:T(8,128)(2,1)S(1)}, bf16[4,128,512]{2,1,0:T(8,128)(2,1)}, u32[]{:S(2)}) copy-start(bf16[4,128,512]{2,1,0:T(8,128)(2,1)} %get-tuple-element.35) | copy-start | bytes 1572868
  244.4 3.7 copy-start.18
  246.7 2.8 copy-start.22
  246.7 230.2 %reduce-scatter.8.cloned.1.call-start = ((), (), s32[]{:S(2)}) async-start(), calls=%async_computation.6 | async-start | bytes 2621440 | tf_op jit(solution)/shard_map/reduce_scatter | solution.py:634
  299.2 5.8 slice-start
  334.8 7.0 slice-start.1
  338.4 0.8 copy-start.17
  339.2 2.5 slice-start.2
  341.8 3.4 copy-start
  345.2 3.6 copy-start.1
  356.8 2.2 copy-start.2
  356.8 3.2 copy-start.6
  358.2 3.1 copy-start.11
  360.0 1.6 copy-start.7
  361.6 1.8 copy-start.4
  361.6 1.8 copy-start.16
  366.1 1.0 copy-start.5
  366.1 154.5 %reduce-scatter.4.cloned.1.call-start = ((), (), s32[]{:S(2)}) async-start(), calls=%async_computation.3 | async-start | bytes 2621440 | tf_op jit(solution)/shard_map/reduce_scatter | solution.py:634
  366.7 396.7 %all-reduce.8.cloned.1.call-start = ((), (), s32[]{:S(2)}) async-start(), calls=%async_computation.7 | async-start | bytes 48234496 | tf_op jit(solution)/shard_map/psum | solution.py:654
  380.5 11.7 %copy-start.24 = (bf16[4,128,2048]{2,1,0:T(8,128)(2,1)S(1)}, bf16[4,128,2048]{2,1,0:T(8,128)(2,1)}, u32[]{:S(2)}) copy-start(bf16[4,128,2048]{2,1,0:T(8,128)(2,1)} %get-tuple-element.39) | copy-start | bytes 6291460
  392.2 2.7 copy-start.12
  397.5 2.7 copy-start.25
  397.5 2.7 copy-start.26
  456.2 7.4 copy-start.23
  456.2 64.4 %copy-start.9 = (bf16[1,128,2048]{2,1,0:T(8,128)(2,1)S(1)}, bf16[1,128,2048]{2,1,0:T(8,128)(2,1)}, u32[]{:S(2)}) copy-start(bf16[1,128,2048]{2,1,0:T(8,128)(2,1)} %param.27) | copy-start | bytes 1572868
  456.2 64.4 %copy-start.10 = (bf16[128,2048]{1,0:T(8,128)(2,1)S(1)}, bf16[128,2048]{1,0:T(8,128)(2,1)}, u32[]{:S(2)}) copy-start(bf16[128,2048]{1,0:T(8,128)(2,1)} %reduce-scatter.6.cloned.1.call-done) | copy-start | bytes 1572868
  763.4 4.4 copy-start.15
  767.7 2.7 copy-start.14
  767.8 9.1 %slice-start.7 = ((s8[5242880]{0:T(1024)(128)(4,1)}), s8[4194304]{0:T(1024)(128)(4,1)S(1)}, s32[]{:S(2)}) async-start(s8[5242880]{0:T(1024)(128)(4,1)} %bitcast.92), calls=%async_computation.15 | async-start | bytes 8388608
  770.5 3.7 copy-start.13
  770.5 6.4 slice-start.8
  774.2 7.9 slice-start.5
  776.9 5.2 slice-start.6
  776.9 10.1 %slice-start.3 = ((s8[5242880]{0:T(1024)(128)(4,1)}), s8[4194304]{0:T(1024)(128)(4,1)S(1)}, s32[]{:S(2)}) async-start(s8[5242880]{0:T(1024)(128)(4,1)} %bitcast.88), calls=%async_computation.11 | async-start | bytes 8388608
  782.1 4.9 slice-start.4
Sparse Core Ops, SparseCore 0:
  173.0 70.0 reduce-scatter.5
  246.9 44.4 all-gather.1
  366.3 43.1 reduce-scatter.7
  411.6 43.1 reduce-scatter.3
  461.9 301.4 all-reduce.7

commit v4 on v3

--- a/solution.py
+++ b/solution.py
@@ -135,7 +135,7 @@
                 self.parts[target] = (
                     self.parts[target].astype(jnp.float32)
                     + self.inbox[side, step].astype(jnp.float32)
-                ).astype(jnp.bfloat16)
+                ).astype(self.parts.dtype)
 
             self.copy(side, step).start()
 
@@ -398,7 +398,7 @@
     count, tile,
     length_ref,
     n2_hbm, cot_hbm, wg_hbm, wu_hbm, wf_hbm,
-    gate_out, up_out, ffn_out, back_out, res_out,
+    flat_out, back_out, res_out,
     n2_all, g_all, wg, wu, wf, hid, grad_gate, grad_up, back_buf, res_buf, turned, stage,
     local_sems, n_sems, out_sems, stage_sems,
 ):
@@ -474,36 +474,41 @@
     for copy in outs:
         copy.start()
 
-    def weight_grad(left, right, target, first):
-        height = target.shape[0]
+    def weight_grad(left, right, base, height):
         depth = right.shape[2]
+        panels = depth // lanes
         factor = right[...].reshape(total, depth)
+
+        def store(slot, panel, row):
+            return pltpu.make_async_copy(
+                stage.at[slot, panel],
+                flat_out.at[pl.ds(base + panel * height + row, tile)],
+                stage_sems.at[slot, panel],
+            )
 
         @pl.loop(0, height // tile)
         def _(index):
             slot = lax.rem(index, 2)
-            here = pl.ds(pl.multiple_of(index * tile, tile), tile)
-            turned[...] = left[:, :, here].reshape(total, tile).T
+            row = pl.multiple_of(index * tile, tile)
+            turned[...] = left[:, :, pl.ds(row, tile)].reshape(total, tile).T
+            product = nn_dot(turned[...], factor).astype(jnp.bfloat16)
 
             @pl.when(index >= 2)
             def _():
-                pltpu.make_async_copy(
-                    stage.at[slot, :, pl.ds(0, depth)], target.at[here], stage_sems.at[slot]
-                ).wait()
-
-            stage[slot, :, pl.ds(0, depth)] = nn_dot(turned[...], factor).astype(jnp.bfloat16)
-            pltpu.make_async_copy(
-                stage.at[slot, :, pl.ds(0, depth)], target.at[here], stage_sems.at[slot]
-            ).start()
+                for panel in range(panels):
+                    store(slot, panel, row).wait()
+
+            for panel in range(panels):
+                stage[slot, panel] = product[:, panel * lanes : (panel + 1) * lanes]
+                store(slot, panel, row).start()
 
         for slot in range(2):
-            pltpu.make_async_copy(
-                stage.at[slot, :, pl.ds(0, depth)], target.at[pl.ds(0, tile)], stage_sems.at[slot]
-            ).wait()
-
-    weight_grad(hid, g_all, ffn_out, 0)
-    weight_grad(n2_all, grad_gate, gate_out, 0)
-    weight_grad(n2_all, grad_up, up_out, 0)
+            for panel in range(panels):
+                store(slot, panel, 0).wait()
+
+    weight_grad(hid, g_all, 0, units)
+    weight_grad(n2_all, grad_gate, units * width // lanes, width)
+    weight_grad(n2_all, grad_up, 2 * units * width // lanes, width)
     line.wait_sends()
     for copy in outs:
         copy.wait()
@@ -521,14 +526,12 @@
         functools.partial(feed_forward_kernel, count, tile),
         name="feed_forward",
         out_shape=(
-            shape(wg.shape, bf),
-            shape(wu.shape, bf),
-            shape(wf.shape, bf),
+            shape((3 * units * width // lanes, lanes), bf),
             shape((count, rows, width), bf),
             shape((count, rows, width), bf),
         ),
         in_specs=[smem_space] + [any_space] * 5,
-        out_specs=[any_space] * 5,
+        out_specs=[any_space] * 3,
         scratch_shapes=[
             pltpu.VMEM((count, rows, width), bf),
             pltpu.VMEM((count, rows, width), bf),
@@ -541,11 +544,11 @@
             pltpu.VMEM((count, rows, width), bf),
             pltpu.VMEM((count, rows, width), bf),
             pltpu.VMEM((tile, count * rows), bf),
-            pltpu.VMEM((2, tile, max(width, units)), bf),
+            pltpu.VMEM((2, max(width, units) // lanes, tile, lanes), bf),
             dma((5,)),
             dma((2, 2, steps)),
             dma((2,)),
-            dma((2,)),
+            dma((2, max(width, units) // lanes)),
         ],
         compiler_params=pltpu.CompilerParams(
             collective_id=1, has_side_effects=True, vmem_limit_bytes=56 * 2**20
@@ -553,55 +556,534 @@
     )(length, n2, cot, wg, wu, wf)
 
 
-highest = lax.Precision.HIGHEST
-
-
-def rms_scale(values, gain):
-    return values * lax.rsqrt(jnp.mean(values * values, axis=-1, keepdims=True) + epsilon) * gain
-
-
-def gated_gelu(gate_pre, up_pre):
-    return jax.nn.gelu(gate_pre, approximate=True) * up_pre
-
-
-def rows_dot(left, right):
-    return lax.dot_general(
-        left, right, (((0,), (0,)), ((), ())), preferred_element_type=jnp.float32
+def when(condition, body):
+    if isinstance(condition, bool):
+        if condition:
+            body()
+    else:
+        pl.when(condition)(body)
+
+
+class ReplicaSum:
+    slots = 4
+
+    def __init__(self, replicas, chunk, chunks, source, target, work, core_box, path_box, sems):
+        self.mine = lax.axis_index("replica")
+        self.chunk, self.chunks, self.source, self.target = chunk, chunks, source, target
+        self.work, self.core_box, self.path_box, self.sems = work, core_box, path_box, sems
+        self.depth = work.shape[0]
+        bits = [1 << index for index in range(1, replicas.bit_length() - 1)]
+        self.orders = (bits, bits[::-1])
+        self.levels = len(bits)
+        self.last_phase = 2 * self.levels + 2
+        self.ticks = chunks + 2 * self.last_phase
+        self.half = chunk // 2
+
+    def bit(self, mask):
+        return jnp.where((self.mine & mask) != 0, 1, 0)
+
+    def region(self, path, level):
+        size = self.half // 2
+        offset = path * size
+        for mask in self.orders[path][:level]:
+            size //= 2
+            offset = offset + self.bit(mask) * size
+        return offset, size
+
+    def out_rows(self, chunk, offset, size):
+        start = chunk * self.chunk + self.bit(1) * self.half + offset
+        return self.target.at[pl.ds(pl.multiple_of(start, 16), size)]
+
+    def sem(self, kind, phase, path, chunk):
+        return self.sems.at[kind, phase, path, chunk % self.slots]
+
+    def remote(self, source, target, phase, path, chunk, mask):
+        return pltpu.make_async_remote_copy(
+            src_ref=source,
+            dst_ref=target,
+            send_sem=self.sem(0, phase, path, chunk),
+            recv_sem=self.sem(1, phase, path, chunk),
+            device_id={"replica": self.mine ^ mask},
+            device_id_type=MESH,
+        )
+
+    def core_copy(self, chunk):
+        start = chunk * self.chunk + (1 - self.bit(1)) * self.half
+        return self.remote(
+            self.source(start, self.half), self.core_box.at[chunk % self.slots], 0, 0, chunk, 1
+        )
+
+    def load_copy(self, chunk):
+        start = chunk * self.chunk + self.bit(1) * self.half
+        return pltpu.make_async_copy(
+            self.source(start, self.half), self.work.at[chunk % self.depth], self.sem(0, 0, 1, chunk)
+        )
+
+    def reduce_copy(self, chunk, path, level):
+        mask = self.orders[path][level - 1]
+        offset, size = self.region(path, level - 1)
+        size //= 2
+        start = pl.multiple_of(offset + (1 - self.bit(mask)) * size, 16)
+        return self.remote(
+            self.work.at[chunk % self.depth, pl.ds(start, size)],
+            self.box(chunk, path, level),
+            level, path, chunk, mask,
+        )
+
+    def box(self, chunk, path, level):
+        size = self.half // 2 >> level
+        start = sum(self.half // 2 >> step for step in range(1, level))
+        return self.path_box.at[chunk % self.slots, path, pl.ds(start, size)]
+
+    def add_box(self, chunk, path, level):
+        offset, size = self.region(path, level)
+        here = pl.ds(pl.multiple_of(offset, 16), size)
+        slot = chunk % self.depth
+        self.work[slot, here, :] = self.work[slot, here, :] + self.box(chunk, path, level)[...]
+
+    def own_copy(self, chunk, path):
+        offset, size = self.region(path, self.levels)
+        return pltpu.make_async_copy(
+            self.work.at[chunk % self.depth, pl.ds(pl.multiple_of(offset, 16), size)],
+            self.out_rows(chunk, offset, size),
+            self.sems.at[1, 0, 1 + path, chunk % self.slots],
+        )
+
+    def spread_copy(self, chunk, path, level):
+        offset, size = self.region(path, level)
+        if level == self.levels:
+            source = self.work.at[chunk % self.depth, pl.ds(pl.multiple_of(offset, 16), size)]
+        else:
+            source = self.out_rows(chunk, offset, size)
+        return self.remote(
+            source, self.out_rows(chunk, offset, size),
+            2 * self.levels + 1 - level, path, chunk, self.orders[path][level - 1],
+        )
+
+    def share_copy(self, chunk):
+        rows = self.out_rows(chunk, 0, self.half)
+        return self.remote(rows, rows, self.last_phase - 1, 0, chunk, 1)
+
+    def advance(self, phase, chunk):
+        levels = self.levels
+        if phase == 0:
+            self.core_copy(chunk).start()
+            self.load_copy(chunk).start()
+        elif phase <= levels + 1:
+            if phase == 1:
+                self.load_copy(chunk).wait()
+                self.core_copy(chunk).wait()
+                slot = chunk % self.depth
+                self.work[slot] = self.work[slot] + self.core_box[chunk % self.slots]
+            for path in range(2):
+                if phase > 1:
+                    self.reduce_copy(chunk, path, phase - 1).wait()
+                    self.add_box(chunk, path, phase - 1)
+                if phase <= levels:
+                    self.reduce_copy(chunk, path, phase).start()
+                else:
+                    self.own_copy(chunk, path).start()
+                    self.spread_copy(chunk, path, levels).start()
+        else:
+            level = 2 * levels + 1 - phase
+            if level >= 0:
+                for path in range(2):
+                    self.spread_copy(chunk, path, level + 1).wait()
+                    if level + 1 == levels:
+                        self.own_copy(chunk, path).wait()
+                    if level >= 1:
+                        self.spread_copy(chunk, path, level).start()
+                if level == 0:
+                    self.share_copy(chunk).start()
+
+
+def rms_backward(values, grads, gain):
+    scale = rms_rows(values)
+    unit = values * scale
+    scaled = grads * gain
+    inner = jnp.mean(scaled * unit, axis=-1, keepdims=True)
+    return scale * (scaled - unit * inner), jnp.sum(grads * unit, axis=0, keepdims=True)
+
+
+def backward_kernel(
+    count, replicas, chunk, chunks,
+    length_ref,
+    flat_hbm, back_hbm, res_hbm, middle_hbm, cot_hbm, x_hbm, q_hbm, k_hbm, v_hbm, att_hbm, lse_hbm, n1_hbm,
+    wq_hbm, wk_hbm, wv_hbm, wo_hbm, gains_ref, bias_ref, ids_ref,
+    sums_out, flat_out, result_out, input_out, small_out,
+    back, res, middle, cot, x_own, q_buf, k_buf, v_buf, att_buf, lse_buf, n1_buf, wq, wk, wv, wo,
+    back_box, res_box, total_buf, middle_grad, branch, grad_att, key_acc, value_acc, grad_qkv,
+    reverse, offsets, turned, stage, out_buf, small, small_parts, small_box, pair_box,
+    work, core_box, path_box,
+    load_sems, b_sems, r_sems, f_sems, a_sems, p_sems, pair_sems, stage_sems, out_sems, sum_sems,
+):
+    me = lax.axis_index("group")
+    mine = lax.axis_index("replica")
+    rows, width = middle.shape
+    total = rows * count
+    columns = wq.shape[1]
+    local_heads = columns // head_dim
+    sources = [
+        back_hbm, res_hbm, middle_hbm, cot_hbm, x_hbm, wo_hbm, att_hbm, q_hbm, k_hbm, v_hbm, lse_hbm, n1_hbm,
+        wq_hbm, wk_hbm, wv_hbm,
+    ]
+    targets = [
+        back, res, middle, cot, x_own, wo, att_buf, q_buf, k_buf, v_buf, lse_buf, n1_buf, wq, wk, wv
+    ]
+    loads = [
+        pltpu.make_async_copy(source, target, load_sems.at[index])
+        for index, (source, target) in enumerate(zip(sources, targets))
+    ]
+    masks = [1 << index for index in range(replicas.bit_length() - 1)]
+    barrier = pltpu.get_barrier_semaphore()
+
+    @pl.when(me > 0)
+    def _():
+        pl.semaphore_signal(barrier, inc=1, device_id={"group": me - 1}, device_id_type=MESH)
+
+    @pl.when(me < count - 1)
+    def _():
+        pl.semaphore_signal(barrier, inc=1, device_id={"group": me + 1}, device_id_type=MESH)
+
+    for mask in masks:
+        pl.semaphore_signal(barrier, inc=1, device_id={"replica": mine ^ mask}, device_id_type=MESH)
+    peers = jnp.where(me > 0, 1, 0) + jnp.where(me < count - 1, 1, 0) + len(masks)
+    for load in loads[:5]:
+        load.start()
+    pl.semaphore_wait(barrier, peers)
+
+    ffn_rows = flat_hbm.shape[0]
+    from_ffn = ffn_rows // chunk
+
+    def make_sum(source_ref, base):
+        return lambda start, size: source_ref.at[pl.ds(pl.multiple_of(start - base, 16), size)]
+
+    parts = ReplicaSum(
+        replicas, chunk, chunks, None, sums_out, work, core_box, path_box, sum_sems
     )
-
-
-def cols_dot(left, right):
-    return lax.dot_general(
-        left, right, (((1,), (1,)), ((), ())), preferred_element_type=jnp.float32
+    from_first, from_second = make_sum(flat_hbm, 0), make_sum(flat_out, ffn_rows)
+
+    def tick(time):
+        for phase in range(parts.last_phase, -1, -1):
+            piece = time - 2 * phase
+            if isinstance(piece, int):
+                inside = 0 <= piece < chunks
+            else:
+                inside = (piece >= 0) & (piece < chunks)
+
+            def body(phase=phase, piece=piece):
+                if phase > 1:
+                    if phase == parts.last_phase:
+                        parts.share_copy(piece).wait()
+                    else:
+                        parts.advance(phase, piece)
+                    return
+                for source, here in (
+                    (from_first, piece < from_ffn),
+                    (from_second, piece >= from_ffn),
+                ):
+                    def start(source=source):
+                        parts.source = source
+                        parts.core_copy(piece).start()
+                        parts.load_copy(piece).start()
+
+                    if phase == 0:
+                        when(here, start)
+                if phase == 1:
+                    parts.source = lambda start, size: flat_hbm.at[pl.ds(0, size)]
+                    parts.advance(1, piece)
+
+            when(inside, body)
+
+    back_line = LineScatter(me, count, back, back_box, b_sems)
+    res_line = LineScatter(me, count, res, res_box, r_sems)
+    first_line = LineScatter(me, count, back, back_box, f_sems)
+    branch_line = LineGather(me, count, branch, a_sems)
+    small_line = LineScatter(me, count, small_parts, small_box, p_sems)
+
+    tick(0)
+    for load in loads[5:]:
+        load.start()
+    anti = lax.broadcasted_iota(jnp.int32, (total, total), 0) + lax.broadcasted_iota(
+        jnp.int32, (total, total), 1
     )
-
-
-def plain_dot(left, right):
-    return jnp.dot(left, right, preferred_element_type=jnp.float32)
-
-
-def spread_offsets(vector, row_count, col_count):
-    span_width = row_count + col_count + 1
-    block_heads = vector.shape[0]
-    tiled_rows = jnp.broadcast_to(vector[:, None, :], (block_heads, row_count, span_width))
-    flattened = tiled_rows.reshape(block_heads, row_count * span_width)[
-        :, : row_count * (span_width - 1)
-    ]
-    return flattened.reshape(block_heads, row_count, span_width - 1)[:, :, row_count:]
-
-
-def fold_offsets(matrix):
-    block_heads, row_count, col_count = matrix.shape
-    padded = jnp.pad(matrix, ((0, 0), (0, 0), (row_count, 0)))
-    flattened = jnp.pad(
-        padded.reshape(block_heads, row_count * (row_count + col_count)), ((0, 0), (0, row_count))
+    reverse[...] = (anti == total - 1).astype(jnp.float32).astype(jnp.bfloat16)
+    loads[0].wait()
+    time = 1
+    for step in range(count - 1):
+        for side in range(2):
+            back_line.forward(side, step)
+        tick(time)
+        time += 1
+    for load in loads[2:5]:
+        load.wait()
+    total_buf[...] = back[me].astype(jnp.float32)
+    back_line.finish(total_buf)
+    position = me * rows + lax.broadcasted_iota(jnp.int32, (rows, 1), 0)
+    valid = (position < length_ref[0]).astype(jnp.float32)
+    grad_mid, gain_grad = rms_backward(middle[...], total_buf[...], gains_ref[1:2, :])
+    middle_grad[...] = cot[...].astype(jnp.float32) * valid + grad_mid
+    branch[me] = middle_grad[...].astype(jnp.bfloat16)
+    small_parts[...] = jnp.zeros_like(small_parts)
+    part_width = width // count
+    for owner in range(count):
+        small_parts[owner, 1:2, :] = gain_grad[:, owner * part_width : (owner + 1) * part_width]
+    branch_line.start(0)
+    for load in loads[5:]:
+        load.wait()
+
+    def attended_grad(block):
+        grad_att[block] = nt_dot(branch[block], wo[...]).astype(jnp.bfloat16)
+
+    attended_grad(me)
+    tick(time)
+    time += 1
+    for step in range(count - 1):
+        for side in range(2):
+            branch_line.wait_arrival(side, step)
+        if step + 1 < count - 1:
+            branch_line.start(step + 1)
+
+        @pl.loop(0, 2)
+        def _(side):
+            arrives = jnp.where(side == 0, me - 1 - step >= 0, me + 1 + step < count)
+
+            @pl.when(arrives)
+            def _():
+                attended_grad(jnp.where(side == 0, me - 1 - step, me + 1 + step))
+
+        if step + 1 < count - 1:
+            tick(time)
+            time += 1
+
+    tile = 256
+
+    def weight_grad(left, factor, base, height, per_output):
+        panels = factor.shape[1] // lanes
+        per_panel = per_output // lanes
+
+        def store(slot, panel, row):
+            return pltpu.make_async_copy(
+                stage.at[slot, panel],
+                flat_out.at[pl.ds(base + panel * height + row, tile)],
+                stage_sems.at[slot, panel],
+            )
+
+        @pl.loop(0, height // tile)
+        def _(index):
+            slot = lax.rem(index, 2)
+            row = pl.multiple_of(index * tile, tile)
+            turned[...] = left[:, :, pl.ds(row, tile)].reshape(total, tile).T
+            product = nn_dot(turned[...], factor).astype(jnp.bfloat16)
+
+            @pl.when(index >= 2)
+            def _():
+                for panel in range(panels):
+                    store(slot, panel, row).wait()
+
+            for panel in range(panels):
+                stage[slot, panel] = product[:, panel * lanes : (panel + 1) * lanes]
+                store(slot, panel, row).start()
+
+        for slot in range(min(2, height // tile)):
+            for panel in range(panels):
+                store(slot, panel, 0).wait()
+
+    weight_grad(att_buf, branch[...].reshape(total, width), 0, columns, width)
+    loads[1].wait()
+
+    mask_first, mask_second = head_masks()
+    key_valid = lax.broadcasted_iota(jnp.int32, (1, total), 1) < length_ref[0]
+    lane = lax.broadcasted_iota(jnp.int32, (1, lanes), 1)
+    offsets[...] = jnp.zeros_like(offsets)
+
+    def head_pair(pair):
+        cols = pl.ds(pl.multiple_of(pair * lanes, lanes), lanes)
+        key = k_buf[:, :, cols].reshape(total, lanes)
+        value = v_buf[:, :, cols].reshape(total, lanes)
+        key_acc[...] = jnp.zeros_like(key_acc)
+        value_acc[...] = jnp.zeros_like(value_acc)
+
+        @pl.loop(0, count)
+        def _(block):
+            query = q_buf[block, :, cols]
+            grads = grad_att[block, :, cols]
+            logs = lse_buf[block]
+            query_parts = []
+            for half, mask in enumerate((mask_first, mask_second)):
+                head = pair * 2 + half
+                query_half, grads_half = query * mask, grads * mask
+                scores = nt_dot(query_half, key)
+                scores = scores + offset_bias(bias_ref, head, block * rows, rows, total)
+                scores = jnp.where(key_valid, scores, negative)
+                log_total = jnp.sum(jnp.where(lane == head, logs, 0.0), axis=-1, keepdims=True)
+                probs = jnp.exp(scores - log_total)
+                grad_probs = nt_dot(grads_half, value)
+                inner = jnp.sum(probs * grad_probs, axis=-1, keepdims=True)
+                grad_scores = (probs * (grad_probs - inner)).astype(jnp.bfloat16)
+                query_parts.append(nn_dot(grad_scores, key))
+                key_acc[...] += nn_dot(query_half.astype(jnp.float32).T.astype(jnp.bfloat16), grad_scores)
+                value_acc[...] += nn_dot(
+                    grads_half.astype(jnp.float32).T.astype(jnp.bfloat16), probs.astype(jnp.bfloat16)
+                )
+                turned_scores = nn_dot(grad_scores, reverse[...])
+                padded = jnp.concatenate([turned_scores, jnp.zeros_like(turned_scores)], axis=1)
+                sheared = pltpu.roll(padded, 0, 1, stride=1, stride_axis=0)
+                sums = jnp.broadcast_to(jnp.sum(sheared, axis=0, keepdims=True), (8, 2 * total))
+                sums = pltpu.roll(sums, block * rows, 1)
+                offsets[pl.ds(head, 1), :] += sums[0:1, :]
+            grad_qkv[pl.ds(pl.multiple_of(block * rows, rows), rows), cols] = jnp.where(
+                lane < head_dim, query_parts[0], query_parts[1]
+            ).astype(jnp.bfloat16)
+
+        grad_qkv[:, pl.ds(pl.multiple_of(columns + pair * lanes, lanes), lanes)] = key_acc[
+            ...
+        ].T.astype(jnp.bfloat16)
+        grad_qkv[:, pl.ds(pl.multiple_of(2 * columns + pair * lanes, lanes), lanes)] = value_acc[
+            ...
+        ].T.astype(jnp.bfloat16)
+
+    pairs = local_heads // 2
+    for step in range(count - 1):
+        for side in range(2):
+            res_line.forward(side, step)
+        tick(time)
+        time += 1
+        if step < pairs:
+            head_pair(step)
+    for pair in range(count - 1, pairs):
+        head_pair(pair)
+    total_buf[...] = middle[...] + res[me].astype(jnp.float32)
+    res_line.finish(total_buf)
+    out_buf[0] = total_buf[...].astype(jnp.bfloat16)
+    result_copy = pltpu.make_async_copy(out_buf.at[0], result_out, out_sems.at[0])
+    result_copy.start()
+    tick(time)
+    time += 1
+    weight_grad(n1_buf, grad_qkv[...], columns * width // lanes, width, columns)
+    tick(time)
+    time += 1
+
+    back_line.wait_sends()
+
+    def first_part(block):
+        here = pl.ds(pl.multiple_of(block * rows, rows), rows)
+        back[block] = (
+            nt_dot(grad_qkv[here, 0:columns], wq[...])
+            + nt_dot(grad_qkv[here, columns : 2 * columns], wk[...])
+            + nt_dot(grad_qkv[here, 2 * columns :], wv[...])
+        ).astype(jnp.bfloat16)
+
+    @pl.loop(0, count)
+    def _(block):
+        first_part(block)
+
+    for step in range(count - 1):
+        for side in range(2):
+            first_line.forward(side, step)
+        tick(time)
+        time += 1
+    total_buf[...] = back[me].astype(jnp.float32)
+    first_line.finish(total_buf)
+    grad_in, gain_grad = rms_backward(
+        x_own[...].astype(jnp.float32), total_buf[...], gains_ref[0:1, :]
     )
-    sums_all = flattened.reshape(block_heads, row_count, row_count + col_count + 1).sum(axis=1)
-    return sums_all[:, 1 : row_count + col_count]
-
-
-def heads(matrix):
-    return matrix.reshape(matrix.shape[0], -1, head_dim)
+    out_buf[1] = (middle_grad[...] + grad_in).astype(jnp.bfloat16)
+    input_copy = pltpu.make_async_copy(out_buf.at[1], input_out, out_sems.at[1])
+    input_copy.start()
+    for owner in range(count):
+        small_parts[owner, 0:1, :] = gain_grad[:, owner * part_width : (owner + 1) * part_width]
+    for step in range(count - 1):
+        for side in range(2):
+            small_line.forward(side, step)
+        tick(time)
+        time += 1
+    small[0:8, :] = small_parts[me]
+    small_line.finish(small.at[pl.ds(0, 8)])
+    bucket = lax.broadcasted_iota(jnp.int32, (lanes, ids_ref.shape[1]), 0)
+    one_hot = (bucket == ids_ref[...]).astype(jnp.float32).astype(jnp.bfloat16)
+    high = offsets[...].astype(jnp.bfloat16)
+    rest = offsets[...] - high.astype(jnp.float32)
+    middle_part = rest.astype(jnp.bfloat16)
+    low_part = (rest - middle_part.astype(jnp.float32)).astype(jnp.bfloat16)
+    small[8:16, 0:lanes] = nt_dot(high, one_hot) + nt_dot(middle_part, one_hot) + nt_dot(low_part, one_hot)
+    small[8:16, lanes:] = jnp.zeros((8, part_width - lanes), jnp.float32)
+    for index, mask in enumerate(masks):
+        copy = pltpu.make_async_remote_copy(
+            src_ref=small,
+            dst_ref=pair_box.at[index],
+            send_sem=pair_sems.at[0, index],
+            recv_sem=pair_sems.at[1, index],
+            device_id={"replica": mine ^ mask},
+            device_id_type=MESH,
+        )
+        copy.start()
+        tick(time)
+        time += 1
+        copy.wait()
+        small[...] += pair_box[index]
+    small_out[...] = small[...]
+
+    @pl.loop(time, parts.ticks)
+    def _(now):
+        tick(now)
+
+    for line in (res_line, first_line, branch_line, small_line):
+        line.wait_sends()
+    result_copy.wait()
+    input_copy.wait()
+
+
+def backward(count, replicas, length, flat, back, res, middle, cot, x, q, k, v, att, lse, n1, wq, wk, wv, wo, gains, bias, ids):
+    rows, width = middle.shape
+    total = count * rows
+    columns = wq.shape[1]
+    bf, f32 = jnp.bfloat16, jnp.float32
+    shape = jax.ShapeDtypeStruct
+    steps = count - 1
+    dma = pltpu.SemaphoreType.DMA
+    chunk = flat.shape[0] // 15
+    attn_rows = 4 * columns * width // lanes
+    chunks = 15 + attn_rows // chunk
+    levels = replicas.bit_length() - 2
+    masks = levels + 1
+    depth = 2 * (levels + 2) + 2
+    part_width = width // count
+    vmem = pltpu.VMEM
+    blocks = lambda kind: vmem((count, rows, width), kind)
+    narrow = lambda: vmem((count, rows, columns), bf)
+    boxes = lambda: vmem((2, steps, rows, width), bf)
+    return pl.pallas_call(
+        functools.partial(backward_kernel, count, replicas, chunk, chunks),
+        name="backward",
+        out_shape=(
+            shape((flat.shape[0] + attn_rows, lanes), bf),
+            shape((attn_rows, lanes), bf),
+            shape((rows, width), bf),
+            shape((rows, width), bf),
+            shape((16, part_width), f32),
+        ),
+        in_specs=[smem_space] + [any_space] * 16 + [vmem_space] * 3,
+        out_specs=[any_space] * 4 + [vmem_space],
+        scratch_shapes=[
+            blocks(bf), blocks(bf), vmem((rows, width), f32), vmem((rows, width), bf), vmem((rows, width), bf),
+            narrow(), narrow(), narrow(), narrow(), vmem((count, rows, lanes), f32), blocks(bf),
+            vmem(wq.shape, bf), vmem(wk.shape, bf), vmem(wv.shape, bf), vmem(wo.shape, bf),
+            boxes(), boxes(), vmem((rows, width), f32), vmem((rows, width), f32), blocks(bf), narrow(),
+            vmem((lanes, total), f32), vmem((lanes, total), f32), vmem((total, 3 * columns), bf),
+            vmem((total, total), bf), vmem((8, 2 * total), f32), vmem((256, total), bf),
+            vmem((2, width // lanes, 256, lanes), bf), vmem((2, rows, width), bf),
+            vmem((16, part_width), f32), vmem((count, 8, part_width), f32), vmem((2, steps, 8, part_width), f32),
+            vmem((masks, 16, part_width), f32),
+            vmem((depth, chunk // 2, lanes), bf), vmem((4, chunk // 2, lanes), bf), vmem((4, 2, chunk // 4, lanes), bf),
+            dma((15,)), dma((2, 2, steps)), dma((2, 2, steps)), dma((2, 2, steps)), dma((2, 2, steps)),
+            dma((2, 2, steps)), dma((2, masks)), dma((2, width // lanes)), dma((2,)),
+            dma((2, 2 * levels + 3, 3, 4)),
+        ],
+        compiler_params=pltpu.CompilerParams(
+            collective_id=2, has_side_effects=True, vmem_limit_bytes=60 * 2**20
+        ),
+    )(length, flat, back, res, middle, cot, x, q, k, v, att, lse, n1, wq, wk, wv, wo, gains, bias, ids)
 
 
 def local(
@@ -620,115 +1102,48 @@
     w_ffn_out,
     cotangent,
 ):
-    group = lax.axis_index("group")
-    rows = inputs.shape[1]
-    length = seq_lengths[0]
-    total = rows * lax.axis_size("group")
-    start = group * rows
-    valid = jnp.arange(total) < length
-
-    def gather(values):
-        return lax.all_gather(values, "group", axis=0, tiled=True)
-
-    def scatter(values):
-        return lax.psum_scatter(
-            values.astype(jnp.bfloat16), "group", scatter_dimension=0, tiled=True
-        ).astype(jnp.float32)
-
     count = lax.axis_size("group")
+    replicas = lax.axis_size("replica")
     gains_local = jnp.pad(
         jnp.stack([norm1_gain, norm2_gain]).astype(jnp.float32), ((0, 6), (0, 0))
     )
     ids = jnp.pad(bucket_ids, (0, 1))[None, :]
-    (
-        normed_one, query, key, value, attended, log_totals, g_all, middle, normed_two, gains, bias_rows,
-    ) = attention_forward(
-        count, seq_lengths, inputs[0], cotangent[0], gains_local,
-        w_query, w_key, w_value, w_attn_out, ids, bias_table.T,
+    ids_back = jnp.pad(bucket_ids[::-1], (0, 1), constant_values=-1)[None, :]
+    normed_one, query, key, value, attended, log_totals, g_all, middle, normed_two, gains, bias = (
+        attention_forward(
+            count, seq_lengths, inputs[0], cotangent[0], gains_local,
+            w_query, w_key, w_value, w_attn_out, ids, bias_table.T,
+        )
     )
-    gate_part, up_part, ffn_part, back_part, result_part = feed_forward(
+    flat, back_part, result_part = feed_forward(
         count, seq_lengths, normed_two, g_all, w_gate, w_up, w_ffn_out
     )
-
-    def total_sum(values):
-        return lax.psum(values.astype(jnp.bfloat16), "replica").astype(jnp.float32)
-
-    ffn_out_grad, gate_grad, up_grad = total_sum(ffn_part), total_sum(gate_part), total_sum(up_part)
-    grad_normed_two = scatter(back_part.reshape(total, -1))
-    result = (middle + scatter(result_part.reshape(total, -1))).astype(jnp.bfloat16)
-    normed_one, query, key, value, attended = (
-        array.reshape(total, -1) for array in (normed_one, query, key, value, attended)
+    sums, _, result, input_grad, small = backward(
+        count, replicas, seq_lengths, flat, back_part, result_part, middle, cotangent[0], inputs[0],
+        query, key, value, attended, log_totals, normed_one,
+        w_query, w_key, w_value, w_attn_out, gains, bias, ids_back,
     )
-    gain_first, gain_second = gains[0], gains[1]
-    x_local = inputs[0].astype(jnp.float32)
-    buckets = bias_table.shape[0]
-    one_hot = (bucket_ids[:, None] == jnp.arange(buckets)[None, :]).astype(jnp.float32)
-    bias = spread_offsets(jnp.pad(bias_rows[:, :-1], ((0, 0), (1, 1))), total, total)
-    scores = jnp.einsum(
-        "qhd,khd->hqk", heads(query), heads(key), preferred_element_type=jnp.float32
-    )
-    scores = jnp.where(valid[None, None, :], scores + bias, negative)
-    log_rows = log_totals.reshape(total, -1)[:, : bias.shape[0]].T
-    probs = jnp.exp(scores - log_rows[:, :, None])
-    probs_low = probs.astype(jnp.bfloat16)
-
-    row_valid = start + jnp.arange(rows) < length
-    g_local = jnp.where(row_valid[:, None], cotangent[0], jnp.bfloat16(0)).astype(jnp.float32)
-    _, pull_two = jax.vjp(rms_scale, middle, gain_second)
-    grad_mid_norm, gain_two_grad = pull_two(grad_normed_two)
-    grad_middle = g_local + grad_mid_norm
-    grad_branch = gather(grad_middle.astype(jnp.bfloat16))
-
-    attn_out_grad = rows_dot(attended, grad_branch)
-    grad_attended = cols_dot(grad_branch, w_attn_out).astype(jnp.bfloat16)
-    grad_probs = jnp.einsum(
-        "qhd,khd->hqk", heads(grad_attended), heads(value), preferred_element_type=jnp.float32
-    )
-    inner_sum = jnp.sum(probs * grad_probs, axis=-1, keepdims=True)
-    grad_scores = (probs * (grad_probs - inner_sum)).astype(jnp.bfloat16)
-
-    def merge(values):
-        return values.reshape(total, -1).astype(jnp.bfloat16)
-
-    grad_query = merge(
-        jnp.einsum("hqk,khd->qhd", grad_scores, heads(key), preferred_element_type=jnp.float32)
-    )
-    grad_key = merge(
-        jnp.einsum("hqk,qhd->khd", grad_scores, heads(query), preferred_element_type=jnp.float32)
-    )
-    grad_value = merge(
-        jnp.einsum(
-            "hqk,qhd->khd", probs_low, heads(grad_attended), preferred_element_type=jnp.float32
-        )
-    )
-    offset_sums = fold_offsets(grad_scores.astype(jnp.float32))
-    table_grad = jnp.dot(offset_sums, one_hot, precision=highest).T
-    query_grad = rows_dot(normed_one, grad_query)
-    key_grad = rows_dot(normed_one, grad_key)
-    value_grad = rows_dot(normed_one, grad_value)
-    grad_normed_one = scatter(
-        cols_dot(grad_query, w_query) + cols_dot(grad_key, w_key) + cols_dot(grad_value, w_value)
-    )
-    query_grad, key_grad, value_grad, attn_out_grad = (
-        total_sum(query_grad), total_sum(key_grad), total_sum(value_grad), total_sum(attn_out_grad)
-    )
-    table_grad = lax.psum(table_grad, "replica")
-    _, pull_one = jax.vjp(rms_scale, x_local, gain_first)
-    grad_in_norm, gain_one_grad = pull_one(grad_normed_one)
-    input_grad = (grad_middle + grad_in_norm).astype(jnp.bfloat16)
-    gain_sums = lax.psum(jnp.stack([gain_one_grad, gain_two_grad]), ("replica", "group"))
-    width = norm1_gain.shape[0]
-    gain_sums = lax.dynamic_slice_in_dim(gain_sums, group * width, width, axis=1)
+    start = 0
+    grads = []
+    for weight in (w_ffn_out, w_gate, w_up, w_attn_out, w_query, w_key, w_value):
+        height, depth = weight.shape
+        panels = depth // lanes
+        part = sums[start : start + panels * height].reshape(panels, height, lanes)
+        grads.append(part.transpose(1, 0, 2).reshape(height, depth).astype(jnp.float32))
+        start += panels * height
+    ffn_out_grad, gate_grad, up_grad, attn_out_grad, query_grad, key_grad, value_grad = grads
+    buckets, local_heads = bias_table.shape
+    table_grad = small[8 : 8 + local_heads, :buckets].T
     return (
         result[None],
         input_grad[None],
-        gain_sums[0],
+        small[0],
         query_grad,
         key_grad,
         value_grad,
         attn_out_grad,
         table_grad,
-        gain_sums[1],
+        small[1],
         gate_grad,
         up_grad,
         ffn_out_grad,

time: 809 us -> 594 us (0.73)
  Pallas kernels: 162 us -> 507 us
  waiting for transfers between devices: 309 us -> 0 us
  local copies, waits for them, and re-layouts: 164 us -> 58.8 us
  blocking collectives: 54.3 us -> 0 us
  other arithmetic: 62.9 us -> 19.3 us
  matrix products: 31.7 us -> 0 us
  between operations: 15.1 us -> 1.8 us
    pallas_call x0 -> x1, Pallas kernels: none -> 345 us  [backward(): pl.pallas_call(functools.partial(backward_kernel, count, replicas, chunk,...]
    psum x1 -> x0, waiting for transfers between devices: 240 us -> none  [total_sum(): return lax.psum(values.astype(jnp.bfloat16), 'replica').astype(jnp.float32)]
    reduce_scatter x3 -> x0, waiting for transfers between devices: 68.9 us -> none  [scatter(): lax.psum_scatter(values.astype(jnp.bfloat16), 'group', scatter_dimension=...]
    unnamed x77 -> x14, local copies, waits for them, and re-layouts: 92 us -> 25.3 us
    psum x2 -> x0, blocking collectives: 54.3 us -> none  [the longest x1 41.4 us: local(): lax.psum(jnp.stack([gain_one_grad, gain_two_grad]), ('replica', 'group'))]
    reshape x2 -> x0, local copies, waits for them, and re-layouts: 47 us -> none  [the longest x1 30.5 us: fold_offsets(): flattened.reshape(block_heads, row_count, row_count + col_count + 1)]
    dot_general x14 -> x0, matrix products: 31.7 us -> none  [the longest x4 10.5 us: rows_dot(): lax.dot_general(left, right, (((0,), (0,)), ((), ())), preferred_element_...]
    convert_element_type x9 -> x4, other arithmetic: 38.4 us -> 18.7 us  [local(): part.transpose(1, 0, 2).reshape(height, depth).astype(jnp.float32)]
  transfers between devices with their start and end apart: 5 -> 0, of which waited for: 2 -> 0; matrix products, arithmetic and copies ran while one was open for 23% -> 0% of each run, Pallas kernels for 0% -> 0%
where the time goes in v4:
time: 594 us; the launch traced here: 586 us
  Pallas kernels  507 us (85%)
  local copies, waits for them, and re-layouts  58.8 us (10%)
  other arithmetic  19.3 us (3%)
    pallas_call x1, Pallas kernels, backward(): pl.pallas_call(functools.partial(backward_kernel, count, replicas, chunk,...  345 us
    pallas_call x1, Pallas kernels, attention_forward(): pl.pallas_call(functools.partial(attention_forward_kernel, count), name='...  101 us
    pallas_call x1, Pallas kernels, feed_forward(): pl.pallas_call(functools.partial(feed_forward_kernel, count, tile), name=...  60 us
    unnamed x14, local copies, waits for them, and re-layouts  25.3 us
    convert_element_type x4, other arithmetic, local(): part.transpose(1, 0, 2).reshape(height, depth).astype(jnp.float32)  18.7 us
    convert_element_type x2, local copies, waits for them, and re-layouts, local(): part.transpose(1, 0, 2).reshape(height, depth).astype(jnp.float32)  17.2 us

profile of v4, /device:TPU:17, one launch (start us, length us, event | category | flops | bytes accessed | tf_op | source)
XLA Modules:
  0.0 586.4 jit_solution(17904463744571670374)
XLA Ops:
  1.3 0.7 stack.10
  2.0 0.7 stack.9
  2.7 0.6 fusion.3.gains_hbm
  3.3 1.3 pad.15
  4.6 101.3 %attention_forward.1 = (bf16[4,128,2048]{2,1,0:T(8,128)(2,1)}, bf16[4,128,512]{2,1,0:T(8,128)(2,1)}, bf16[4,128,512]{2,1,0:T(8,128)(2,1)}, bf16[4,128,512]{2,1,0...) custom-call(s32[1]{0:T(128)S(6)} %copy.54.length_ref, ...), custom_call_target="tpu_custom_call" | custom-call | tf_op jit(solution)/shard_map/attention_forward/pallas_call | solution.py:340
  105.9 0.0 copy-start.3
  105.9 60.0 %feed_forward.1 = (bf16[61440,128]{1,0:T(8,128)(2,1)}, bf16[4,128,2048]{2,1,0:T(8,128)(2,1)}, bf16[4,128,2048]{2,1,0:T(8,128)(2,1)}) custom-call(s32[1]{0:T(128)S(6)} %copy.54.length_ref, bf16[128,2048]{1,0:T(8,128)(2,1)} %get-tuple-element.30.n2_hbm, bf16[4,128,2048]{2,1,0:T(8,128)(2,1)} %get-tuple-element.31.cot_hbm, bf16[2048,1280]{1,0:T(8,128)(2,1)} %wg_hbm.1, ...), custom_call_target="tpu_custom_call" | custom-call | tf_op jit(solution)/shard_map/feed_forward/pallas_call | solution.py:525
  165.9 0.0 copy-done.3
  165.9 0.1 reverse
  166.0 0.1 slice.41
  166.1 0.6 pad.16
  166.7 345.2 %backward.1 = (bf16[94208,128]{1,0:T(8,128)(2,1)}, bf16[32768,128]{1,0:T(8,128)(2,1)}, bf16[128,2048]{1,0:T(8,128)(2,1)}, bf16[128,2048]{1,0:T(8,128)(2,1)}, f32[16,512]{1,0:T(8,128)}) custom-call(s32[1]{0:T(128)S(6)} %copy.54.length_ref, bf16[61440,128]{1,0:T(8,128)(2,1)} %get-tuple-element.32.flat_hbm, bf16[4,128,2048]{2,1,0:T(8,128)(2,1)} %get-tuple-element.33.back_hbm, ...), custom_call_target="tpu_custom_call" | custom-call | tf_op jit(solution)/shard_map/backward/pallas_call | solution.py:1056
  511.9 1.4 fusion.6
  513.3 3.7 fusion.5
  517.0 0.0 copy-start
  517.0 2.7 copy_bitcast_fusion.4
  519.7 5.3 copy_bitcast_fusion.2
  524.9 2.7 copy_bitcast_fusion.1
  527.6 2.0 slice_bitcast_fusion
  529.6 1.1 copy-done
  530.8 5.9 %fusion.4 = (bf16[20480,128]{1,0:T(8,128)(2,1)}, bf16[20480,128]{1,0:T(8,128)(2,1)}, bf16[20480,128]{1,0:T(8,128)(2,1)}) fusion(bf16[94208,128]{1,0:T(8,128)(2,1)S(1)} %copy-done), kind=kLoop, calls=%fused_computation.16 | loop fusion | bytes 31457280 | tf_op jit(solution)/shard_map/slice | solution.py:1131
  536.7 8.6 %copy.37 = f32[10,2048,128]{1,2,0:T(8,128)} copy(bf16[10,2048,128]{2,1,0:T(8,128)(2,1)} %bitcast.66) | data formatting | bytes 15728640 | tf_op jit(solution)/shard_map/convert_element_type | solution.py:1132
  545.3 11.2 %copy.40 = f32[2048,1280]{1,0:T(8,128)} copy(f32[2048,1280]{0,1:T(8,128)} %bitcast.62) | data formatting | bytes 20971520
  556.5 8.6 %copy.38 = f32[10,2048,128]{1,2,0:T(8,128)} copy(bf16[10,2048,128]{2,1,0:T(8,128)(2,1)} %bitcast.65) | data formatting | bytes 15728640 | tf_op jit(solution)/shard_map/convert_element_type | solution.py:1132
  565.1 11.2 %copy.41 = f32[2048,1280]{1,0:T(8,128)} copy(f32[2048,1280]{0,1:T(8,128)} %bitcast.63) | data formatting | bytes 20971520
  576.3 0.0 copy-start.2
  576.3 0.0 copy-start.1
  576.3 8.1 %copy_bitcast_fusion = f32[1280,2048]{1,0:T(8,128)} fusion(bf16[16,1280,128]{2,1,0:T(8,128)(2,1)} %bitcast.64), kind=kLoop, calls=%fused_computation | loop fusion | flops 2621440 | bytes 15728640 | tf_op jit(solution)/shard_map/convert_element_type | solution.py:1132
  584.3 0.0 copy-done.2
  584.3 0.8 copy.55
  585.1 0.0 copy-done.1
  585.1 0.8 copy.56
Async XLA Ops:
  105.9 60.0 %copy-start.3 = (s32[1023]{0:T(1024)S(1)}, s32[1023]{0:T(1024)}, u32[]{:S(2)}) copy-start(s32[1023]{0:T(1024)} %param.16) | copy-start | bytes 12280
  517.0 13.8 %copy-start = (bf16[94208,128]{1,0:T(8,128)(2,1)S(1)}, bf16[94208,128]{1,0:T(8,128)(2,1)}, u32[]{:S(2)}) copy-start(bf16[94208,128]{1,0:T(8,128)(2,1)} %get-tuple-element.47) | copy-start | bytes 72351744
  576.3 8.1 %copy-start.2 = (bf16[128,2048]{1,0:T(8,128)(2,1)S(1)}, bf16[128,2048]{1,0:T(8,128)(2,1)}, u32[]{:S(2)}) copy-start(bf16[128,2048]{1,0:T(8,128)(2,1)} %get-tuple-element.44) | copy-start | bytes 1572868
  576.3 8.9 %copy-start.1 = (bf16[128,2048]{1,0:T(8,128)(2,1)S(1)}, bf16[128,2048]{1,0:T(8,128)(2,1)}, u32[]{:S(2)}) copy-start(bf16[128,2048]{1,0:T(8,128)(2,1)} %get-tuple-element.45) | copy-start | bytes 1572868

commit v5 on v4

--- a/solution.py
+++ b/solution.py
@@ -42,119 +42,148 @@
 
 
 class LineGather:
-    def __init__(self, me, count, buffer, sems):
-        self.me, self.count, self.buffer, self.sems = me, count, buffer, sems
-
-    def copy(self, side, step):
-        shift = 1 if side == 0 else -1
-        block = self.me - step if side == 0 else self.me + step
+    def __init__(self, me, count, buffer, sems, subs=1):
+        self.me, self.count, self.buffer, self.sems, self.subs = me, count, buffer, sems, subs
+        self.pieces = (count - 1) * subs
+        self.size = buffer.shape[1] // subs
+
+    def copy(self, side, piece, hops):
+        block = self.me - hops if side == 0 else self.me + hops
+        here = self.buffer.at[block, pl.ds(piece % self.subs * self.size, self.size)]
         return pltpu.make_async_remote_copy(
-            src_ref=self.buffer.at[block],
-            dst_ref=self.buffer.at[block],
-            send_sem=self.sems.at[side, 0, step],
-            recv_sem=self.sems.at[side, 1, step],
-            device_id={"group": self.me + shift},
+            src_ref=here,
+            dst_ref=here,
+            send_sem=self.sems.at[side, 0, piece],
+            recv_sem=self.sems.at[side, 1, piece],
+            device_id={"group": self.me + (1 if side == 0 else -1)},
             device_id_type=MESH,
         )
 
-    def sends(self, side, step):
+    def sends(self, side, piece):
+        hops = piece // self.subs
         if side == 0:
-            return (self.me - step >= 0) & (self.me + 1 < self.count)
-        return (self.me + step < self.count) & (self.me >= 1)
-
-    def arrives(self, side, step):
+            return (self.me - hops >= 0) & (self.me + 1 < self.count)
+        return (self.me + hops < self.count) & (self.me >= 1)
+
+    def arrives(self, side, piece):
+        hops = piece // self.subs
         if side == 0:
-            return self.me - 1 - step >= 0
-        return self.me + 1 + step < self.count
-
-    def arrived_block(self, side, step):
-        return self.me - 1 - step if side == 0 else self.me + 1 + step
-
-    def start(self, step):
+            return self.me - 1 - hops >= 0
+        return self.me + 1 + hops < self.count
+
+    def send(self, piece):
         for side in range(2):
-            @pl.when(self.sends(side, step))
+            @pl.when(self.sends(side, piece))
             def _():
-                self.copy(side, step).start()
-
-    def wait_arrival(self, side, step):
-        @pl.when(self.arrives(side, step))
-        def _():
-            block = self.arrived_block(side, step)
-            pltpu.make_async_remote_copy(
-                src_ref=self.buffer.at[block],
-                dst_ref=self.buffer.at[block],
-                send_sem=self.sems.at[side, 0, step],
-                recv_sem=self.sems.at[side, 1, step],
-                device_id={"group": self.me},
-                device_id_type=MESH,
-            ).wait_recv()
+                self.copy(side, piece, piece // self.subs).start()
+
+    def begin(self):
+        for piece in range(self.subs):
+            self.send(piece)
+
+    def arrive(self, piece):
+        for side in range(2):
+            @pl.when(self.arrives(side, piece))
+            def _():
+                self.copy(side, piece, piece // self.subs + 1).wait_recv()
+
+        if piece + self.subs < self.pieces:
+            self.send(piece + self.subs)
+
+    def arrive_block(self, hops, body):
+        for piece in range(hops * self.subs, (hops + 1) * self.subs):
+            self.arrive(piece)
+        self.each_block(hops, body)
+
+    def each_block(self, hops, body):
+        @pl.loop(0, 2)
+        def _(side):
+            block = jnp.where(side == 0, self.me - 1 - hops, self.me + 1 + hops)
+
+            @pl.when((block >= 0) & (block < self.count))
+            def _():
+                body(block)
 
     def wait_sends(self):
-        for step in range(self.count - 1):
+        for piece in range(self.pieces):
             for side in range(2):
-                @pl.when(self.sends(side, step))
+                @pl.when(self.sends(side, piece))
                 def _():
-                    self.copy(side, step).wait_send()
+                    self.copy(side, piece, piece // self.subs).wait_send()
 
 
 class LineScatter:
-    def __init__(self, me, count, parts, inbox, sems):
-        self.me, self.count, self.parts, self.inbox, self.sems = me, count, parts, inbox, sems
-
-    def target(self, side, step):
-        return step if side == 0 else self.count - 1 - step
-
-    def passes(self, side, step):
-        if side == 0:
-            return step < self.me
-        return self.count - 1 - step > self.me
-
-    def receives(self, side, step):
-        if side == 0:
-            return (step <= self.me) & (self.me + 1 < self.count)
-        return (self.count - 1 - step >= self.me) & (self.me >= 1)
-
-    def copy(self, side, step):
-        shift = -1 if side == 0 else 1
+    def __init__(self, me, count, parts, inbox, total, sems, subs=1):
+        self.me, self.count, self.parts, self.inbox = me, count, parts, inbox
+        self.total, self.sems, self.subs = total, sems, subs
+        self.times = (count - 1) * subs + 1
+        self.size = parts.shape[1] // subs
+
+    def order(self, index):
+        picked = 0
+        for device in range(self.count):
+            due = [(step * self.subs + self.count - 1 - device, step) for step in range(device)]
+            due += [
+                (step * self.subs + device, self.count - 1 - step)
+                for step in range(self.count - 1 - device)
+            ]
+            blocks = [block for _, block in sorted(due)] + [device]
+            picked = picked + jnp.where(self.me == device, blocks[index], 0)
+        return picked
+
+    def copy(self, side, piece):
+        step = piece // self.subs
+        here = pl.ds(pl.multiple_of(piece % self.subs * self.size, self.size), self.size)
+        owner = step if side == 0 else self.count - 1 - step
         return pltpu.make_async_remote_copy(
-            src_ref=self.parts.at[self.target(side, step)],
-            dst_ref=self.inbox.at[side, step],
-            send_sem=self.sems.at[side, 0, step],
-            recv_sem=self.sems.at[side, 1, step],
-            device_id={"group": self.me + shift},
+            src_ref=self.parts.at[owner, here],
+            dst_ref=self.inbox.at[self.slot(side, step), here],
+            send_sem=self.sems.at[side, 0, piece],
+            recv_sem=self.sems.at[side, 1, piece],
+            device_id={"group": self.me + (-1 if side == 0 else 1)},
             device_id_type=MESH,
         )
 
-    def forward(self, side, step):
-        @pl.when(self.passes(side, step))
-        def _():
-            @pl.when(self.receives(side, step))
+    def slot(self, side, step):
+        return step if side == 0 else self.count - step
+
+    def at_time(self, time):
+        for side in range(2):
+            before = self.count - 1 - self.me if side == 0 else self.me
+            after = self.count - 1 - before
+            piece = time - before
+            step = piece // self.subs
+
+            @pl.when((piece >= 0) & (step < after))
             def _():
-                self.copy(side, step).wait_recv()
-                target = self.target(side, step)
-                self.parts[target] = (
-                    self.parts[target].astype(jnp.float32)
-                    + self.inbox[side, step].astype(jnp.float32)
-                ).astype(self.parts.dtype)
-
-            self.copy(side, step).start()
-
-    def finish(self, total_ref):
-        for side in range(2):
-            has = self.me + 1 < self.count if side == 0 else self.me >= 1
-
-            @pl.when(has)
+                owner = step if side == 0 else self.count - 1 - step
+                here = pl.ds(pl.multiple_of(piece % self.subs * self.size, self.size), self.size)
+
+                @pl.when(before > 0)
+                def _():
+                    self.copy(side, piece).wait_recv()
+                    self.parts[owner, here, :] = (
+                        self.parts[owner, here, :].astype(jnp.float32)
+                        + self.inbox[self.slot(side, step), here, :].astype(jnp.float32)
+                    ).astype(self.parts.dtype)
+
+                self.copy(side, piece).start()
+
+            @pl.when((piece >= 0) & (step == after) & (before > 0))
             def _():
-                step = self.me if side == 0 else self.count - 1 - self.me
-                self.copy(side, step).wait_recv()
-                total_ref[...] += self.inbox[side, step].astype(jnp.float32)
+                here = pl.ds(pl.multiple_of(piece % self.subs * self.size, self.size), self.size)
+                self.copy(side, piece).wait_recv()
+                self.total[here, :] += self.inbox[self.slot(side, step), here, :].astype(jnp.float32)
 
     def wait_sends(self):
-        for step in range(self.count - 1):
+        for piece in range((self.count - 1) * self.subs):
+            step = piece // self.subs
             for side in range(2):
-                @pl.when(self.passes(side, step))
+                after = self.me if side == 0 else self.count - 1 - self.me
+
+                @pl.when(step < after)
                 def _():
-                    self.copy(side, step).wait_send()
+                    self.copy(side, piece).wait_send()
 
 
 def head_masks():
@@ -176,7 +205,7 @@
 
 
 def attention_forward_kernel(
-    count,
+    count, subs,
     length_ref,
     x_hbm, cot_hbm, gains_hbm, wq_hbm, wk_hbm, wv_hbm, wo_hbm, ids_ref, table_ref,
     n1_out, q_out, k_out, v_out, att_out, lse_out, cot_out, middle_out, n2_out, gains_out, bias_out,
@@ -205,23 +234,20 @@
     for load in loads:
         load.start()
     line_barrier(me, count)
-    x_line = LineGather(me, count, x_all, x_sems)
+    x_line = LineGather(me, count, x_all, x_sems, subs)
     g_line = LineGather(me, count, gains_all, g_sems)
-    c_line = LineGather(me, count, cot_out, c_sems)
+    c_line = LineGather(me, count, cot_out, c_sems, subs)
     loads[1].wait()
-    g_line.start(0)
+    g_line.begin()
     loads[0].wait()
-    x_line.start(0)
+    x_line.begin()
 
     bucket = lax.broadcasted_iota(jnp.int32, (table_ref.shape[1], ids_ref.shape[1]), 0)
     one_hot = (bucket == ids_ref[...]).astype(jnp.float32).astype(jnp.bfloat16)
     bias_out[...] = nn_dot(table_ref[...], one_hot)
 
-    for step in range(count - 1):
-        for side in range(2):
-            g_line.wait_arrival(side, step)
-        if step + 1 < count - 1:
-            g_line.start(step + 1)
+    for piece in range(g_line.pieces):
+        g_line.arrive(piece)
     for owner in range(count):
         gains_out[:, owner * (width // count) : (owner + 1) * (width // count)] = gains_all[owner]
     for load in loads[2:5]:
@@ -235,23 +261,15 @@
         k_buf[block] = nn_dot(normed, wk[...]).astype(jnp.bfloat16)
         v_buf[block] = nn_dot(normed, wv[...]).astype(jnp.bfloat16)
 
+    for piece in range(subs):
+        x_line.arrive(piece)
     project(me)
-    for step in range(count - 1):
-        for side in range(2):
-            x_line.wait_arrival(side, step)
-        if step + 1 < count - 1:
-            x_line.start(step + 1)
-
-        @pl.loop(0, 2)
-        def _(side):
-            arrives = jnp.where(side == 0, me - 1 - step >= 0, me + 1 + step < count)
-
-            @pl.when(arrives)
-            def _():
-                project(jnp.where(side == 0, me - 1 - step, me + 1 + step))
+    x_line.each_block(0, project)
+    for hops in range(1, count - 1):
+        x_line.arrive_block(hops, project)
 
     loads[6].wait()
-    c_line.start(0)
+    c_line.begin()
     loads[5].wait()
     mask_first, mask_second = head_masks()
     key_valid = lax.broadcasted_iota(jnp.int32, (1, total), 1) < length_ref[0]
@@ -282,27 +300,15 @@
                 jnp.bfloat16
             )
 
-    def attend_and_project(block):
+    scatter = LineScatter(me, count, parts, inbox, total_buf, s_sems, subs)
+    arrived = 0
+    for index in range(count - 1):
+        block = scatter.order(index)
         attend(block)
         parts[block] = nn_dot(att_buf[block], wo[...]).astype(jnp.bfloat16)
-
-    scatter = LineScatter(me, count, parts, inbox, s_sems)
-    for step in range(count - 1):
-        @pl.loop(0, 2)
-        def _(side):
-            passes = jnp.where(side == 0, step < me, count - 1 - step > me)
-
-            @pl.when(passes)
-            def _():
-                attend_and_project(jnp.where(side == 0, step, count - 1 - step))
-
-        for side in range(2):
-            scatter.forward(side, step)
-        if step < count - 2:
-            for side in range(2):
-                c_line.wait_arrival(side, step)
-            c_line.start(step + 1)
+        scatter.at_time(index)
     attend(me)
+    total_buf[...] = x_all[me].astype(jnp.float32) + nn_dot(att_buf[me], wo[...])
     outs = [
         pltpu.make_async_copy(source, target, out_sems.at[index])
         for index, (source, target) in enumerate(
@@ -311,8 +317,11 @@
     ]
     for copy in outs:
         copy.start()
-    total_buf[...] = x_all[me].astype(jnp.float32) + nn_dot(att_buf[me], wo[...])
-    scatter.finish(total_buf)
+    for time in range(count - 1, scatter.times):
+        scatter.at_time(time)
+        if arrived < c_line.pieces:
+            c_line.arrive(arrived)
+            arrived += 1
     middle = total_buf[...]
     n2_buf[...] = (middle * rms_rows(middle) * gains_out[1:2, :]).astype(jnp.bfloat16)
     tail = [
@@ -321,8 +330,8 @@
     ]
     for copy in tail:
         copy.start()
-    for side in range(2):
-        c_line.wait_arrival(side, count - 2)
+    for piece in range(arrived, c_line.pieces):
+        c_line.arrive(piece)
     for line in (g_line, x_line, c_line, scatter):
         line.wait_sends()
     for copy in outs + tail:
@@ -336,9 +345,10 @@
     bf, f32 = jnp.bfloat16, jnp.float32
     shape = jax.ShapeDtypeStruct
     steps = count - 1
+    subs = 2
     dma = pltpu.SemaphoreType.DMA
     return pl.pallas_call(
-        functools.partial(attention_forward_kernel, count),
+        functools.partial(attention_forward_kernel, count, subs),
         name="attention_forward",
         out_shape=(
             shape((count, rows, width), bf),
@@ -363,7 +373,7 @@
             pltpu.VMEM(wv.shape, bf),
             pltpu.VMEM(wo.shape, bf),
             pltpu.VMEM((count, rows, width), bf),
-            pltpu.VMEM((2, steps, rows, width), bf),
+            pltpu.VMEM((count + 1, rows, width), bf),
             pltpu.VMEM((count, rows, width), bf),
             pltpu.VMEM((count, rows, columns), bf),
             pltpu.VMEM((count, rows, columns), bf),
@@ -373,10 +383,10 @@
             pltpu.VMEM((rows, width), f32),
             pltpu.VMEM((rows, width), bf),
             dma((7,)),
+            dma((2, 2, steps * subs)),
             dma((2, 2, steps)),
-            dma((2, 2, steps)),
-            dma((2, 2, steps)),
-            dma((2, 2, steps)),
+            dma((2, 2, steps * subs)),
+            dma((2, 2, steps * subs)),
             dma((8,)),
         ],
         compiler_params=pltpu.CompilerParams(
@@ -395,7 +405,7 @@
 
 
 def feed_forward_kernel(
-    count, tile,
+    count, tile, subs,
     length_ref,
     n2_hbm, cot_hbm, wg_hbm, wu_hbm, wf_hbm,
     flat_out, back_out, res_out,
@@ -415,9 +425,9 @@
     for load in loads:
         load.start()
     line_barrier(me, count)
-    line = LineGather(me, count, n2_all, n_sems)
+    line = LineGather(me, count, n2_all, n_sems, subs)
     loads[0].wait()
-    line.start(0)
+    line.begin()
     for load in loads[1:]:
         load.wait()
 
@@ -453,20 +463,8 @@
             res_buf[block, :, cols] = nn_dot(hid[block], wf[:, cols]).astype(jnp.bfloat16)
 
     block_pass(me)
-    for step in range(count - 1):
-        for side in range(2):
-            line.wait_arrival(side, step)
-        if step + 1 < count - 1:
-            line.start(step + 1)
-
-        @pl.loop(0, 2)
-        def _(side):
-            arrives = jnp.where(side == 0, me - 1 - step >= 0, me + 1 + step < count)
-
-            @pl.when(arrives)
-            def _():
-                block_pass(jnp.where(side == 0, me - 1 - step, me + 1 + step))
-
+    for hops in range(count - 1):
+        line.arrive_block(hops, block_pass)
     outs = [
         pltpu.make_async_copy(back_buf, back_out, out_sems.at[0]),
         pltpu.make_async_copy(res_buf, res_out, out_sems.at[1]),
@@ -521,9 +519,10 @@
     bf = jnp.bfloat16
     shape = jax.ShapeDtypeStruct
     steps = count - 1
+    subs = 2
     dma = pltpu.SemaphoreType.DMA
     return pl.pallas_call(
-        functools.partial(feed_forward_kernel, count, tile),
+        functools.partial(feed_forward_kernel, count, tile, subs),
         name="feed_forward",
         out_shape=(
             shape((3 * units * width // lanes, lanes), bf),
@@ -546,7 +545,7 @@
             pltpu.VMEM((tile, count * rows), bf),
             pltpu.VMEM((2, max(width, units) // lanes, tile, lanes), bf),
             dma((5,)),
-            dma((2, 2, steps)),
+            dma((2, 2, steps * subs)),
             dma((2,)),
             dma((2, max(width, units) // lanes)),
         ],
@@ -565,18 +564,15 @@
 
 
 class ReplicaSum:
-    slots = 4
-
-    def __init__(self, replicas, chunk, chunks, source, target, work, core_box, path_box, sems):
+    def __init__(self, replicas, chunk, source, target, work, core_box, path_box, sems):
         self.mine = lax.axis_index("replica")
-        self.chunk, self.chunks, self.source, self.target = chunk, chunks, source, target
+        self.chunk, self.source, self.target = chunk, source, target
         self.work, self.core_box, self.path_box, self.sems = work, core_box, path_box, sems
-        self.depth = work.shape[0]
+        self.depth, self.slots = work.shape[0], core_box.shape[0]
         bits = [1 << index for index in range(1, replicas.bit_length() - 1)]
         self.orders = (bits, bits[::-1])
         self.levels = len(bits)
         self.last_phase = 2 * self.levels + 2
-        self.ticks = chunks + 2 * self.last_phase
         self.half = chunk // 2
 
     def bit(self, mask):
@@ -697,6 +693,9 @@
                     self.share_copy(chunk).start()
 
 
+scatter_pace, both_pace, pair_pace = 0.7, 0.9, 0.34
+
+
 def rms_backward(values, grads, gain):
     scale = rms_rows(values)
     unit = values * scale
@@ -706,13 +705,13 @@
 
 
 def backward_kernel(
-    count, replicas, chunk, chunks,
+    count, replicas, chunk, attn_chunks, skew, subs,
     length_ref,
     flat_hbm, back_hbm, res_hbm, middle_hbm, cot_hbm, x_hbm, q_hbm, k_hbm, v_hbm, att_hbm, lse_hbm, n1_hbm,
     wq_hbm, wk_hbm, wv_hbm, wo_hbm, gains_ref, bias_ref, ids_ref,
     sums_out, flat_out, result_out, input_out, small_out,
     back, res, middle, cot, x_own, q_buf, k_buf, v_buf, att_buf, lse_buf, n1_buf, wq, wk, wv, wo,
-    back_box, res_box, total_buf, middle_grad, branch, grad_att, key_acc, value_acc, grad_qkv,
+    back_box, res_box, total_buf, res_total, middle_grad, branch, grad_att, key_acc, value_acc, grad_qkv,
     reverse, offsets, turned, stage, out_buf, small, small_parts, small_box, pair_box,
     work, core_box, path_box,
     load_sems, b_sems, r_sems, f_sems, a_sems, p_sems, pair_sems, stage_sems, out_sems, sum_sems,
@@ -754,81 +753,90 @@
 
     ffn_rows = flat_hbm.shape[0]
     from_ffn = ffn_rows // chunk
-
-    def make_sum(source_ref, base):
+    chunks = from_ffn + attn_chunks
+
+    def make_source(source_ref, base):
         return lambda start, size: source_ref.at[pl.ds(pl.multiple_of(start - base, 16), size)]
 
-    parts = ReplicaSum(
-        replicas, chunk, chunks, None, sums_out, work, core_box, path_box, sum_sems
-    )
-    from_first, from_second = make_sum(flat_hbm, 0), make_sum(flat_out, ffn_rows)
+    parts = ReplicaSum(replicas, chunk, None, sums_out, work, core_box, path_box, sum_sems)
+    from_first, from_second = make_source(flat_hbm, 0), make_source(flat_out, ffn_rows)
+    clock = {"time": 0, "gap": None, "credit": 0.0}
+
+    def start_piece(source, piece):
+        parts.source = source
+        parts.core_copy(piece).start()
+        parts.load_copy(piece).start()
 
     def tick(time):
+        gap = clock["gap"]
         for phase in range(parts.last_phase, -1, -1):
-            piece = time - 2 * phase
-            if isinstance(piece, int):
-                inside = 0 <= piece < chunks
+            entry = time - skew * phase
+            if isinstance(entry, int):
+                early = 0 <= entry < from_ffn
+                late = gap is not None and from_ffn + gap <= entry < chunks + gap
+                piece = entry if early else entry - (gap or 0)
+                inside = early or late
             else:
-                inside = (piece >= 0) & (piece < chunks)
+                early = (entry >= 0) & (entry < from_ffn)
+                late = (entry >= from_ffn + gap) & (entry < chunks + gap)
+                piece = jnp.where(entry < from_ffn, entry, entry - gap)
+                inside = early | late
 
             def body(phase=phase, piece=piece):
-                if phase > 1:
-                    if phase == parts.last_phase:
-                        parts.share_copy(piece).wait()
-                    else:
-                        parts.advance(phase, piece)
-                    return
-                for source, here in (
-                    (from_first, piece < from_ffn),
-                    (from_second, piece >= from_ffn),
-                ):
-                    def start(source=source):
-                        parts.source = source
-                        parts.core_copy(piece).start()
-                        parts.load_copy(piece).start()
-
-                    if phase == 0:
-                        when(here, start)
-                if phase == 1:
+                if phase == parts.last_phase:
+                    parts.share_copy(piece).wait()
+                elif phase:
                     parts.source = lambda start, size: flat_hbm.at[pl.ds(0, size)]
-                    parts.advance(1, piece)
-
-            when(inside, body)
-
-    back_line = LineScatter(me, count, back, back_box, b_sems)
-    res_line = LineScatter(me, count, res, res_box, r_sems)
-    first_line = LineScatter(me, count, back, back_box, f_sems)
-    branch_line = LineGather(me, count, branch, a_sems)
-    small_line = LineScatter(me, count, small_parts, small_box, p_sems)
+                    parts.advance(phase, piece)
+
+            if phase:
+                when(inside, body)
+            else:
+                when(early, functools.partial(start_piece, from_first, piece))
+                when(late, functools.partial(start_piece, from_second, piece))
+
+    def pace(amount):
+        clock["credit"] += amount
+        while clock["credit"] >= 1:
+            tick(clock["time"])
+            clock["time"] += 1
+            clock["credit"] -= 1
+
+    back_line = LineScatter(me, count, back, back_box, total_buf, b_sems, subs)
+    res_line = LineScatter(me, count, res, res_box, res_total, r_sems, subs)
+    first_line = LineScatter(me, count, back, back_box, total_buf, f_sems, subs)
+    branch_line = LineGather(me, count, branch, a_sems, subs)
+    small_line = LineScatter(me, count, small_parts, small_box, small.at[pl.ds(0, 8)], p_sems)
 
     tick(0)
     for load in loads[5:]:
         load.start()
+    loads[0].wait()
+    total_buf[...] = back[me].astype(jnp.float32)
+    back_line.at_time(0)
+    clock["time"] = 1
+    pace(2 * skew - 1)
     anti = lax.broadcasted_iota(jnp.int32, (total, total), 0) + lax.broadcasted_iota(
         jnp.int32, (total, total), 1
     )
     reverse[...] = (anti == total - 1).astype(jnp.float32).astype(jnp.bfloat16)
-    loads[0].wait()
-    time = 1
-    for step in range(count - 1):
-        for side in range(2):
-            back_line.forward(side, step)
-        tick(time)
-        time += 1
-    for load in loads[2:5]:
+    for now in range(1, back_line.times):
+        back_line.at_time(now)
+        pace(scatter_pace)
+    for load in loads[1:5]:
         load.wait()
-    total_buf[...] = back[me].astype(jnp.float32)
-    back_line.finish(total_buf)
     position = me * rows + lax.broadcasted_iota(jnp.int32, (rows, 1), 0)
     valid = (position < length_ref[0]).astype(jnp.float32)
     grad_mid, gain_grad = rms_backward(middle[...], total_buf[...], gains_ref[1:2, :])
     middle_grad[...] = cot[...].astype(jnp.float32) * valid + grad_mid
     branch[me] = middle_grad[...].astype(jnp.bfloat16)
+    branch_line.begin()
+    res_total[...] = middle[...] + res[me].astype(jnp.float32)
+    res_line.at_time(0)
     small_parts[...] = jnp.zeros_like(small_parts)
     part_width = width // count
     for owner in range(count):
         small_parts[owner, 1:2, :] = gain_grad[:, owner * part_width : (owner + 1) * part_width]
-    branch_line.start(0)
     for load in loads[5:]:
         load.wait()
 
@@ -836,25 +844,16 @@
         grad_att[block] = nt_dot(branch[block], wo[...]).astype(jnp.bfloat16)
 
     attended_grad(me)
-    tick(time)
-    time += 1
-    for step in range(count - 1):
-        for side in range(2):
-            branch_line.wait_arrival(side, step)
-        if step + 1 < count - 1:
-            branch_line.start(step + 1)
-
-        @pl.loop(0, 2)
-        def _(side):
-            arrives = jnp.where(side == 0, me - 1 - step >= 0, me + 1 + step < count)
-
-            @pl.when(arrives)
-            def _():
-                attended_grad(jnp.where(side == 0, me - 1 - step, me + 1 + step))
-
-        if step + 1 < count - 1:
-            tick(time)
-            time += 1
+    pace(both_pace)
+    for now in range(1, res_line.times):
+        branch_line.arrive(now - 1)
+        res_line.at_time(now)
+        pace(both_pace)
+        if now % subs == 0:
+            branch_line.each_block(now // subs - 1, attended_grad)
+    out_buf[0] = res_total[...].astype(jnp.bfloat16)
+    result_copy = pltpu.make_async_copy(out_buf.at[0], result_out, out_sems.at[0])
+    result_copy.start()
 
     tile = 256
 
@@ -888,9 +887,6 @@
         for slot in range(min(2, height // tile)):
             for panel in range(panels):
                 store(slot, panel, 0).wait()
-
-    weight_grad(att_buf, branch[...].reshape(total, width), 0, columns, width)
-    loads[1].wait()
 
     mask_first, mask_second = head_masks()
     key_valid = lax.broadcasted_iota(jnp.int32, (1, total), 1) < length_ref[0]
@@ -943,26 +939,9 @@
             ...
         ].T.astype(jnp.bfloat16)
 
-    pairs = local_heads // 2
-    for step in range(count - 1):
-        for side in range(2):
-            res_line.forward(side, step)
-        tick(time)
-        time += 1
-        if step < pairs:
-            head_pair(step)
-    for pair in range(count - 1, pairs):
+    for pair in range(local_heads // 2):
         head_pair(pair)
-    total_buf[...] = middle[...] + res[me].astype(jnp.float32)
-    res_line.finish(total_buf)
-    out_buf[0] = total_buf[...].astype(jnp.bfloat16)
-    result_copy = pltpu.make_async_copy(out_buf.at[0], result_out, out_sems.at[0])
-    result_copy.start()
-    tick(time)
-    time += 1
-    weight_grad(n1_buf, grad_qkv[...], columns * width // lanes, width, columns)
-    tick(time)
-    time += 1
+        pace(pair_pace)
 
     back_line.wait_sends()
 
@@ -974,17 +953,20 @@
             + nt_dot(grad_qkv[here, 2 * columns :], wv[...])
         ).astype(jnp.bfloat16)
 
-    @pl.loop(0, count)
-    def _(block):
-        first_part(block)
-
-    for step in range(count - 1):
-        for side in range(2):
-            first_line.forward(side, step)
-        tick(time)
-        time += 1
+    for index in range(count):
+        first_part(first_line.order(index))
+        if index < count - 1:
+            first_line.at_time(index)
+        if index == count // 2 - 1:
+            pace(1)
     total_buf[...] = back[me].astype(jnp.float32)
-    first_line.finish(total_buf)
+    weight_grad(att_buf, branch[...].reshape(total, width), 0, columns, width)
+    weight_grad(n1_buf, grad_qkv[...], columns * width // lanes, width, columns)
+    clock["gap"] = max(clock["time"] - from_ffn, 0)
+    pace(1)
+    for now in range(count - 1, first_line.times):
+        first_line.at_time(now)
+        pace(1)
     grad_in, gain_grad = rms_backward(
         x_own[...].astype(jnp.float32), total_buf[...], gains_ref[0:1, :]
     )
@@ -993,13 +975,10 @@
     input_copy.start()
     for owner in range(count):
         small_parts[owner, 0:1, :] = gain_grad[:, owner * part_width : (owner + 1) * part_width]
-    for step in range(count - 1):
-        for side in range(2):
-            small_line.forward(side, step)
-        tick(time)
-        time += 1
     small[0:8, :] = small_parts[me]
-    small_line.finish(small.at[pl.ds(0, 8)])
+    for now in range(small_line.times):
+        small_line.at_time(now)
+        pace(1)
     bucket = lax.broadcasted_iota(jnp.int32, (lanes, ids_ref.shape[1]), 0)
     one_hot = (bucket == ids_ref[...]).astype(jnp.float32).astype(jnp.bfloat16)
     high = offsets[...].astype(jnp.bfloat16)
@@ -1018,13 +997,12 @@
             device_id_type=MESH,
         )
         copy.start()
-        tick(time)
-        time += 1
+        pace(1)
         copy.wait()
         small[...] += pair_box[index]
     small_out[...] = small[...]
 
-    @pl.loop(time, parts.ticks)
+    @pl.loop(clock["time"], chunks + clock["gap"] + skew * parts.last_phase)
     def _(now):
         tick(now)
 
@@ -1044,17 +1022,19 @@
     dma = pltpu.SemaphoreType.DMA
     chunk = flat.shape[0] // 15
     attn_rows = 4 * columns * width // lanes
-    chunks = 15 + attn_rows // chunk
+    skew, subs = 3, 2
     levels = replicas.bit_length() - 2
     masks = levels + 1
-    depth = 2 * (levels + 2) + 2
+    depth = skew * (levels + 2)
     part_width = width // count
     vmem = pltpu.VMEM
     blocks = lambda kind: vmem((count, rows, width), kind)
     narrow = lambda: vmem((count, rows, columns), bf)
-    boxes = lambda: vmem((2, steps, rows, width), bf)
+    boxes = lambda: vmem((count + 1, rows, width), bf)
     return pl.pallas_call(
-        functools.partial(backward_kernel, count, replicas, chunk, chunks),
+        functools.partial(
+            backward_kernel, count, replicas, chunk, attn_rows // chunk, skew, subs
+        ),
         name="backward",
         out_shape=(
             shape((flat.shape[0] + attn_rows, lanes), bf),
@@ -1069,21 +1049,79 @@
             blocks(bf), blocks(bf), vmem((rows, width), f32), vmem((rows, width), bf), vmem((rows, width), bf),
             narrow(), narrow(), narrow(), narrow(), vmem((count, rows, lanes), f32), blocks(bf),
             vmem(wq.shape, bf), vmem(wk.shape, bf), vmem(wv.shape, bf), vmem(wo.shape, bf),
-            boxes(), boxes(), vmem((rows, width), f32), vmem((rows, width), f32), blocks(bf), narrow(),
+            boxes(), boxes(), vmem((rows, width), f32), vmem((rows, width), f32), vmem((rows, width), f32), blocks(bf),
+            narrow(),
             vmem((lanes, total), f32), vmem((lanes, total), f32), vmem((total, 3 * columns), bf),
             vmem((total, total), bf), vmem((8, 2 * total), f32), vmem((256, total), bf),
             vmem((2, width // lanes, 256, lanes), bf), vmem((2, rows, width), bf),
-            vmem((16, part_width), f32), vmem((count, 8, part_width), f32), vmem((2, steps, 8, part_width), f32),
+            vmem((16, part_width), f32), vmem((count, 8, part_width), f32), vmem((count + 1, 8, part_width), f32),
             vmem((masks, 16, part_width), f32),
-            vmem((depth, chunk // 2, lanes), bf), vmem((4, chunk // 2, lanes), bf), vmem((4, 2, chunk // 4, lanes), bf),
-            dma((15,)), dma((2, 2, steps)), dma((2, 2, steps)), dma((2, 2, steps)), dma((2, 2, steps)),
+            vmem((depth, chunk // 2, lanes), bf), vmem((2 * skew, chunk // 2, lanes), bf),
+            vmem((2 * skew, 2, chunk // 4, lanes), bf),
+            dma((15,)), dma((2, 2, steps * subs)), dma((2, 2, steps * subs)), dma((2, 2, steps * subs)),
+            dma((2, 2, steps * subs)),
             dma((2, 2, steps)), dma((2, masks)), dma((2, width // lanes)), dma((2,)),
-            dma((2, 2 * levels + 3, 3, 4)),
+            dma((2, 2 * levels + 3, 3, 2 * skew)),
         ],
         compiler_params=pltpu.CompilerParams(
-            collective_id=2, has_side_effects=True, vmem_limit_bytes=60 * 2**20
+            collective_id=2, has_side_effects=True, vmem_limit_bytes=61 * 2**20
         ),
     )(length, flat, back, res, middle, cot, x, q, k, v, att, lse, n1, wq, wk, wv, wo, gains, bias, ids)
+
+
+def widen_kernel(source, target):
+    target[...] = source[...].astype(jnp.float32)
+
+
+def widen(sums, start, shape):
+    height, depth = shape
+    return pl.pallas_call(
+        widen_kernel,
+        name="widen",
+        out_shape=jax.ShapeDtypeStruct(shape, jnp.float32),
+        grid=(depth // lanes,),
+        in_specs=[pl.BlockSpec((height, lanes), lambda index: (start // height + index, 0))],
+        out_specs=pl.BlockSpec((height, lanes), lambda index: (0, index)),
+        compiler_params=pltpu.CompilerParams(vmem_limit_bytes=32 * 2**20),
+    )(sums)
+
+
+def widen_tall_kernel(bounds, source, *targets):
+    index = pl.program_id(0)
+    for target, (first, last) in zip(targets, bounds):
+        @pl.when((index >= first) & (index < last))
+        def _():
+            target[...] = source[...].astype(jnp.float32)
+
+
+def widen_tall(sums, start, weights, skipped):
+    height = weights[0].shape[0]
+    bounds, first = [], 0
+    for weight in weights:
+        panels = weight.shape[1] // lanes
+        bounds.append((first, first + panels))
+        first += panels
+    split, jump, base = bounds[2][0], skipped // height, start // height
+
+    def out_spec(low, high):
+        return pl.BlockSpec(
+            (height, lanes), lambda index: (0, jnp.clip(index - low, 0, high - low - 1))
+        )
+
+    return pl.pallas_call(
+        functools.partial(widen_tall_kernel, bounds),
+        name="widen_tall",
+        out_shape=[jax.ShapeDtypeStruct(weight.shape, jnp.float32) for weight in weights],
+        grid=(first,),
+        in_specs=[
+            pl.BlockSpec(
+                (height, lanes),
+                lambda index: (base + index + jnp.where(index >= split, jump, 0), 0),
+            )
+        ],
+        out_specs=[out_spec(low, high) for low, high in bounds],
+        compiler_params=pltpu.CompilerParams(vmem_limit_bytes=48 * 2**20),
+    )(sums)
 
 
 def local(
@@ -1123,15 +1161,11 @@
         query, key, value, attended, log_totals, normed_one,
         w_query, w_key, w_value, w_attn_out, gains, bias, ids_back,
     )
-    start = 0
-    grads = []
-    for weight in (w_ffn_out, w_gate, w_up, w_attn_out, w_query, w_key, w_value):
-        height, depth = weight.shape
-        panels = depth // lanes
-        part = sums[start : start + panels * height].reshape(panels, height, lanes)
-        grads.append(part.transpose(1, 0, 2).reshape(height, depth).astype(jnp.float32))
-        start += panels * height
-    ffn_out_grad, gate_grad, up_grad, attn_out_grad, query_grad, key_grad, value_grad = grads
+    gate_grad, up_grad, query_grad, key_grad, value_grad = widen_tall(
+        sums, w_ffn_out.size // lanes, (w_gate, w_up, w_query, w_key, w_value), w_attn_out.size // lanes
+    )
+    ffn_out_grad = widen(sums, 0, w_ffn_out.shape)
+    attn_out_grad = widen(sums, (3 * w_gate.size) // lanes, w_attn_out.shape)
     buckets, local_heads = bias_table.shape
     table_grad = small[8 : 8 + local_heads, :buckets].T
     return (

time: 594 us -> 495 us (0.83)
  local copies, waits for them, and re-layouts: 58.8 us -> 7.65 us
  Pallas kernels: 507 us -> 476 us
  other arithmetic: 19.3 us -> 0.62 us
    pallas_call x1, Pallas kernels: 345 us -> 274 us  [backward(): pl.pallas_call(functools.partial(backward_kernel, count, replicas, chunk,...]
    pallas_call x2 -> x5, Pallas kernels: 161 us -> 202 us  [the longest x1 92.9 us: attention_forward(): pl.pallas_call(functools.partial(attention_forward_kernel, count, subs),...]
    unnamed x14 -> x10, local copies, waits for them, and re-layouts: 25.3 us -> 1.75 us
    convert_element_type x4 -> x0, other arithmetic: 18.7 us -> none  [local(): part.transpose(1, 0, 2).reshape(height, depth).astype(jnp.float32)]
    convert_element_type x2 -> x0, local copies, waits for them, and re-layouts: 17.2 us -> none  [local(): part.transpose(1, 0, 2).reshape(height, depth).astype(jnp.float32)]
    slice x2 -> x0, local copies, waits for them, and re-layouts: 9.59 us -> none  [local(): part = sums[start:start + panels * height].reshape(panels, height, lanes)]
where the time goes in v5:
time: 495 us; the launch traced here: 486 us
  Pallas kernels  476 us (96%)
  local copies, waits for them, and re-layouts  7.65 us (2%)
    pallas_call x1, Pallas kernels, backward(): pl.pallas_call(functools.partial(backward_kernel, count, replicas, chunk,...  274 us
    pallas_call x1, Pallas kernels, attention_forward(): pl.pallas_call(functools.partial(attention_forward_kernel, count, subs),...  92.9 us
    pallas_call x1, Pallas kernels, feed_forward(): pl.pallas_call(functools.partial(feed_forward_kernel, count, tile, subs),...  60.1 us
    pallas_call x1, Pallas kernels, widen_tall(): pl.pallas_call(functools.partial(widen_tall_kernel, bounds), name='widen_...  27.5 us
    pallas_call x2, Pallas kernels, widen(): pl.pallas_call(widen_kernel, name='widen', out_shape=jax.ShapeDtypeStruct...  21.3 us

profile of v5, /device:TPU:17, one launch (start us, length us, event | category | flops | bytes accessed | tf_op | source)
XLA Modules:
  0.0 485.8 jit_solution(17968734121771975212)
XLA Ops:
  1.3 0.7 stack.10
  2.0 0.7 stack.9
  2.7 0.6 fusion.3.gains_hbm
  3.3 1.3 pad.15
  4.6 92.9 %attention_forward.1 = (bf16[4,128,2048]{2,1,0:T(8,128)(2,1)}, bf16[4,128,512]{2,1,0:T(8,128)(2,1)}, bf16[4,128,512]{2,1,0:T(8,128)(2,1)}, bf16[4,128,512]{2,1,0...) custom-call(s32[1]{0:T(128)S(6)} %copy.28.length_ref, ...), custom_call_target="tpu_custom_call" | custom-call | tf_op jit(solution)/shard_map/attention_forward/pallas_call | solution.py:350
  97.5 0.0 copy-start.2
  97.5 60.1 %feed_forward.1 = (bf16[61440,128]{1,0:T(8,128)(2,1)}, bf16[4,128,2048]{2,1,0:T(8,128)(2,1)}, bf16[4,128,2048]{2,1,0:T(8,128)(2,1)}) custom-call(s32[1]{0:T(128)S(6)} %copy.28.length_ref, bf16[128,2048]{1,0:T(8,128)(2,1)} %get-tuple-element.35.n2_hbm, bf16[4,128,2048]{2,1,0:T(8,128)(2,1)} %get-tuple-element.36.cot_hbm, bf16[2048,1280]{1,0:T(8,128)(2,1)} %wg_hbm.1, ...), custom_call_target="tpu_custom_call" | custom-call | tf_op jit(solution)/shard_map/feed_forward/pallas_call | solution.py:524
  157.6 0.0 copy-done.2
  157.6 0.1 reverse
  157.7 0.1 slice.13
  157.7 0.6 pad.16
  158.3 274.1 %backward.1 = (bf16[94208,128]{1,0:T(8,128)(2,1)}, bf16[32768,128]{1,0:T(8,128)(2,1)}, bf16[128,2048]{1,0:T(8,128)(2,1)}, bf16[128,2048]{1,0:T(8,128)(2,1)}, f32[16,512]{1,0:T(8,128)}) custom-call(s32[1]{0:T(128)S(6)} %copy.28.length_ref, bf16[61440,128]{1,0:T(8,128)(2,1)} %get-tuple-element.37.flat_hbm, bf16[4,128,2048]{2,1,0:T(8,128)(2,1)} %get-tuple-element.38.back_hbm, ...), custom_call_target="tpu_custom_call" | custom-call | tf_op jit(solution)/shard_map/backward/pallas_call | solution.py:1034
  432.4 1.4 fusion.4
  433.8 27.5 %widen_tall.1 = (f32[2048,1280]{1,0:T(8,128)}, f32[2048,1280]{1,0:T(8,128)}, f32[2048,512]{1,0:T(8,128)}, f32[2048,512]{1,0:T(8,128)}, f32[2048,512]{1,0:T(8,128)}) custom-call(bf16[94208,128]{1,0:T(8,128)(2,1)} %get-tuple-element.52.source), custom_call_target="tpu_custom_call" | custom-call | tf_op jit(solution)/shard_map/widen_tall/pallas_call | solution.py:1111
  461.3 9.8 %widen.2 = f32[512,2048]{1,0:T(8,128)} custom-call(bf16[94208,128]{1,0:T(8,128)(2,1)} %get-tuple-element.52.source), custom_call_target="tpu_custom_call" | custom-call | tf_op jit(solution)/shard_map/widen/pallas_call | solution.py:1078
  471.1 1.3 slice_bitcast_fusion
  472.4 0.0 copy-start.1
  472.4 0.0 copy-start
  472.4 11.5 %widen.3 = f32[1280,2048]{1,0:T(8,128)} custom-call(bf16[94208,128]{1,0:T(8,128)(2,1)} %get-tuple-element.52.source), custom_call_target="tpu_custom_call" | custom-call | tf_op jit(solution)/shard_map/widen/pallas_call | solution.py:1078
  483.9 0.0 copy-done.1
  483.9 0.8 copy.29
  484.7 0.0 copy-done
  484.7 0.8 copy.30
Async XLA Ops:
  97.5 60.1 %copy-start.2 = (s32[1023]{0:T(1024)S(1)}, s32[1023]{0:T(1024)}, u32[]{:S(2)}) copy-start(s32[1023]{0:T(1024)} %param.16) | copy-start | bytes 12280
  472.4 11.5 %copy-start.1 = (bf16[128,2048]{1,0:T(8,128)(2,1)S(1)}, bf16[128,2048]{1,0:T(8,128)(2,1)}, u32[]{:S(2)}) copy-start(bf16[128,2048]{1,0:T(8,128)(2,1)} %get-tuple-element.49) | copy-start | bytes 1572868
  472.4 12.3 %copy-start = (bf16[128,2048]{1,0:T(8,128)(2,1)S(1)}, bf16[128,2048]{1,0:T(8,128)(2,1)}, u32[]{:S(2)}) copy-start(bf16[128,2048]{1,0:T(8,128)(2,1)} %get-tuple-element.50) | copy-start | bytes 1572868
